TPU v7x, 512 devices: a whole 4x8x8 slice. The times are simulated.
512 devices in a mesh: depth: 16 (over y, core), lat: 32 (over z, x).
Axes of the slice: x: 4, y: 8, z: 8, core: 2. Of those that a mesh axis runs over, the one named last changes fastest.
Arguments:
- potential: float32 [2, 16, 2, 1024, 2048], P(None, 'depth', None, 'lat'), may hold values from -3 to 3, as said below
- incident: float32 [2, 2, 1024, 1024], P(None, None, 'lat'), may hold values from -6 to 6
- measured: float32 [2, 1024, 1024], P(None, 'lat'), may hold values from 0 to 3
- offsets: int32 [2, 2], replicated, may hold values from 0 to 1024, as said below
- kernel: bfloat16 [2, 9], replicated, may hold values from -1 to 1
Outputs:
- potential_grad: float32 [2, 16, 2, 1024, 2048], P(None, 'depth', None, 'lat')
Inputs may be any that keep to these rules, and one draw needn't show every extreme that they name: Row offsets are multiples of 32 from 0 to 1024; column offsets run from 0 to 1024. `potential`: part 0 (phase) lies in -3 to 3; part 1 (absorption) lies in 0.004 to 0.05.
All inputs are finite; a program needn't handle non-finite values.
Results may differ from a plain program's by a relative error of at most 0.038.
Values may be sent and summed in bfloat16 or wider, within the bound.
No kernel may reach another device: no remote copies, remote signals or barrier semaphores. Data moves between devices by JAX's collectives and lax.ppermute only.
A program may use at most 64 MiB of HBM per device.

v0:
```python
import jax
import jax.numpy as jnp
from jax import lax
from jax.sharding import PartitionSpec as P


def with_halo(cells, sides, width):
    for axis, dim in sides:
        count = lax.axis_size(axis)
        head = lax.slice_in_dim(cells, 0, width, axis=dim)
        tail = lax.slice_in_dim(cells, cells.shape[dim] - width, cells.shape[dim], axis=dim)
        cells = jnp.concatenate(
            [
                lax.ppermute(tail, axis, [(i, (i + 1) % count) for i in range(count)]),
                cells,
                lax.ppermute(head, axis, [((i + 1) % count, i) for i in range(count)]),
            ],
            axis=dim,
        )
    return cells


def from_behind(array, axis, by):
    count = lax.axis_size(axis)
    pairs = [(i, i + by) for i in range(count) if 0 <= i + by < count]
    return lax.ppermute(array, axis, pairs)


def rounded(field_in):
    return lax.optimization_barrier(field_in.astype(jnp.bfloat16)).astype(jnp.float32)


def band_matrix(taps_re, taps_im, row_count, col_count, half_width, transposed):
    row_index = lax.broadcasted_iota(jnp.int32, (row_count, col_count), 0)
    col_index = lax.broadcasted_iota(jnp.int32, (row_count, col_count), 1)
    offset = row_index - col_index if transposed else col_index - row_index
    chooser = (offset[:, :, None] == jnp.arange(2 * half_width + 1, dtype=jnp.int32)).astype(
        jnp.float32
    )
    real_part = jnp.sum(chooser * taps_re, axis=2).astype(jnp.bfloat16)
    imag_part = jnp.sum(chooser * taps_im, axis=2).astype(jnp.bfloat16)
    return (real_part, imag_part)


def along_rows(field_in, real_mat, imag_mat):
    direct = jnp.einsum("rq,xpqc->xprc", real_mat, field_in, preferred_element_type=jnp.float32)
    crossed = jnp.einsum("rq,xpqc->xprc", imag_mat, field_in, preferred_element_type=jnp.float32)
    return jnp.stack([direct[0] - crossed[1], crossed[0] + direct[1]])


def along_cols(field_in, real_slab, imag_slab, half_width):
    columns = field_in.shape[-1]
    blocks = columns // 128
    padded = jnp.pad(field_in, ((0, 0), (0, 0), (0, 0), (half_width, 128 - half_width)))
    main_part = padded[..., :columns].reshape(field_in.shape[:-1] + (blocks, 128))
    extra_part = padded[..., 128 : columns + 128].reshape(field_in.shape[:-1] + (blocks, 128))[
        ..., : 2 * half_width
    ]
    slab_rows = jnp.concatenate([main_part, extra_part], axis=-1)
    direct = jnp.einsum("xprbq,qo->xprbo", slab_rows, real_slab, preferred_element_type=jnp.float32)
    crossed = jnp.einsum(
        "xprbq,qo->xprbo", slab_rows, imag_slab, preferred_element_type=jnp.float32
    )
    joined = jnp.stack([direct[0] - crossed[1], crossed[0] + direct[1]])
    return joined.reshape(field_in.shape)


def local(potential, incident, measured, offsets, kernel):
    lat_count = lax.axis_size("lat")
    depth_count = lax.axis_size("depth")
    lat_index = lax.axis_index("lat")
    depth_index = lax.axis_index("depth")
    band_rows = potential.shape[3]
    window = incident.shape[3]
    probe_count = incident.shape[1]
    half_width = (kernel.shape[1] - 1) // 2
    taps_re = kernel[0].astype(jnp.float32)
    taps_im = kernel[1].astype(jnp.float32)
    back_re = taps_re[::-1]
    back_im = -taps_im[::-1]
    row_pixel = offsets[:, 0]
    col_pixel = offsets[:, 1]
    first_band = row_pixel // band_rows
    place_band = (lat_index - first_band) % lat_count
    layer_pot = potential[:, 0]
    reach_steps = 2
    margin = reach_steps * half_width
    full_rows = band_rows + 2 * margin
    most_out = full_rows - 2 * half_width
    row_forward = band_matrix(taps_re, taps_im, most_out, full_rows, half_width, False)
    row_adjoint = band_matrix(back_re, back_im, most_out, full_rows, half_width, False)
    column_forward = band_matrix(taps_re, taps_im, 128 + 2 * half_width, 128, half_width, True)
    column_adjoint = band_matrix(back_re, back_im, 128 + 2 * half_width, 128, half_width, True)
    local_rows = jnp.arange(full_rows, dtype=jnp.int32) - margin
    window_row = place_band[:, None] * band_rows + local_rows[None, :]
    valid_rows = (window_row >= 0) & (window_row < window)
    keep_mask = valid_rows[None, :, :, None]
    padded_pot = with_halo(layer_pot, (("lat", 2),), margin)
    local_rows = jnp.arange(band_rows + 2 * margin, dtype=jnp.int32) - margin
    side_rows = (local_rows >= band_rows).astype(jnp.int32) - (local_rows < 0).astype(jnp.int32)
    halves = jnp.clip(
        (first_band[:, None] + place_band[:, None] + side_rows[None, :]) // lat_count, 0, 1
    )

    def cut_window(col_start):
        return lax.dynamic_slice_in_dim(padded_pot, col_start, window, 3)

    windows = jax.vmap(cut_window)(col_pixel)
    chosen = jnp.where((halves == 0)[:, None, :, None], windows[:, :, 0], windows[:, :, 1])
    damping = jnp.exp(-chosen[:, 1])
    phase_part = chosen[:, 0]
    transmit = jnp.stack([damping * jnp.cos(phase_part), damping * jnp.sin(phase_part)])

    def forward_segment(wave_ext, extent):
        low_row = margin - extent
        rows_in = band_rows + 2 * extent
        rows_out = rows_in - 2 * half_width
        factor = transmit[:, :, low_row : low_row + rows_in]
        inside = keep_mask[:, :, low_row : low_row + rows_in]
        values = wave_ext.astype(jnp.float32)
        product = jnp.stack(
            [
                factor[0] * values[0] - factor[1] * values[1],
                factor[0] * values[1] + factor[1] * values[0],
            ]
        )
        product = jnp.where(inside, product, 0.0).astype(jnp.bfloat16)
        spread = along_rows(
            product, row_forward[0][:rows_out, :rows_in], row_forward[1][:rows_out, :rows_in]
        ).astype(jnp.bfloat16)
        return along_cols(spread, column_forward[0], column_forward[1], half_width).astype(
            jnp.bfloat16
        )

    def backward_segment(adjoint, extent, entry):
        low_row = margin - extent
        rows_in = band_rows + 2 * extent
        rows_out = rows_in - 2 * half_width
        inside = keep_mask[:, :, low_row : low_row + rows_in]
        masked = jnp.where(inside, adjoint, jnp.zeros_like(adjoint))
        spread = along_cols(masked, column_adjoint[0], column_adjoint[1], half_width).astype(
            jnp.bfloat16
        )
        local_grad = rounded(
            along_rows(
                spread, row_adjoint[0][:rows_out, :rows_in], row_adjoint[1][:rows_out, :rows_in]
            )
        )
        factor = transmit[:, :, low_row + half_width : low_row + half_width + rows_out]
        earlier = jnp.stack(
            [
                factor[0] * local_grad[0] + factor[1] * local_grad[1],
                factor[0] * local_grad[1] - factor[1] * local_grad[0],
            ]
        ).astype(jnp.bfloat16)
        centre = extent - half_width
        own_rows = local_grad[:, :, centre : centre + band_rows]
        own_factor = factor[:, :, centre : centre + band_rows]
        entry_wave = entry.astype(jnp.float32)
        cross_re = entry_wave[0] * own_rows[0] + entry_wave[1] * own_rows[1]
        cross_im = entry_wave[0] * own_rows[1] - entry_wave[1] * own_rows[0]
        turned_re = own_factor[0] * cross_re + own_factor[1] * cross_im
        turned_im = own_factor[0] * cross_im - own_factor[1] * cross_re
        return (earlier, jnp.stack([turned_im, -turned_re]))

    start_wave = incident.astype(jnp.bfloat16)
    zeros_wave = jnp.zeros_like(start_wave)
    blocks = depth_count // reach_steps

    def forward_block(block_index, carry):
        moving, stored, leaving = carry
        entering = jnp.where(depth_index == 0, start_wave, moving)
        wave_ext = with_halo(entering, (("lat", 2),), margin)
        for sub_step in range(reach_steps):
            extent = margin - sub_step * half_width
            result = forward_segment(wave_ext, extent)
            active = depth_index == block_index * reach_steps + sub_step
            stored = jnp.where(active, wave_ext[:, :, extent : extent + band_rows], stored)
            if sub_step == reach_steps - 1:
                leaving = jnp.where(active, result, leaving)
            wave_ext = from_behind(result, "depth", 1)
        return (wave_ext, stored, leaving)

    moving, stored, leaving = lax.fori_loop(
        0, blocks, forward_block, (zeros_wave, zeros_wave, zeros_wave)
    )
    exit_vals = leaving.astype(jnp.float32)
    residual = exit_vals[0] * exit_vals[0] + exit_vals[1] * exit_vals[1] - measured
    seed_wave = (2.0 * residual[None] * exit_vals).astype(jnp.bfloat16)
    zeros_term = jnp.zeros(start_wave.shape, jnp.float32)

    def backward_block(block_index, carry):
        moving_back, collected = carry
        entering = jnp.where(depth_index == depth_count - 1, seed_wave, moving_back)
        adjoint = with_halo(entering, (("lat", 2),), margin)
        for sub_step in range(reach_steps):
            extent = margin - sub_step * half_width
            earlier, grad_term = backward_segment(adjoint, extent, stored)
            active = depth_index == depth_count - 1 - (block_index * reach_steps + sub_step)
            collected = jnp.where(active, grad_term, collected)
            adjoint = from_behind(earlier, "depth", -1)
        return (adjoint, collected)

    moving_back, gathered = lax.fori_loop(0, blocks, backward_block, (zeros_wave, zeros_term))
    own_half = (first_band + place_band) // lat_count
    gradient = jnp.zeros_like(layer_pot)

    def accumulate(probe_index, running):
        portion = lax.dynamic_index_in_dim(gathered, probe_index, 1, keepdims=False)
        zero_index = jnp.zeros((), jnp.int32)
        corner = (zero_index, own_half[probe_index], zero_index, col_pixel[probe_index])
        current = lax.dynamic_slice(running, corner, (2, 1, band_rows, window))
        return lax.dynamic_update_slice(running, current + portion[:, None], corner)

    gradient = lax.fori_loop(0, probe_count, accumulate, gradient)
    return gradient[:, None]


def solution(mesh):
    in_specs = (
        P(None, "depth", None, "lat", None),
        P(None, None, "lat", None),
        P(None, "lat", None),
        P(),
        P(),
    )
    out_specs = P(None, "depth", None, "lat", None)
    return jax.shard_map(local, mesh=mesh, in_specs=in_specs, out_specs=out_specs, check_vma=False)
```

profile of v0, /device:TPU:25, one launch (start us, length us, event | category | flops | bytes accessed | tf_op | source)
XLA Modules:
  0.0 686.3 jit_solution(6714270978107301532)
XLA Ops:
  4.3 11.7 %collective-permute-start.9 = (f32[2,2,8,2048]{3,2,1,0:T(8,128)S(1)}, f32[2,2,8,2048]{3,2,1,0:T(8,128)}, u32[]{:S(2)}, u32[]{:S(2)}) collective-permute-start(f32[2,2,8,2048]{3,2,1,0:T(8,128)S(1)} %get-tuple-element.968), channel_id=1, source_target_pairs={{1,0},{2,1},{3,2},{4,3},{5,4},{6,5},{7,6},{8,7},{9,8},{10,9},{11,1... | collective-permute-start | bytes 786440 | tf_op jit(solution)/shard_map/ppermute | solution.py:16
  32.1 334.2 %while.54 = (s32[]{:T(128)}, bf16[2,2,32,1024]{3,2,1,0:T(8,128)(2,1)}, bf16[2,2,32,1024]{3,2,1,0:T(8,128)(2,1)S(1)}, bf16[2,2,32,1024]{3,2,1,0:T(8,128)(2,1)}, p...) while((s32[]{:T(128)}, ...), condition=%wide.region_5.6_spmd.clone, body=%wide.region_4.5_spmd.clone.sunk | while | flops 226873344 | bytes 33341824 | solution.py:184
  33.1 6.0 collective-permute-start
  41.1 6.4 collective-permute-done.1
  52.7 7.3 %collective-permute-start.2 = (bf16[2,2,40,1024]{3,2,1,0:T(8,128)(2,1)S(1)}, bf16[2,2,40,1024]{3,2,1,0:T(8,128)(2,1)S(1)}, u32[]{:S(2)}, u32[]{:S(2)}) collective-permute-start(bf16[2,2,40,1024]{3,2,1,0:T(8,128)(2,1)S(1)} %pad_maximum_fusion.36), channel_id=1, source_target_pairs={{0,32},{32,64},{64,96},{96,128},{128,160},{160,192},{192,224},{224... | collective-permute-start | bytes 983048 | tf_op jit(solution)/shard_map/while/body/eval_jaxpr/ppermute | solution.py:26
  68.9 5.6 collective-permute-start.3
  84.1 5.1 collective-permute-done.1
  94.5 6.7 collective-permute-start.2
  110.1 5.6 collective-permute-start.3
  125.3 4.9 collective-permute-done.1
  135.5 6.9 collective-permute-start.2
  151.3 5.6 collective-permute-start.3
  166.6 4.9 collective-permute-done.1
  176.7 6.9 collective-permute-start.2
  192.6 5.6 collective-permute-start.3
  207.8 4.9 collective-permute-done.1
  218.0 6.9 collective-permute-start.2
  233.8 5.6 collective-permute-start.3
  249.0 4.9 collective-permute-done.1
  259.2 6.9 collective-permute-start.2
  275.0 5.6 collective-permute-start.3
  300.4 6.9 collective-permute-start.2
  316.2 5.6 collective-permute-start.3
  331.4 4.9 collective-permute-done.1
  341.6 6.9 collective-permute-start.2
  357.4 5.6 collective-permute-start.3
  368.5 303.1 %while.55 = (s32[]{:T(128)}, bf16[2,2,32,1024]{3,2,1,0:T(8,128)(2,1)S(1)}, f32[2,2,32,1024]{3,2,1,0:T(8,128)S(1)}, f32[2,2,48,1024]{3,2,1,0:T(8,128)S(1)}, pred[...) while((s32[]{:T(128)}, ...), condition=%wide.region_11.12_spmd.clone, body=%wide.region_10.11_spmd.clone.sunk | while | flops 259112960 | bytes 46096776 | solution.py:204
  373.9 4.9 collective-permute-done.5
  384.8 9.6 %collective-permute-done.6 = bf16[2,2,40,1024]{3,2,1,0:T(8,128)(2,1)S(1)} collective-permute-done((bf16[2,2,40,1024]{3,2,1,0:T(8,128)(2,1)S(1)}, bf16[2,2,40,1024]{3,2,1,0:T(8,128)(2,1)S(1)}, u32[]{:S(2)}, u32[]{:S(2)}) %collective-permute-start.6) | collective-permute-done | bytes 327712 | tf_op jit(solution)/shard_map/while/body/eval_jaxpr/ppermute | solution.py:26
  401.2 6.9 %collective-permute-done.7 = bf16[2,2,32,1024]{3,2,1,0:T(8,128)(2,1)S(1)} collective-permute-done((bf16[2,2,32,1024]{3,2,1,0:T(8,128)(2,1)}, bf16[2,2,32,1024]{3,2,1,0:T(8,128)(2,1)S(1)}, u32[]{:S(2)}, u32[]{:S(2)}) %collective-permute-start.7) | collective-permute-done | bytes 262176 | tf_op jit(solution)/shard_map/while/body/eval_jaxpr/ppermute | solution.py:26
  413.5 4.9 collective-permute-done.5
  424.5 7.6 %collective-permute-done.6 = bf16[2,2,40,1024]{3,2,1,0:T(8,128)(2,1)S(1)} collective-permute-done((bf16[2,2,40,1024]{3,2,1,0:T(8,128)(2,1)S(1)}, bf16[2,2,40,1024]{3,2,1,0:T(8,128)(2,1)S(1)}, u32[]{:S(2)}, u32[]{:S(2)}) %collective-permute-start.6) | collective-permute-done | bytes 327712 | tf_op jit(solution)/shard_map/while/body/eval_jaxpr/ppermute | solution.py:26
  438.8 6.9 %collective-permute-done.7 = bf16[2,2,32,1024]{3,2,1,0:T(8,128)(2,1)S(1)} collective-permute-done((bf16[2,2,32,1024]{3,2,1,0:T(8,128)(2,1)}, bf16[2,2,32,1024]{3,2,1,0:T(8,128)(2,1)S(1)}, u32[]{:S(2)}, u32[]{:S(2)}) %collective-permute-start.7) | collective-permute-done | bytes 262176 | tf_op jit(solution)/shard_map/while/body/eval_jaxpr/ppermute | solution.py:26
  451.2 4.9 collective-permute-done.5
  462.1 7.6 %collective-permute-done.6 = bf16[2,2,40,1024]{3,2,1,0:T(8,128)(2,1)S(1)} collective-permute-done((bf16[2,2,40,1024]{3,2,1,0:T(8,128)(2,1)S(1)}, bf16[2,2,40,1024]{3,2,1,0:T(8,128)(2,1)S(1)}, u32[]{:S(2)}, u32[]{:S(2)}) %collective-permute-start.6) | collective-permute-done | bytes 327712 | tf_op jit(solution)/shard_map/while/body/eval_jaxpr/ppermute | solution.py:26
  476.5 6.9 %collective-permute-done.7 = bf16[2,2,32,1024]{3,2,1,0:T(8,128)(2,1)S(1)} collective-permute-done((bf16[2,2,32,1024]{3,2,1,0:T(8,128)(2,1)}, bf16[2,2,32,1024]{3,2,1,0:T(8,128)(2,1)S(1)}, u32[]{:S(2)}, u32[]{:S(2)}) %collective-permute-start.7) | collective-permute-done | bytes 262176 | tf_op jit(solution)/shard_map/while/body/eval_jaxpr/ppermute | solution.py:26
  488.8 4.9 collective-permute-done.5
  499.7 7.6 %collective-permute-done.6 = bf16[2,2,40,1024]{3,2,1,0:T(8,128)(2,1)S(1)} collective-permute-done((bf16[2,2,40,1024]{3,2,1,0:T(8,128)(2,1)S(1)}, bf16[2,2,40,1024]{3,2,1,0:T(8,128)(2,1)S(1)}, u32[]{:S(2)}, u32[]{:S(2)}) %collective-permute-start.6) | collective-permute-done | bytes 327712 | tf_op jit(solution)/shard_map/while/body/eval_jaxpr/ppermute | solution.py:26
  514.1 6.9 %collective-permute-done.7 = bf16[2,2,32,1024]{3,2,1,0:T(8,128)(2,1)S(1)} collective-permute-done((bf16[2,2,32,1024]{3,2,1,0:T(8,128)(2,1)}, bf16[2,2,32,1024]{3,2,1,0:T(8,128)(2,1)S(1)}, u32[]{:S(2)}, u32[]{:S(2)}) %collective-permute-start.7) | collective-permute-done | bytes 262176 | tf_op jit(solution)/shard_map/while/body/eval_jaxpr/ppermute | solution.py:26
  537.4 7.6 %collective-permute-done.6 = bf16[2,2,40,1024]{3,2,1,0:T(8,128)(2,1)S(1)} collective-permute-done((bf16[2,2,40,1024]{3,2,1,0:T(8,128)(2,1)S(1)}, bf16[2,2,40,1024]{3,2,1,0:T(8,128)(2,1)S(1)}, u32[]{:S(2)}, u32[]{:S(2)}) %collective-permute-start.6) | collective-permute-done | bytes 327712 | tf_op jit(solution)/shard_map/while/body/eval_jaxpr/ppermute | solution.py:26
  551.7 6.9 %collective-permute-done.7 = bf16[2,2,32,1024]{3,2,1,0:T(8,128)(2,1)S(1)} collective-permute-done((bf16[2,2,32,1024]{3,2,1,0:T(8,128)(2,1)}, bf16[2,2,32,1024]{3,2,1,0:T(8,128)(2,1)S(1)}, u32[]{:S(2)}, u32[]{:S(2)}) %collective-permute-start.7) | collective-permute-done | bytes 262176 | tf_op jit(solution)/shard_map/while/body/eval_jaxpr/ppermute | solution.py:26
  575.0 7.6 %collective-permute-done.6 = bf16[2,2,40,1024]{3,2,1,0:T(8,128)(2,1)S(1)} collective-permute-done((bf16[2,2,40,1024]{3,2,1,0:T(8,128)(2,1)S(1)}, bf16[2,2,40,1024]{3,2,1,0:T(8,128)(2,1)S(1)}, u32[]{:S(2)}, u32[]{:S(2)}) %collective-permute-start.6) | collective-permute-done | bytes 327712 | tf_op jit(solution)/shard_map/while/body/eval_jaxpr/ppermute | solution.py:26
  589.4 6.9 %collective-permute-done.7 = bf16[2,2,32,1024]{3,2,1,0:T(8,128)(2,1)S(1)} collective-permute-done((bf16[2,2,32,1024]{3,2,1,0:T(8,128)(2,1)}, bf16[2,2,32,1024]{3,2,1,0:T(8,128)(2,1)S(1)}, u32[]{:S(2)}, u32[]{:S(2)}) %collective-permute-start.7) | collective-permute-done | bytes 262176 | tf_op jit(solution)/shard_map/while/body/eval_jaxpr/ppermute | solution.py:26
  612.6 7.6 %collective-permute-done.6 = bf16[2,2,40,1024]{3,2,1,0:T(8,128)(2,1)S(1)} collective-permute-done((bf16[2,2,40,1024]{3,2,1,0:T(8,128)(2,1)S(1)}, bf16[2,2,40,1024]{3,2,1,0:T(8,128)(2,1)S(1)}, u32[]{:S(2)}, u32[]{:S(2)}) %collective-permute-start.6) | collective-permute-done | bytes 327712 | tf_op jit(solution)/shard_map/while/body/eval_jaxpr/ppermute | solution.py:26
  627.0 6.9 %collective-permute-done.7 = bf16[2,2,32,1024]{3,2,1,0:T(8,128)(2,1)S(1)} collective-permute-done((bf16[2,2,32,1024]{3,2,1,0:T(8,128)(2,1)}, bf16[2,2,32,1024]{3,2,1,0:T(8,128)(2,1)S(1)}, u32[]{:S(2)}, u32[]{:S(2)}) %collective-permute-start.7) | collective-permute-done | bytes 262176 | tf_op jit(solution)/shard_map/while/body/eval_jaxpr/ppermute | solution.py:26
  650.3 7.6 %collective-permute-done.6 = bf16[2,2,40,1024]{3,2,1,0:T(8,128)(2,1)S(1)} collective-permute-done((bf16[2,2,40,1024]{3,2,1,0:T(8,128)(2,1)S(1)}, bf16[2,2,40,1024]{3,2,1,0:T(8,128)(2,1)S(1)}, u32[]{:S(2)}, u32[]{:S(2)}) %collective-permute-start.6) | collective-permute-done | bytes 327712 | tf_op jit(solution)/shard_map/while/body/eval_jaxpr/ppermute | solution.py:26
  664.6 6.9 %collective-permute-done.7 = bf16[2,2,32,1024]{3,2,1,0:T(8,128)(2,1)S(1)} collective-permute-done((bf16[2,2,32,1024]{3,2,1,0:T(8,128)(2,1)}, bf16[2,2,32,1024]{3,2,1,0:T(8,128)(2,1)S(1)}, u32[]{:S(2)}, u32[]{:S(2)}) %collective-permute-start.7) | collective-permute-done | bytes 262176 | tf_op jit(solution)/shard_map/while/body/eval_jaxpr/ppermute | solution.py:26
  671.7 13.6 %while.52 = (s32[]{:T(128)}, f32[2,2,32,2048]{3,2,1,0:T(8,128)S(1)}, s32[2]{0:T(128)}, s32[2]{0:T(128)S(1)}, f32[2,2,32,1024]{3,2,1,0:T(8,128)S(1)}, /*index=5*/s32[]{:T(128)}, s32[]{:T(128)}, s32[]{:T(128)}, s32[]{:T(128)}) while((s32[]{:T(128)}, f32[2,2,32,2048]{3,2,1,0:T(8,128)S(1)}, s32[2]{0:T(128)}, s32[2]{0:T(128)S(1)}, ...), condition=%wide.region_13.14_spmd, body=%wide.region_12.13_spmd.sunk | while | flops 65544 | bytes 1310921 | solution.py:215
  (855 shorter events, 385.8 us)
Async XLA Ops:
  1.2 21.3 %collective-permute-start.8 = (f32[2,2,8,2048]{3,2,1,0:T(8,128)S(1)}, f32[2,2,8,2048]{3,2,1,0:T(8,128)}, u32[]{:S(2)}, u32[]{:S(2)}) collective-permute-start(f32[2,2,8,2048]{3,2,1,0:T(8,128)S(1)} %get-tuple-element.967), channel_id=1, source_target_pairs={{0,1},{1,2},{2,3},{3,4},{4,5},{5,6},{6,7},{7,8},{8,9},{9,10},{10,1... | collective-permute-start | bytes 786440 | tf_op jit(solution)/shard_map/ppermute | solution.py:14
  4.3 18.1 %collective-permute-start.9 = (f32[2,2,8,2048]{3,2,1,0:T(8,128)S(1)}, f32[2,2,8,2048]{3,2,1,0:T(8,128)}, u32[]{:S(2)}, u32[]{:S(2)}) collective-permute-start(f32[2,2,8,2048]{3,2,1,0:T(8,128)S(1)} %get-tuple-element.968), channel_id=1, source_target_pairs={{1,0},{2,1},{3,2},{4,3},{5,4},{6,5},{7,6},{8,7},{9,8},{10,9},{11,1... | collective-permute-start | bytes 786440 | tf_op jit(solution)/shard_map/ppermute | solution.py:16
  39.1 8.3 %collective-permute-start.1 = (bf16[2,2,8,1024]{3,2,1,0:T(8,128)(2,1)S(1)}, bf16[2,2,8,1024]{3,2,1,0:T(8,128)(2,1)S(1)}, u32[]{:S(2)}, u32[]{:S(2)}) collective-permute-start(bf16[2,2,8,1024]{3,2,1,0:T(8,128)(2,1)S(1)} %get-tuple-element.1238), channel_id=1, source_target_pairs={{0,1},{1,2},{2,3},{3,4},{4,5},{5,6},{6,7},{7,8},{8,9},{9,10},{10,1... | collective-permute-start | bytes 196616 | tf_op jit(solution)/shard_map/while/body/eval_jaxpr/ppermute | solution.py:14
  52.7 11.3 %collective-permute-start.2 = (bf16[2,2,40,1024]{3,2,1,0:T(8,128)(2,1)S(1)}, bf16[2,2,40,1024]{3,2,1,0:T(8,128)(2,1)S(1)}, u32[]{:S(2)}, u32[]{:S(2)}) collective-permute-start(bf16[2,2,40,1024]{3,2,1,0:T(8,128)(2,1)S(1)} %pad_maximum_fusion.36), channel_id=1, source_target_pairs={{0,32},{32,64},{64,96},{96,128},{128,160},{160,192},{192,224},{224... | collective-permute-start | bytes 983048 | tf_op jit(solution)/shard_map/while/body/eval_jaxpr/ppermute | solution.py:26
  68.9 8.9 %collective-permute-start.3 = (bf16[2,2,32,1024]{3,2,1,0:T(8,128)(2,1)S(1)}, bf16[2,2,32,1024]{3,2,1,0:T(8,128)(2,1)}, u32[]{:S(2)}, u32[]{:S(2)}) collective-permute-start(bf16[2,2,32,1024]{3,2,1,0:T(8,128)(2,1)S(1)} %constant_dynamic-update-slice_fusion.13), channel_id=1, source_target_pairs={{0,32},{32,64},{64,96},{96,128},{128,160},{160,192},{192,224},{224... | collective-permute-start | bytes 786440 | tf_op jit(solution)/shard_map/while/body/eval_jaxpr/ppermute | solution.py:26
  80.8 8.5 %collective-permute-start.1 = (bf16[2,2,8,1024]{3,2,1,0:T(8,128)(2,1)S(1)}, bf16[2,2,8,1024]{3,2,1,0:T(8,128)(2,1)S(1)}, u32[]{:S(2)}, u32[]{:S(2)}) collective-permute-start(bf16[2,2,8,1024]{3,2,1,0:T(8,128)(2,1)S(1)} %get-tuple-element.1238), channel_id=1, source_target_pairs={{0,1},{1,2},{2,3},{3,4},{4,5},{5,6},{6,7},{7,8},{8,9},{9,10},{10,1... | collective-permute-start | bytes 196616 | tf_op jit(solution)/shard_map/while/body/eval_jaxpr/ppermute | solution.py:14
  94.5 10.7 %collective-permute-start.2 = (bf16[2,2,40,1024]{3,2,1,0:T(8,128)(2,1)S(1)}, bf16[2,2,40,1024]{3,2,1,0:T(8,128)(2,1)S(1)}, u32[]{:S(2)}, u32[]{:S(2)}) collective-permute-start(bf16[2,2,40,1024]{3,2,1,0:T(8,128)(2,1)S(1)} %pad_maximum_fusion.36), channel_id=1, source_target_pairs={{0,32},{32,64},{64,96},{96,128},{128,160},{160,192},{192,224},{224... | collective-permute-start | bytes 983048 | tf_op jit(solution)/shard_map/while/body/eval_jaxpr/ppermute | solution.py:26
  110.1 8.9 %collective-permute-start.3 = (bf16[2,2,32,1024]{3,2,1,0:T(8,128)(2,1)S(1)}, bf16[2,2,32,1024]{3,2,1,0:T(8,128)(2,1)}, u32[]{:S(2)}, u32[]{:S(2)}) collective-permute-start(bf16[2,2,32,1024]{3,2,1,0:T(8,128)(2,1)S(1)} %constant_dynamic-update-slice_fusion.13), channel_id=1, source_target_pairs={{0,32},{32,64},{64,96},{96,128},{128,160},{160,192},{192,224},{224... | collective-permute-start | bytes 786440 | tf_op jit(solution)/shard_map/while/body/eval_jaxpr/ppermute | solution.py:26
  122.0 8.3 %collective-permute-start.1 = (bf16[2,2,8,1024]{3,2,1,0:T(8,128)(2,1)S(1)}, bf16[2,2,8,1024]{3,2,1,0:T(8,128)(2,1)S(1)}, u32[]{:S(2)}, u32[]{:S(2)}) collective-permute-start(bf16[2,2,8,1024]{3,2,1,0:T(8,128)(2,1)S(1)} %get-tuple-element.1238), channel_id=1, source_target_pairs={{0,1},{1,2},{2,3},{3,4},{4,5},{5,6},{6,7},{7,8},{8,9},{9,10},{10,1... | collective-permute-start | bytes 196616 | tf_op jit(solution)/shard_map/while/body/eval_jaxpr/ppermute | solution.py:14
  135.5 10.9 %collective-permute-start.2 = (bf16[2,2,40,1024]{3,2,1,0:T(8,128)(2,1)S(1)}, bf16[2,2,40,1024]{3,2,1,0:T(8,128)(2,1)S(1)}, u32[]{:S(2)}, u32[]{:S(2)}) collective-permute-start(bf16[2,2,40,1024]{3,2,1,0:T(8,128)(2,1)S(1)} %pad_maximum_fusion.36), channel_id=1, source_target_pairs={{0,32},{32,64},{64,96},{96,128},{128,160},{160,192},{192,224},{224... | collective-permute-start | bytes 983048 | tf_op jit(solution)/shard_map/while/body/eval_jaxpr/ppermute | solution.py:26
  151.3 8.9 %collective-permute-start.3 = (bf16[2,2,32,1024]{3,2,1,0:T(8,128)(2,1)S(1)}, bf16[2,2,32,1024]{3,2,1,0:T(8,128)(2,1)}, u32[]{:S(2)}, u32[]{:S(2)}) collective-permute-start(bf16[2,2,32,1024]{3,2,1,0:T(8,128)(2,1)S(1)} %constant_dynamic-update-slice_fusion.13), channel_id=1, source_target_pairs={{0,32},{32,64},{64,96},{96,128},{128,160},{160,192},{192,224},{224... | collective-permute-start | bytes 786440 | tf_op jit(solution)/shard_map/while/body/eval_jaxpr/ppermute | solution.py:26
  163.2 8.3 %collective-permute-start.1 = (bf16[2,2,8,1024]{3,2,1,0:T(8,128)(2,1)S(1)}, bf16[2,2,8,1024]{3,2,1,0:T(8,128)(2,1)S(1)}, u32[]{:S(2)}, u32[]{:S(2)}) collective-permute-start(bf16[2,2,8,1024]{3,2,1,0:T(8,128)(2,1)S(1)} %get-tuple-element.1238), channel_id=1, source_target_pairs={{0,1},{1,2},{2,3},{3,4},{4,5},{5,6},{6,7},{7,8},{8,9},{9,10},{10,1... | collective-permute-start | bytes 196616 | tf_op jit(solution)/shard_map/while/body/eval_jaxpr/ppermute | solution.py:14
  176.7 10.9 %collective-permute-start.2 = (bf16[2,2,40,1024]{3,2,1,0:T(8,128)(2,1)S(1)}, bf16[2,2,40,1024]{3,2,1,0:T(8,128)(2,1)S(1)}, u32[]{:S(2)}, u32[]{:S(2)}) collective-permute-start(bf16[2,2,40,1024]{3,2,1,0:T(8,128)(2,1)S(1)} %pad_maximum_fusion.36), channel_id=1, source_target_pairs={{0,32},{32,64},{64,96},{96,128},{128,160},{160,192},{192,224},{224... | collective-permute-start | bytes 983048 | tf_op jit(solution)/shard_map/while/body/eval_jaxpr/ppermute | solution.py:26
  192.6 8.9 %collective-permute-start.3 = (bf16[2,2,32,1024]{3,2,1,0:T(8,128)(2,1)S(1)}, bf16[2,2,32,1024]{3,2,1,0:T(8,128)(2,1)}, u32[]{:S(2)}, u32[]{:S(2)}) collective-permute-start(bf16[2,2,32,1024]{3,2,1,0:T(8,128)(2,1)S(1)} %constant_dynamic-update-slice_fusion.13), channel_id=1, source_target_pairs={{0,32},{32,64},{64,96},{96,128},{128,160},{160,192},{192,224},{224... | collective-permute-start | bytes 786440 | tf_op jit(solution)/shard_map/while/body/eval_jaxpr/ppermute | solution.py:26
  204.4 8.3 %collective-permute-start.1 = (bf16[2,2,8,1024]{3,2,1,0:T(8,128)(2,1)S(1)}, bf16[2,2,8,1024]{3,2,1,0:T(8,128)(2,1)S(1)}, u32[]{:S(2)}, u32[]{:S(2)}) collective-permute-start(bf16[2,2,8,1024]{3,2,1,0:T(8,128)(2,1)S(1)} %get-tuple-element.1238), channel_id=1, source_target_pairs={{0,1},{1,2},{2,3},{3,4},{4,5},{5,6},{6,7},{7,8},{8,9},{9,10},{10,1... | collective-permute-start | bytes 196616 | tf_op jit(solution)/shard_map/while/body/eval_jaxpr/ppermute | solution.py:14
  218.0 10.9 %collective-permute-start.2 = (bf16[2,2,40,1024]{3,2,1,0:T(8,128)(2,1)S(1)}, bf16[2,2,40,1024]{3,2,1,0:T(8,128)(2,1)S(1)}, u32[]{:S(2)}, u32[]{:S(2)}) collective-permute-start(bf16[2,2,40,1024]{3,2,1,0:T(8,128)(2,1)S(1)} %pad_maximum_fusion.36), channel_id=1, source_target_pairs={{0,32},{32,64},{64,96},{96,128},{128,160},{160,192},{192,224},{224... | collective-permute-start | bytes 983048 | tf_op jit(solution)/shard_map/while/body/eval_jaxpr/ppermute | solution.py:26
  233.8 8.9 %collective-permute-start.3 = (bf16[2,2,32,1024]{3,2,1,0:T(8,128)(2,1)S(1)}, bf16[2,2,32,1024]{3,2,1,0:T(8,128)(2,1)}, u32[]{:S(2)}, u32[]{:S(2)}) collective-permute-start(bf16[2,2,32,1024]{3,2,1,0:T(8,128)(2,1)S(1)} %constant_dynamic-update-slice_fusion.13), channel_id=1, source_target_pairs={{0,32},{32,64},{64,96},{96,128},{128,160},{160,192},{192,224},{224... | collective-permute-start | bytes 786440 | tf_op jit(solution)/shard_map/while/body/eval_jaxpr/ppermute | solution.py:26
  245.6 8.3 %collective-permute-start.1 = (bf16[2,2,8,1024]{3,2,1,0:T(8,128)(2,1)S(1)}, bf16[2,2,8,1024]{3,2,1,0:T(8,128)(2,1)S(1)}, u32[]{:S(2)}, u32[]{:S(2)}) collective-permute-start(bf16[2,2,8,1024]{3,2,1,0:T(8,128)(2,1)S(1)} %get-tuple-element.1238), channel_id=1, source_target_pairs={{0,1},{1,2},{2,3},{3,4},{4,5},{5,6},{6,7},{7,8},{8,9},{9,10},{10,1... | collective-permute-start | bytes 196616 | tf_op jit(solution)/shard_map/while/body/eval_jaxpr/ppermute | solution.py:14
  259.2 10.9 %collective-permute-start.2 = (bf16[2,2,40,1024]{3,2,1,0:T(8,128)(2,1)S(1)}, bf16[2,2,40,1024]{3,2,1,0:T(8,128)(2,1)S(1)}, u32[]{:S(2)}, u32[]{:S(2)}) collective-permute-start(bf16[2,2,40,1024]{3,2,1,0:T(8,128)(2,1)S(1)} %pad_maximum_fusion.36), channel_id=1, source_target_pairs={{0,32},{32,64},{64,96},{96,128},{128,160},{160,192},{192,224},{224... | collective-permute-start | bytes 983048 | tf_op jit(solution)/shard_map/while/body/eval_jaxpr/ppermute | solution.py:26
  275.0 8.9 %collective-permute-start.3 = (bf16[2,2,32,1024]{3,2,1,0:T(8,128)(2,1)S(1)}, bf16[2,2,32,1024]{3,2,1,0:T(8,128)(2,1)}, u32[]{:S(2)}, u32[]{:S(2)}) collective-permute-start(bf16[2,2,32,1024]{3,2,1,0:T(8,128)(2,1)S(1)} %constant_dynamic-update-slice_fusion.13), channel_id=1, source_target_pairs={{0,32},{32,64},{64,96},{96,128},{128,160},{160,192},{192,224},{224... | collective-permute-start | bytes 786440 | tf_op jit(solution)/shard_map/while/body/eval_jaxpr/ppermute | solution.py:26
  286.8 8.3 %collective-permute-start.1 = (bf16[2,2,8,1024]{3,2,1,0:T(8,128)(2,1)S(1)}, bf16[2,2,8,1024]{3,2,1,0:T(8,128)(2,1)S(1)}, u32[]{:S(2)}, u32[]{:S(2)}) collective-permute-start(bf16[2,2,8,1024]{3,2,1,0:T(8,128)(2,1)S(1)} %get-tuple-element.1238), channel_id=1, source_target_pairs={{0,1},{1,2},{2,3},{3,4},{4,5},{5,6},{6,7},{7,8},{8,9},{9,10},{10,1... | collective-permute-start | bytes 196616 | tf_op jit(solution)/shard_map/while/body/eval_jaxpr/ppermute | solution.py:14
  300.4 10.9 %collective-permute-start.2 = (bf16[2,2,40,1024]{3,2,1,0:T(8,128)(2,1)S(1)}, bf16[2,2,40,1024]{3,2,1,0:T(8,128)(2,1)S(1)}, u32[]{:S(2)}, u32[]{:S(2)}) collective-permute-start(bf16[2,2,40,1024]{3,2,1,0:T(8,128)(2,1)S(1)} %pad_maximum_fusion.36), channel_id=1, source_target_pairs={{0,32},{32,64},{64,96},{96,128},{128,160},{160,192},{192,224},{224... | collective-permute-start | bytes 983048 | tf_op jit(solution)/shard_map/while/body/eval_jaxpr/ppermute | solution.py:26
  316.2 8.9 %collective-permute-start.3 = (bf16[2,2,32,1024]{3,2,1,0:T(8,128)(2,1)S(1)}, bf16[2,2,32,1024]{3,2,1,0:T(8,128)(2,1)}, u32[]{:S(2)}, u32[]{:S(2)}) collective-permute-start(bf16[2,2,32,1024]{3,2,1,0:T(8,128)(2,1)S(1)} %constant_dynamic-update-slice_fusion.13), channel_id=1, source_target_pairs={{0,32},{32,64},{64,96},{96,128},{128,160},{160,192},{192,224},{224... | collective-permute-start | bytes 786440 | tf_op jit(solution)/shard_map/while/body/eval_jaxpr/ppermute | solution.py:26
  328.0 8.3 %collective-permute-start.1 = (bf16[2,2,8,1024]{3,2,1,0:T(8,128)(2,1)S(1)}, bf16[2,2,8,1024]{3,2,1,0:T(8,128)(2,1)S(1)}, u32[]{:S(2)}, u32[]{:S(2)}) collective-permute-start(bf16[2,2,8,1024]{3,2,1,0:T(8,128)(2,1)S(1)} %get-tuple-element.1238), channel_id=1, source_target_pairs={{0,1},{1,2},{2,3},{3,4},{4,5},{5,6},{6,7},{7,8},{8,9},{9,10},{10,1... | collective-permute-start | bytes 196616 | tf_op jit(solution)/shard_map/while/body/eval_jaxpr/ppermute | solution.py:14
  341.6 10.9 %collective-permute-start.2 = (bf16[2,2,40,1024]{3,2,1,0:T(8,128)(2,1)S(1)}, bf16[2,2,40,1024]{3,2,1,0:T(8,128)(2,1)S(1)}, u32[]{:S(2)}, u32[]{:S(2)}) collective-permute-start(bf16[2,2,40,1024]{3,2,1,0:T(8,128)(2,1)S(1)} %pad_maximum_fusion.36), channel_id=1, source_target_pairs={{0,32},{32,64},{64,96},{96,128},{128,160},{160,192},{192,224},{224... | collective-permute-start | bytes 983048 | tf_op jit(solution)/shard_map/while/body/eval_jaxpr/ppermute | solution.py:26
  357.4 8.9 %collective-permute-start.3 = (bf16[2,2,32,1024]{3,2,1,0:T(8,128)(2,1)S(1)}, bf16[2,2,32,1024]{3,2,1,0:T(8,128)(2,1)}, u32[]{:S(2)}, u32[]{:S(2)}) collective-permute-start(bf16[2,2,32,1024]{3,2,1,0:T(8,128)(2,1)S(1)} %constant_dynamic-update-slice_fusion.13), channel_id=1, source_target_pairs={{0,32},{32,64},{64,96},{96,128},{128,160},{160,192},{192,224},{224... | collective-permute-start | bytes 786440 | tf_op jit(solution)/shard_map/while/body/eval_jaxpr/ppermute | solution.py:26
  370.5 8.3 %collective-permute-start.5 = (bf16[2,2,8,1024]{3,2,1,0:T(8,128)(2,1)S(1)}, bf16[2,2,8,1024]{3,2,1,0:T(8,128)(2,1)S(1)}, u32[]{:S(2)}, u32[]{:S(2)}) collective-permute-start(bf16[2,2,8,1024]{3,2,1,0:T(8,128)(2,1)S(1)} %get-tuple-element.1271), channel_id=1, source_target_pairs={{0,1},{1,2},{2,3},{3,4},{4,5},{5,6},{6,7},{7,8},{8,9},{9,10},{10,1... | collective-permute-start | bytes 196616 | tf_op jit(solution)/shard_map/while/body/eval_jaxpr/ppermute | solution.py:14
  382.8 11.6 %collective-permute-start.6 = (bf16[2,2,40,1024]{3,2,1,0:T(8,128)(2,1)S(1)}, bf16[2,2,40,1024]{3,2,1,0:T(8,128)(2,1)S(1)}, u32[]{:S(2)}, u32[]{:S(2)}) collective-permute-start(bf16[2,2,40,1024]{3,2,1,0:T(8,128)(2,1)S(1)} %pad_maximum_fusion.42), channel_id=1, source_target_pairs={{32,0},{64,32},{96,64},{128,96},{160,128},{192,160},{224,192},{256... | collective-permute-start | bytes 983048 | tf_op jit(solution)/shard_map/while/body/eval_jaxpr/ppermute | solution.py:26
  399.0 9.1 %collective-permute-start.7 = (bf16[2,2,32,1024]{3,2,1,0:T(8,128)(2,1)}, bf16[2,2,32,1024]{3,2,1,0:T(8,128)(2,1)S(1)}, u32[]{:S(2)}, u32[]{:S(2)}) collective-permute-start(bf16[2,2,32,1024]{3,2,1,0:T(8,128)(2,1)} %pad_maximum_fusion.44), channel_id=1, source_target_pairs={{32,0},{64,32},{96,64},{128,96},{160,128},{192,160},{224,192},{256... | collective-permute-start | bytes 786440 | tf_op jit(solution)/shard_map/while/body/eval_jaxpr/ppermute | solution.py:26
  410.2 8.3 %collective-permute-start.5 = (bf16[2,2,8,1024]{3,2,1,0:T(8,128)(2,1)S(1)}, bf16[2,2,8,1024]{3,2,1,0:T(8,128)(2,1)S(1)}, u32[]{:S(2)}, u32[]{:S(2)}) collective-permute-start(bf16[2,2,8,1024]{3,2,1,0:T(8,128)(2,1)S(1)} %get-tuple-element.1271), channel_id=1, source_target_pairs={{0,1},{1,2},{2,3},{3,4},{4,5},{5,6},{6,7},{7,8},{8,9},{9,10},{10,1... | collective-permute-start | bytes 196616 | tf_op jit(solution)/shard_map/while/body/eval_jaxpr/ppermute | solution.py:14
  422.4 9.6 %collective-permute-start.6 = (bf16[2,2,40,1024]{3,2,1,0:T(8,128)(2,1)S(1)}, bf16[2,2,40,1024]{3,2,1,0:T(8,128)(2,1)S(1)}, u32[]{:S(2)}, u32[]{:S(2)}) collective-permute-start(bf16[2,2,40,1024]{3,2,1,0:T(8,128)(2,1)S(1)} %pad_maximum_fusion.42), channel_id=1, source_target_pairs={{32,0},{64,32},{96,64},{128,96},{160,128},{192,160},{224,192},{256... | collective-permute-start | bytes 983048 | tf_op jit(solution)/shard_map/while/body/eval_jaxpr/ppermute | solution.py:26
  436.7 9.1 %collective-permute-start.7 = (bf16[2,2,32,1024]{3,2,1,0:T(8,128)(2,1)}, bf16[2,2,32,1024]{3,2,1,0:T(8,128)(2,1)S(1)}, u32[]{:S(2)}, u32[]{:S(2)}) collective-permute-start(bf16[2,2,32,1024]{3,2,1,0:T(8,128)(2,1)} %pad_maximum_fusion.44), channel_id=1, source_target_pairs={{32,0},{64,32},{96,64},{128,96},{160,128},{192,160},{224,192},{256... | collective-permute-start | bytes 786440 | tf_op jit(solution)/shard_map/while/body/eval_jaxpr/ppermute | solution.py:26
  447.8 8.3 %collective-permute-start.5 = (bf16[2,2,8,1024]{3,2,1,0:T(8,128)(2,1)S(1)}, bf16[2,2,8,1024]{3,2,1,0:T(8,128)(2,1)S(1)}, u32[]{:S(2)}, u32[]{:S(2)}) collective-permute-start(bf16[2,2,8,1024]{3,2,1,0:T(8,128)(2,1)S(1)} %get-tuple-element.1271), channel_id=1, source_target_pairs={{0,1},{1,2},{2,3},{3,4},{4,5},{5,6},{6,7},{7,8},{8,9},{9,10},{10,1... | collective-permute-start | bytes 196616 | tf_op jit(solution)/shard_map/while/body/eval_jaxpr/ppermute | solution.py:14
  460.0 9.6 %collective-permute-start.6 = (bf16[2,2,40,1024]{3,2,1,0:T(8,128)(2,1)S(1)}, bf16[2,2,40,1024]{3,2,1,0:T(8,128)(2,1)S(1)}, u32[]{:S(2)}, u32[]{:S(2)}) collective-permute-start(bf16[2,2,40,1024]{3,2,1,0:T(8,128)(2,1)S(1)} %pad_maximum_fusion.42), channel_id=1, source_target_pairs={{32,0},{64,32},{96,64},{128,96},{160,128},{192,160},{224,192},{256... | collective-permute-start | bytes 983048 | tf_op jit(solution)/shard_map/while/body/eval_jaxpr/ppermute | solution.py:26
  474.3 9.1 %collective-permute-start.7 = (bf16[2,2,32,1024]{3,2,1,0:T(8,128)(2,1)}, bf16[2,2,32,1024]{3,2,1,0:T(8,128)(2,1)S(1)}, u32[]{:S(2)}, u32[]{:S(2)}) collective-permute-start(bf16[2,2,32,1024]{3,2,1,0:T(8,128)(2,1)} %pad_maximum_fusion.44), channel_id=1, source_target_pairs={{32,0},{64,32},{96,64},{128,96},{160,128},{192,160},{224,192},{256... | collective-permute-start | bytes 786440 | tf_op jit(solution)/shard_map/while/body/eval_jaxpr/ppermute | solution.py:26
  485.4 8.3 %collective-permute-start.5 = (bf16[2,2,8,1024]{3,2,1,0:T(8,128)(2,1)S(1)}, bf16[2,2,8,1024]{3,2,1,0:T(8,128)(2,1)S(1)}, u32[]{:S(2)}, u32[]{:S(2)}) collective-permute-start(bf16[2,2,8,1024]{3,2,1,0:T(8,128)(2,1)S(1)} %get-tuple-element.1271), channel_id=1, source_target_pairs={{0,1},{1,2},{2,3},{3,4},{4,5},{5,6},{6,7},{7,8},{8,9},{9,10},{10,1... | collective-permute-start | bytes 196616 | tf_op jit(solution)/shard_map/while/body/eval_jaxpr/ppermute | solution.py:14
  497.7 9.6 %collective-permute-start.6 = (bf16[2,2,40,1024]{3,2,1,0:T(8,128)(2,1)S(1)}, bf16[2,2,40,1024]{3,2,1,0:T(8,128)(2,1)S(1)}, u32[]{:S(2)}, u32[]{:S(2)}) collective-permute-start(bf16[2,2,40,1024]{3,2,1,0:T(8,128)(2,1)S(1)} %pad_maximum_fusion.42), channel_id=1, source_target_pairs={{32,0},{64,32},{96,64},{128,96},{160,128},{192,160},{224,192},{256... | collective-permute-start | bytes 983048 | tf_op jit(solution)/shard_map/while/body/eval_jaxpr/ppermute | solution.py:26
  511.9 9.1 %collective-permute-start.7 = (bf16[2,2,32,1024]{3,2,1,0:T(8,128)(2,1)}, bf16[2,2,32,1024]{3,2,1,0:T(8,128)(2,1)S(1)}, u32[]{:S(2)}, u32[]{:S(2)}) collective-permute-start(bf16[2,2,32,1024]{3,2,1,0:T(8,128)(2,1)} %pad_maximum_fusion.44), channel_id=1, source_target_pairs={{32,0},{64,32},{96,64},{128,96},{160,128},{192,160},{224,192},{256... | collective-permute-start | bytes 786440 | tf_op jit(solution)/shard_map/while/body/eval_jaxpr/ppermute | solution.py:26
  523.1 8.3 %collective-permute-start.5 = (bf16[2,2,8,1024]{3,2,1,0:T(8,128)(2,1)S(1)}, bf16[2,2,8,1024]{3,2,1,0:T(8,128)(2,1)S(1)}, u32[]{:S(2)}, u32[]{:S(2)}) collective-permute-start(bf16[2,2,8,1024]{3,2,1,0:T(8,128)(2,1)S(1)} %get-tuple-element.1271), channel_id=1, source_target_pairs={{0,1},{1,2},{2,3},{3,4},{4,5},{5,6},{6,7},{7,8},{8,9},{9,10},{10,1... | collective-permute-start | bytes 196616 | tf_op jit(solution)/shard_map/while/body/eval_jaxpr/ppermute | solution.py:14
  535.3 9.6 %collective-permute-start.6 = (bf16[2,2,40,1024]{3,2,1,0:T(8,128)(2,1)S(1)}, bf16[2,2,40,1024]{3,2,1,0:T(8,128)(2,1)S(1)}, u32[]{:S(2)}, u32[]{:S(2)}) collective-permute-start(bf16[2,2,40,1024]{3,2,1,0:T(8,128)(2,1)S(1)} %pad_maximum_fusion.42), channel_id=1, source_target_pairs={{32,0},{64,32},{96,64},{128,96},{160,128},{192,160},{224,192},{256... | collective-permute-start | bytes 983048 | tf_op jit(solution)/shard_map/while/body/eval_jaxpr/ppermute | solution.py:26
  549.6 9.1 %collective-permute-start.7 = (bf16[2,2,32,1024]{3,2,1,0:T(8,128)(2,1)}, bf16[2,2,32,1024]{3,2,1,0:T(8,128)(2,1)S(1)}, u32[]{:S(2)}, u32[]{:S(2)}) collective-permute-start(bf16[2,2,32,1024]{3,2,1,0:T(8,128)(2,1)} %pad_maximum_fusion.44), channel_id=1, source_target_pairs={{32,0},{64,32},{96,64},{128,96},{160,128},{192,160},{224,192},{256... | collective-permute-start | bytes 786440 | tf_op jit(solution)/shard_map/while/body/eval_jaxpr/ppermute | solution.py:26
  560.7 8.3 %collective-permute-start.5 = (bf16[2,2,8,1024]{3,2,1,0:T(8,128)(2,1)S(1)}, bf16[2,2,8,1024]{3,2,1,0:T(8,128)(2,1)S(1)}, u32[]{:S(2)}, u32[]{:S(2)}) collective-permute-start(bf16[2,2,8,1024]{3,2,1,0:T(8,128)(2,1)S(1)} %get-tuple-element.1271), channel_id=1, source_target_pairs={{0,1},{1,2},{2,3},{3,4},{4,5},{5,6},{6,7},{7,8},{8,9},{9,10},{10,1... | collective-permute-start | bytes 196616 | tf_op jit(solution)/shard_map/while/body/eval_jaxpr/ppermute | solution.py:14
  572.9 9.6 %collective-permute-start.6 = (bf16[2,2,40,1024]{3,2,1,0:T(8,128)(2,1)S(1)}, bf16[2,2,40,1024]{3,2,1,0:T(8,128)(2,1)S(1)}, u32[]{:S(2)}, u32[]{:S(2)}) collective-permute-start(bf16[2,2,40,1024]{3,2,1,0:T(8,128)(2,1)S(1)} %pad_maximum_fusion.42), channel_id=1, source_target_pairs={{32,0},{64,32},{96,64},{128,96},{160,128},{192,160},{224,192},{256... | collective-permute-start | bytes 983048 | tf_op jit(solution)/shard_map/while/body/eval_jaxpr/ppermute | solution.py:26
  587.2 9.1 %collective-permute-start.7 = (bf16[2,2,32,1024]{3,2,1,0:T(8,128)(2,1)}, bf16[2,2,32,1024]{3,2,1,0:T(8,128)(2,1)S(1)}, u32[]{:S(2)}, u32[]{:S(2)}) collective-permute-start(bf16[2,2,32,1024]{3,2,1,0:T(8,128)(2,1)} %pad_maximum_fusion.44), channel_id=1, source_target_pairs={{32,0},{64,32},{96,64},{128,96},{160,128},{192,160},{224,192},{256... | collective-permute-start | bytes 786440 | tf_op jit(solution)/shard_map/while/body/eval_jaxpr/ppermute | solution.py:26
  610.6 9.6 %collective-permute-start.6 = (bf16[2,2,40,1024]{3,2,1,0:T(8,128)(2,1)S(1)}, bf16[2,2,40,1024]{3,2,1,0:T(8,128)(2,1)S(1)}, u32[]{:S(2)}, u32[]{:S(2)}) collective-permute-start(bf16[2,2,40,1024]{3,2,1,0:T(8,128)(2,1)S(1)} %pad_maximum_fusion.42), channel_id=1, source_target_pairs={{32,0},{64,32},{96,64},{128,96},{160,128},{192,160},{224,192},{256... | collective-permute-start | bytes 983048 | tf_op jit(solution)/shard_map/while/body/eval_jaxpr/ppermute | solution.py:26
  624.8 9.1 %collective-permute-start.7 = (bf16[2,2,32,1024]{3,2,1,0:T(8,128)(2,1)}, bf16[2,2,32,1024]{3,2,1,0:T(8,128)(2,1)S(1)}, u32[]{:S(2)}, u32[]{:S(2)}) collective-permute-start(bf16[2,2,32,1024]{3,2,1,0:T(8,128)(2,1)} %pad_maximum_fusion.44), channel_id=1, source_target_pairs={{32,0},{64,32},{96,64},{128,96},{160,128},{192,160},{224,192},{256... | collective-permute-start | bytes 786440 | tf_op jit(solution)/shard_map/while/body/eval_jaxpr/ppermute | solution.py:26
  648.2 9.6 %collective-permute-start.6 = (bf16[2,2,40,1024]{3,2,1,0:T(8,128)(2,1)S(1)}, bf16[2,2,40,1024]{3,2,1,0:T(8,128)(2,1)S(1)}, u32[]{:S(2)}, u32[]{:S(2)}) collective-permute-start(bf16[2,2,40,1024]{3,2,1,0:T(8,128)(2,1)S(1)} %pad_maximum_fusion.42), channel_id=1, source_target_pairs={{32,0},{64,32},{96,64},{128,96},{160,128},{192,160},{224,192},{256... | collective-permute-start | bytes 983048 | tf_op jit(solution)/shard_map/while/body/eval_jaxpr/ppermute | solution.py:26
  662.5 9.1 %collective-permute-start.7 = (bf16[2,2,32,1024]{3,2,1,0:T(8,128)(2,1)}, bf16[2,2,32,1024]{3,2,1,0:T(8,128)(2,1)S(1)}, u32[]{:S(2)}, u32[]{:S(2)}) collective-permute-start(bf16[2,2,32,1024]{3,2,1,0:T(8,128)(2,1)} %pad_maximum_fusion.44), channel_id=1, source_target_pairs={{32,0},{64,32},{96,64},{128,96},{160,128},{192,160},{224,192},{256... | collective-permute-start | bytes 786440 | tf_op jit(solution)/shard_map/while/body/eval_jaxpr/ppermute | solution.py:26
  (69 other events, 845.0 us)
where the time goes:
time: 694 us; the launch traced here: 686 us
  waiting for transfers between devices  242 us (35%)
  starting transfers between devices  233 us (34%)
  matrix products  106 us (15%)
  other arithmetic  62 us (9%)
  local copies, waits for them, and re-layouts  29.5 us (4%)
  loops' own time  13.5 us (2%)
    ppermute x32, waiting for transfers between devices, from_behind(): return lax.ppermute(array, axis, pairs)  161 us
    ppermute x32, starting transfers between devices, from_behind(): return lax.ppermute(array, axis, pairs)  131 us
    ppermute x17, waiting for transfers between devices, with_halo(): lax.ppermute(tail, axis, [(i, (i + 1) % count) for i in range(count)])  80.8 us
    ppermute x17, starting transfers between devices, with_halo(): lax.ppermute(tail, axis, [(i, (i + 1) % count) for i in range(count)])  55.5 us
    ppermute x17, starting transfers between devices, with_halo(): lax.ppermute(head, axis, [((i + 1) % count, i) for i in range(count)])  46.5 us
    dot_general x32, matrix products, along_rows(): jnp.einsum('rq,xpqc->xprc', real_mat, field_in, preferred_element_type=jn...  30.6 us
    dot_general x32, matrix products, along_rows(): jnp.einsum('rq,xpqc->xprc', imag_mat, field_in, preferred_element_type=jn...  30.6 us
    dot_general x32, matrix products, along_cols(): jnp.einsum('xprbq,qo->xprbo', slab_rows, real_slab, preferred_element_typ...  22.5 us
  transfers between devices with their start and end apart: 66, of which 48 were waited for; matrix products, arithmetic and copies ran while one was open for 3% of the time, Pallas kernels for 0%

commit v1 on v0

v1 whole, which is shorter than its diff:
```python
import functools

import jax
import jax.numpy as jnp
from jax import lax
from jax.experimental import pallas as pl
from jax.experimental.pallas import tpu as pltpu
from jax.sharding import PartitionSpec as P

F32 = jnp.float32
BF16 = jnp.bfloat16
LANES = 128
VMEM_BYTES = 40 * 1024 * 1024


def vmem_spec():
    return pl.BlockSpec(memory_space=pltpu.VMEM)


def smem_spec():
    return pl.BlockSpec(memory_space=pltpu.SMEM)


def call(body, outs, scalars, arrays, flops, moved):
    return pl.pallas_call(
        body,
        out_shape=outs,
        in_specs=[smem_spec()] * len(scalars) + [vmem_spec()] * len(arrays),
        out_specs=jax.tree.map(lambda _: vmem_spec(), outs),
        compiler_params=pltpu.CompilerParams(vmem_limit_bytes=VMEM_BYTES),
        cost_estimate=pl.CostEstimate(flops=flops, bytes_accessed=moved, transcendentals=0),
    )(*scalars, *arrays)


def prepare_body(dims, meta, potential, incident, measured, sent, start, target):
    probes, tiles, halo, window, columns = dims
    width = 2 * halo + LANES
    span = window + 2 * halo
    lane = lax.broadcasted_iota(jnp.int32, (potential.shape[2], span), 1)
    inside = (lane >= halo) & (lane < window + halo)
    for probe in range(probes):
        half = meta[3 + probe]
        turn = lax.rem(columns + halo - meta[3 + probes + probe], columns)
        phase = pltpu.roll(potential[0, half], turn, 1)[:, :span]
        absorb = pltpu.roll(potential[1, half], turn, 1)[:, :span]
        damping = jnp.where(inside, jnp.exp(-absorb), 0.0)
        real = (damping * jnp.cos(phase)).astype(BF16)
        imag = (damping * jnp.sin(phase)).astype(BF16)
        for tile in range(tiles):
            cols = slice(tile * LANES, tile * LANES + width)
            sent[probe * tiles + tile, 0] = real[:, cols]
            sent[probe * tiles + tile, 1] = imag[:, cols]
    own = meta[0]
    turn = lax.rem(window + halo - meta[1] * LANES, window)
    for part in range(2):
        start[part] = pltpu.roll(incident[part, own], turn, 1)[:, :width].astype(BF16)
    target[...] = pltpu.roll(measured[own], turn, 1)[:, :width]


def banded(taps, base, diff, half_width, conj):
    count = 2 * half_width + 1
    real = jnp.zeros(diff.shape, F32)
    imag = jnp.zeros(diff.shape, F32)
    for tap in range(count):
        hit = diff == tap - half_width
        source = count - 1 - tap if conj else tap
        real = jnp.where(hit, taps[source], real)
        value = taps[count + source]
        imag = jnp.where(hit, -value if conj else value, imag)
    return real, imag


def matrices_body(dims, meta, taps, row_fwd, row_bwd, col_fwd, col_bwd):
    band, window, half_width, width = dims
    rows = 3 * band
    out_row = lax.broadcasted_iota(jnp.int32, (rows, rows), 0)
    in_row = lax.broadcasted_iota(jnp.int32, (rows, rows), 1)
    at = in_row + (meta[2] - 1) * band
    row_diff = jnp.where((at >= 0) & (at < window), in_row - out_row, window)
    in_col = lax.broadcasted_iota(jnp.int32, (width, width), 0)
    out_col = lax.broadcasted_iota(jnp.int32, (width, width), 1)
    for conj, row_out, col_out in ((False, row_fwd, col_fwd), (True, row_bwd, col_bwd)):
        real, imag = banded(taps, meta, row_diff, half_width, conj)
        row_out[:rows] = real.astype(BF16)
        row_out[rows:] = imag.astype(BF16)
        real, imag = banded(taps, meta, in_col - out_col, half_width, conj)
        col_out[:width, :width] = real.astype(BF16)
        col_out[:width, width:] = imag.astype(BF16)
        col_out[width:, :width] = (-imag).astype(BF16)
        col_out[width:, width:] = real.astype(BF16)


def stacked(above, own, below, index):
    return jnp.concatenate([above[index], own[index], below[index]], axis=0).astype(F32)


def spread_rows(matrix, field, width):
    both = jnp.dot(matrix, field, preferred_element_type=F32)
    rows = matrix.shape[1]
    direct, crossed = both[:rows], both[rows:]
    return direct[:, :width] - crossed[:, width:], direct[:, width:] + crossed[:, :width]


def forward_steps(steps, band, width, row_mat, col_mat, above, own, below, psi_re, psi_im, kept):
    for step in range(steps):
        t_re = stacked(above, own, below, (step, 0))
        t_im = stacked(above, own, below, (step, 1))
        product = jnp.concatenate(
            [t_re * psi_re - t_im * psi_im, t_re * psi_im + t_im * psi_re], axis=1
        ).astype(BF16)
        kept[step] = product[band : 2 * band]
        h_re, h_im = spread_rows(row_mat[...], product, width)
        spread = jnp.concatenate([h_re, h_im], axis=1).astype(BF16)
        psi = jnp.dot(spread, col_mat[...], preferred_element_type=F32)
        psi_re, psi_im = psi[:, :width], psi[:, width:]
    return psi_re[band : 2 * band], psi_im[band : 2 * band]


def first_forward_body(dims, row_mat, col_mat, above, own, below, kept, leaving):
    steps, band, width = dims
    psi_re = stacked(above, own, below, (steps, 0))
    psi_im = stacked(above, own, below, (steps, 1))
    psi_re, psi_im = forward_steps(
        steps, band, width, row_mat, col_mat, above, own, below, psi_re, psi_im, kept
    )
    leaving[0] = psi_re.astype(BF16)
    leaving[1] = psi_im.astype(BF16)


def second_forward_body(
    dims, row_mat, col_mat, above, own, below, w_above, w_own, w_below, target, kept, seed
):
    steps, band, width = dims
    psi_re = stacked(w_above, w_own, w_below, 0)
    psi_im = stacked(w_above, w_own, w_below, 1)
    psi_re, psi_im = forward_steps(
        steps, band, width, row_mat, col_mat, above, own, below, psi_re, psi_im, kept
    )
    twice = 2.0 * (psi_re * psi_re + psi_im * psi_im - target[...])
    g_re, g_im = twice * psi_re, twice * psi_im
    low = lax.broadcasted_iota(jnp.int32, (band, LANES), 1) < LANES // 2
    turned = pltpu.roll(g_re[:, :LANES], LANES // 2, 1)
    seed[:, :LANES] = jnp.where(low, turned, g_im[:, :LANES]).astype(BF16)
    turned = pltpu.roll(g_im[:, LANES:], LANES // 2, 1)
    seed[:, LANES:] = jnp.where(low, g_re[:, LANES:], turned).astype(BF16)


def backward_steps(
    steps, first, band, width, row_mat, col_mat, above, own, below, g_re, g_im, kept, terms
):
    field = jnp.concatenate([g_re, g_im], axis=1).astype(BF16)
    for step in reversed(range(steps)):
        spread = jnp.dot(field, col_mat[...], preferred_element_type=F32).astype(BF16)
        w_re, w_im = spread_rows(row_mat[...], spread, width)
        product = kept[step].astype(F32)
        u_re, u_im = product[:, :width], product[:, width:]
        v_re, v_im = w_re[band : 2 * band], w_im[band : 2 * band]
        turned = pltpu.roll(u_re * v_im - u_im * v_re, width - LANES // 2, 1)
        terms[first + step, 0] = turned[:, :LANES].astype(BF16)
        turned = pltpu.roll(-(u_re * v_re + u_im * v_im), width - LANES // 2, 1)
        terms[first + step, 1] = turned[:, :LANES].astype(BF16)
        t_re = stacked(above, own, below, (step, 0))
        t_im = stacked(above, own, below, (step, 1))
        field = jnp.concatenate(
            [t_re * w_re + t_im * w_im, t_re * w_im - t_im * w_re], axis=1
        ).astype(BF16)
    return field


def first_backward_body(
    dims, row_mat, col_mat, above, own, below, seeds, left, right, kept, leaving, terms
):
    steps, band, width = dims
    half = LANES // 2
    middle = seeds[...].reshape(3 * band, 2 * LANES).astype(F32)
    left_in = left[...].reshape(3 * band, LANES).astype(F32)
    right_in = right[...].reshape(3 * band, LANES).astype(F32)
    low = lax.broadcasted_iota(jnp.int32, (3 * band, LANES), 1) < half
    first, last = middle[:, :LANES], middle[:, LANES:]
    g_re = jnp.concatenate(
        [
            jnp.where(low, left_in, pltpu.roll(first, half, 1)),
            jnp.where(low, last, pltpu.roll(right_in, half, 1)),
        ],
        axis=1,
    )
    g_im = jnp.concatenate(
        [
            jnp.where(low, pltpu.roll(left_in, half, 1), first),
            jnp.where(low, pltpu.roll(last, half, 1), right_in),
        ],
        axis=1,
    )
    field = backward_steps(
        steps, 0, band, width, row_mat, col_mat, above, own, below, g_re, g_im, kept, terms
    )
    leaving[0] = field[band : 2 * band, :width]
    leaving[1] = field[band : 2 * band, width:]


def second_backward_body(
    dims, row_mat, col_mat, above, own, below, w_above, w_own, w_below, kept, later, terms
):
    steps, band, width = dims
    terms[steps:] = later[...]
    g_re = stacked(w_above, w_own, w_below, 0)
    g_im = stacked(w_above, w_own, w_below, 1)
    backward_steps(
        steps, 0, band, width, row_mat, col_mat, above, own, below, g_re, g_im, kept, terms
    )


def collect_body(dims, meta, terms, gradient):
    probes, tiles, window, columns = dims
    band = terms.shape[2]
    rest = jnp.zeros((band, columns - window), F32)
    for part in range(2):
        moved = []
        for probe in range(probes):
            pieces = [terms[probe * tiles + tile, part].astype(F32) for tile in range(tiles)]
            row = jnp.concatenate(pieces + [rest], axis=1)
            moved.append(pltpu.roll(row, meta[3 + probes + probe], 1))
        for half in range(2):
            total = jnp.zeros((band, columns), F32)
            for probe in range(probes):
                total = total + jnp.where(meta[3 + probe] == half, moved[probe], 0.0)
            gradient[part, half] = total


def local(potential, incident, measured, offsets, kernel):
    lat_count = lax.axis_size("lat")
    depth_count = lax.axis_size("depth")
    lat_index = lax.axis_index("lat")
    depth_index = lax.axis_index("depth")
    band = potential.shape[3]
    columns = potential.shape[4]
    window = incident.shape[3]
    probes = incident.shape[1]
    half_width = (kernel.shape[1] - 1) // 2
    tiles = depth_count // probes
    steps = depth_count // 2
    halo = depth_count * half_width
    width = 2 * halo + LANES

    first_band = offsets[:, 0] // band
    place = (lat_index - first_band) % lat_count
    halves = (first_band + place) // lat_count
    own_probe = depth_index // tiles
    head = jnp.stack([own_probe, depth_index % tiles, jnp.where(own_probe == 0, place[0], place[1])])
    meta = jnp.concatenate([head, halves, offsets[:, 1]]).astype(jnp.int32)
    taps = kernel.astype(F32).reshape(-1)

    downward = [(i, (i + 1) % lat_count) for i in range(lat_count)]
    upward = [((i + 1) % lat_count, i) for i in range(lat_count)]
    inner = [i for i in range(depth_count - 1) if (i + 1) % tiles]

    def row_halo(cells):
        return lax.ppermute(cells, "lat", downward), lax.ppermute(cells, "lat", upward)

    def shape(*dims, dtype=BF16):
        return jax.ShapeDtypeStruct(dims, dtype)

    rows = 3 * band
    sent, start, target = call(
        functools.partial(prepare_body, (probes, tiles, halo, window, columns)),
        (
            shape(depth_count, 2, band, width),
            shape(2, band, width),
            shape(band, width, dtype=F32),
        ),
        [meta],
        [potential[:, 0], incident, measured],
        10_000_000,
        3_000_000,
    )
    row_fwd, row_bwd, col_fwd, col_bwd = call(
        functools.partial(matrices_body, (band, window, half_width, width)),
        (
            shape(2 * rows, rows),
            shape(2 * rows, rows),
            shape(2 * width, 2 * width),
            shape(2 * width, 2 * width),
        ),
        [meta, taps],
        [],
        10_000_000,
        1_500_000,
    )
    layers = lax.all_to_all(sent, "depth", 0, 0, tiled=False)
    early = jnp.concatenate([layers[:steps], start[None]], axis=0)
    early_above, early_below = row_halo(early)
    late = layers[steps:]
    late, early_above, early_below = lax.optimization_barrier((late, early_above, early_below))
    late_above, late_below = row_halo(late)

    flops = 2 * steps * rows * 2 * width * (2 * rows + 2 * width)
    moved = 6 * steps * rows * width
    sizes = (steps, band, width)
    kept_early, wave = call(
        functools.partial(first_forward_body, sizes),
        (shape(steps, band, 2 * width), shape(2, band, width)),
        [],
        [row_fwd, col_fwd, early_above, early, early_below],
        flops,
        moved,
    )
    wave_above, wave_below = row_halo(wave)
    kept_late, seed = call(
        functools.partial(second_forward_body, sizes),
        (shape(steps, band, 2 * width), shape(band, 2 * LANES)),
        [],
        [row_fwd, col_fwd, late_above, late, late_below, wave_above, wave, wave_below, target],
        flops,
        moved,
    )
    seed_above, seed_below = row_halo(seed)
    seeds = jnp.stack([seed_above, seed, seed_below])
    from_left = lax.ppermute(seeds[:, :, LANES:], "depth", [(i, i + 1) for i in inner])
    from_right = lax.ppermute(seeds[:, :, :LANES], "depth", [(i + 1, i) for i in inner])
    adjoint, terms_late = call(
        functools.partial(first_backward_body, sizes),
        (shape(2, band, width), shape(steps, 2, band, LANES)),
        [],
        [
            row_bwd,
            col_bwd,
            late_above,
            late,
            late_below,
            seeds,
            from_left,
            from_right,
            kept_late,
        ],
        flops,
        moved,
    )
    adjoint_above, adjoint_below = row_halo(adjoint)
    terms = call(
        functools.partial(second_backward_body, sizes),
        shape(2 * steps, 2, band, LANES),
        [],
        [
            row_bwd,
            col_bwd,
            early_above,
            early,
            early_below,
            adjoint_above,
            adjoint,
            adjoint_below,
            kept_early,
            terms_late,
        ],
        flops,
        moved,
    )
    gathered = lax.all_to_all(terms, "depth", 0, 0, tiled=False)
    gradient = call(
        functools.partial(collect_body, (probes, tiles, window, columns)),
        shape(2, 2, band, columns, dtype=F32),
        [meta],
        [gathered],
        1_000_000,
        2_000_000,
    )
    return gradient[:, None]


def solution(mesh):
    in_specs = (
        P(None, "depth", None, "lat", None),
        P(None, None, "lat", None),
        P(None, "lat", None),
        P(),
        P(),
    )
    out_specs = P(None, "depth", None, "lat", None)
    return jax.shard_map(local, mesh=mesh, in_specs=in_specs, out_specs=out_specs, check_vma=False)
```

time: 694 us -> 141 us (0.20)
  the two profiles are of different devices: /device:TPU:25 before, /device:TPU:1 now
where the time goes in v1:
time: 141 us
  blocking collectives  44.6 us (32%)
  starting transfers between devices  43.8 us (31%)
  waiting for transfers between devices  27.8 us (20%)
  Pallas kernels  18.1 us (13%)
  local copies, waits for them, and re-layouts  4.92 us (3%)
  between operations  1.47 us (1%)
    all_to_all x1, blocking collectives, local(): layers = lax.all_to_all(sent, 'depth', 0, 0, tiled=False)  26.7 us
    ppermute x5, starting transfers between devices, row_halo(): lax.ppermute(cells, 'lat', upward)  22.9 us
    ppermute x5, waiting for transfers between devices, row_halo(): lax.ppermute(cells, 'lat', downward)  22.5 us
    pallas_call x7, Pallas kernels, call(): pl.pallas_call(body, out_shape=outs, in_specs=[smem_spec()] * len(scalars...  18.1 us
    all_to_all x1, blocking collectives, local(): gathered = lax.all_to_all(terms, 'depth', 0, 0, tiled=False)  18 us
    ppermute x5, starting transfers between devices, row_halo(): lax.ppermute(cells, 'lat', downward)  13.9 us
    ppermute x1, starting transfers between devices, local(): lax.ppermute(seeds[:, :, :LANES], 'depth', [(i + 1, i) for i in inner])  5.08 us
    ppermute x5, waiting for transfers between devices, row_halo(): lax.ppermute(cells, 'lat', upward)  4.15 us
  transfers between devices with their start and end apart: 12, of which 6 were waited for; matrix products, arithmetic and copies ran while one was open for 0% of the time, Pallas kernels for 3%

profile of v1, /device:TPU:1, one launch (start us, length us, event | category | flops | bytes accessed | tf_op | source)
XLA Modules:
  0.0 140.8 jit_solution(10226095902679261754)
XLA Ops:
  0.0 0.0 copy-start.3
  0.0 0.7 copy-done.3
  0.7 0.2 slice_reduce_fusion
  0.9 0.6 fusion.3
  2.8 0.1 concatenate.6.meta
  2.8 0.0 copy-start
  2.8 1.2 copy-done
  4.1 0.0 copy-start.1
  4.1 1.0 copy-done.1
  5.1 0.0 copy-start.2
  5.1 0.9 copy-done.2
  6.1 2.1 %shard_map.56 = (bf16[16,2,32,256]{3,2,1,0:T(8,128)(2,1)S(1)}, bf16[2,32,256]{2,1,0:T(8,128)(2,1)S(1)}, f32[32,256]{1,0:T(8,128)S(1)}) custom-call(s32[7]{0:T(128)S(1)} %concatenate.6.meta, f32[2,2,32,2048]{3,2,1,0:T(8,128)S(1)} %bitcast.13, f32[2,2,32,1024]{3,2,1,0:T(8,128)S(1)} %copy-done.1, f32[2,32,1024]{2,1,0:T(8,128)S(1)} %copy-done.2), custom_call_target="tpu_custom_call" | custom-call | flops 10000000 | bytes 3000000 | tf_op jit(solution)/shard_map/pallas_call | solution.py:25
  8.2 26.7 %all_to_all.10 = bf16[16,2,32,256]{3,2,1,0:T(8,128)(2,1)S(1)} all-to-all(bf16[16,2,32,256]{3,2,1,0:T(8,128)(2,1)S(1)} %get-tuple-element.23), channel_id=1, replica_groups=mesh['depth'=16,'lat'=32] {'depth'}, dimensions={0} | all-to-all | bytes 1048576 | tf_op jit(solution)/shard_map/all_to_all | solution.py:289
  35.0 0.0 copy-start.4
  35.0 11.9 %collective-permute-start.1 = (bf16[9,2,32,256]{3,2,1,0:T(8,128)(2,1)S(1)}, bf16[9,2,32,256]{3,2,1,0:T(8,128)(2,1)S(1)}, u32[]{:S(2)}, u32[]{:S(2)}) collective-permute-start(bf16[9,2,32,256]{3,2,1,0:T(8,128)(2,1)S(1)} %pad_maximum_fusion.own), channel_id=1, source_target_pairs={{1,0},{2,1},{3,2},{4,3},{5,4},{6,5},{7,6},{8,7},{9,8},{10,9},{11,1... | collective-permute-start | bytes 884744 | tf_op jit(solution)/shard_map/ppermute | solution.py:258
  46.9 1.9 %collective-permute-start = (bf16[9,2,32,256]{3,2,1,0:T(8,128)(2,1)S(1)}, bf16[9,2,32,256]{3,2,1,0:T(8,128)(2,1)S(1)}, u32[]{:S(2)}, u32[]{:S(2)}) collective-permute-start(bf16[9,2,32,256]{3,2,1,0:T(8,128)(2,1)S(1)} %pad_maximum_fusion.own), channel_id=1, source_target_pairs={{0,1},{1,2},{2,3},{3,4},{4,5},{5,6},{6,7},{7,8},{8,9},{9,10},{10,1... | collective-permute-start | bytes 884744 | tf_op jit(solution)/shard_map/ppermute | solution.py:258
  48.8 4.1 %collective-permute-done.1.below = bf16[9,2,32,256]{3,2,1,0:T(8,128)(2,1)S(1)} collective-permute-done((bf16[9,2,32,256]{3,2,1,0:T(8,128)(2,1)S(1)}, bf16[9,2,32,256]{3,2,1,0:T(8,128)(2,1)S(1)}, u32[]{:S(2)}, u32[]{:S(2)}) %collective-permute-start.1) | collective-permute-done | bytes 294944 | tf_op jit(solution)/shard_map/ppermute | solution.py:258
  53.0 7.4 %collective-permute-done.above = bf16[9,2,32,256]{3,2,1,0:T(8,128)(2,1)S(1)} collective-permute-done((bf16[9,2,32,256]{3,2,1,0:T(8,128)(2,1)S(1)}, bf16[9,2,32,256]{3,2,1,0:T(8,128)(2,1)S(1)}, u32[]{:S(2)}, u32[]{:S(2)}) %collective-permute-start) | collective-permute-done | bytes 294944 | tf_op jit(solution)/shard_map/ppermute | solution.py:258
  60.4 1.9 %collective-permute-start.3 = (bf16[8,2,32,256]{3,2,1,0:T(8,128)(2,1)S(1)}, bf16[8,2,32,256]{3,2,1,0:T(8,128)(2,1)S(1)}, u32[]{:S(2)}, u32[]{:S(2)}) collective-permute-start(bf16[8,2,32,256]{3,2,1,0:T(8,128)(2,1)S(1)} %get-tuple-element.27.own), channel_id=1, source_target_pairs={{1,0},{2,1},{3,2},{4,3},{5,4},{6,5},{7,6},{8,7},{9,8},{10,9},{11,1... | collective-permute-start | bytes 786440 | tf_op jit(solution)/shard_map/ppermute | solution.py:258
  62.3 3.4 %collective-permute-start.2 = (bf16[8,2,32,256]{3,2,1,0:T(8,128)(2,1)S(1)}, bf16[8,2,32,256]{3,2,1,0:T(8,128)(2,1)S(1)}, u32[]{:S(2)}, u32[]{:S(2)}) collective-permute-start(bf16[8,2,32,256]{3,2,1,0:T(8,128)(2,1)S(1)} %get-tuple-element.27.own), channel_id=1, source_target_pairs={{0,1},{1,2},{2,3},{3,4},{4,5},{5,6},{6,7},{7,8},{8,9},{9,10},{10,1... | collective-permute-start | bytes 786440 | tf_op jit(solution)/shard_map/ppermute | solution.py:258
  65.7 0.0 copy-done.4
  65.7 0.1 reshape.8.taps
  65.8 1.0 shard_map.55
  66.8 3.2 %shard_map.57 = (bf16[8,32,512]{2,1,0:T(8,128)(2,1)S(1)}, bf16[2,32,256]{2,1,0:T(8,128)(2,1)S(1)}) custom-call(bf16[192,96]{1,0:T(8,128)(2,1)S(1)} %get-tuple-element.28.row_mat, bf16[512,512]{1,0:T(8,128)(2,1)S(1)} %get-tuple-element.29.col_mat, bf16[9,2,32,256]{3,2,1,0:T(8,128)(2,1)S(1)} %collective-permute-done.above, ...), custom_call_target="tpu_custom_call" | custom-call | flops 553648128 | bytes 1179648 | tf_op jit(solution)/shard_map/pallas_call | solution.py:25
  70.0 5.2 %collective-permute-start.5 = (bf16[2,32,256]{2,1,0:T(8,128)(2,1)S(1)}, bf16[2,32,256]{2,1,0:T(8,128)(2,1)S(1)}, u32[]{:S(2)}, u32[]{:S(2)}) collective-permute-start(bf16[2,32,256]{2,1,0:T(8,128)(2,1)S(1)} %get-tuple-element.30.w_own), channel_id=1, source_target_pairs={{1,0},{2,1},{3,2},{4,3},{5,4},{6,5},{7,6},{8,7},{9,8},{10,9},{11,1... | collective-permute-start | bytes 98312 | tf_op jit(solution)/shard_map/ppermute | solution.py:258
  75.3 1.9 %collective-permute-start.4 = (bf16[2,32,256]{2,1,0:T(8,128)(2,1)S(1)}, bf16[2,32,256]{2,1,0:T(8,128)(2,1)S(1)}, u32[]{:S(2)}, u32[]{:S(2)}) collective-permute-start(bf16[2,32,256]{2,1,0:T(8,128)(2,1)S(1)} %get-tuple-element.30.w_own), channel_id=1, source_target_pairs={{0,1},{1,2},{2,3},{3,4},{4,5},{5,6},{6,7},{7,8},{8,9},{9,10},{10,1... | collective-permute-start | bytes 98312 | tf_op jit(solution)/shard_map/ppermute | solution.py:258
  77.2 0.0 collective-permute-done.5.w_below
  77.2 6.0 %collective-permute-done.4.w_above = bf16[2,32,256]{2,1,0:T(8,128)(2,1)S(1)} collective-permute-done((bf16[2,32,256]{2,1,0:T(8,128)(2,1)S(1)}, bf16[2,32,256]{2,1,0:T(8,128)(2,1)S(1)}, u32[]{:S(2)}, u32[]{:S(2)}) %collective-permute-start.4) | collective-permute-done | bytes 32800 | tf_op jit(solution)/shard_map/ppermute | solution.py:258
  83.3 0.0 collective-permute-done.3.below
  83.3 0.0 collective-permute-done.2.above
  83.3 3.3 %shard_map.58 = (bf16[8,32,512]{2,1,0:T(8,128)(2,1)S(1)}, bf16[32,256]{1,0:T(8,128)(2,1)S(1)}) custom-call(bf16[192,96]{1,0:T(8,128)(2,1)S(1)} %get-tuple-element.28.row_mat, bf16[512,512]{1,0:T(8,128)(2,1)S(1)} %get-tuple-element.29.col_mat, bf16[8,2,32,256]{3,2,1,0:T(8,128)(2,1)S(1)} %collective-permute-done.2.above, ...), custom_call_target="tpu_custom_call" | custom-call | flops 553648128 | bytes 1179648 | tf_op jit(solution)/shard_map/pallas_call | solution.py:25
  86.5 1.9 %collective-permute-start.7 = (bf16[32,256]{1,0:T(8,128)(2,1)S(1)}, bf16[32,256]{1,0:T(8,128)(2,1)S(1)}, u32[]{:S(2)}, u32[]{:S(2)}) collective-permute-start(bf16[32,256]{1,0:T(8,128)(2,1)S(1)} %get-tuple-element.32), channel_id=1, source_target_pairs={{1,0},{2,1},{3,2},{4,3},{5,4},{6,5},{7,6},{8,7},{9,8},{10,9},{11,1... | collective-permute-start | bytes 49160 | tf_op jit(solution)/shard_map/ppermute | solution.py:258
  88.4 3.4 %collective-permute-start.6 = (bf16[32,256]{1,0:T(8,128)(2,1)S(1)}, bf16[32,256]{1,0:T(8,128)(2,1)S(1)}, u32[]{:S(2)}, u32[]{:S(2)}) collective-permute-start(bf16[32,256]{1,0:T(8,128)(2,1)S(1)} %get-tuple-element.32), channel_id=1, source_target_pairs={{0,1},{1,2},{2,3},{3,4},{4,5},{5,6},{6,7},{7,8},{8,9},{9,10},{10,1... | collective-permute-start | bytes 49160 | tf_op jit(solution)/shard_map/ppermute | solution.py:258
  91.8 0.0 collective-permute-done.7
  91.8 4.4 %collective-permute-done.6 = bf16[32,256]{1,0:T(8,128)(2,1)S(1)} collective-permute-done((bf16[32,256]{1,0:T(8,128)(2,1)S(1)}, bf16[32,256]{1,0:T(8,128)(2,1)S(1)}, u32[]{:S(2)}, u32[]{:S(2)}) %collective-permute-start.6) | collective-permute-done | bytes 16416 | tf_op jit(solution)/shard_map/ppermute | solution.py:258
  96.3 5.1 %collective-permute-start.9 = (bf16[3,32,128]{2,1,0:T(8,128)(2,1)S(1)}, bf16[3,32,128]{2,1,0:T(8,128)(2,1)S(1)}, u32[]{:S(2)}, u32[]{:S(2)}) collective-permute-start(bf16[3,32,128]{2,1,0:T(8,128)(2,1)S(1)} %get-tuple-element.43), channel_id=1, source_target_pairs={{32,0},{64,32},{96,64},{128,96},{160,128},{192,160},{224,192},{288... | collective-permute-start | bytes 73736 | tf_op jit(solution)/shard_map/ppermute | solution.py:319
  101.4 1.9 %collective-permute-start.8 = (bf16[3,32,128]{2,1,0:T(8,128)(2,1)S(1)}, bf16[3,32,128]{2,1,0:T(8,128)(2,1)S(1)}, u32[]{:S(2)}, u32[]{:S(2)}) collective-permute-start(bf16[3,32,128]{2,1,0:T(8,128)(2,1)S(1)} %get-tuple-element.44), channel_id=1, source_target_pairs={{0,32},{32,64},{64,96},{96,128},{128,160},{160,192},{192,224},{256... | collective-permute-start | bytes 73736 | tf_op jit(solution)/shard_map/ppermute | solution.py:318
  103.3 0.0 collective-permute-done.9.right
  103.3 1.2 collective-permute-done.8.left
  104.4 3.3 %shard_map.59 = (bf16[2,32,256]{2,1,0:T(8,128)(2,1)S(1)}, bf16[8,2,32,128]{3,2,1,0:T(8,128)(2,1)S(1)}) custom-call(bf16[192,96]{1,0:T(8,128)(2,1)S(1)} %get-tuple-element.21.row_mat, bf16[512,512]{1,0:T(8,128)(2,1)S(1)} %get-tuple-element.22.col_mat, bf16[8,2,32,256]{3,2,1,0:T(8,128)(2,1)S(1)} %collective-permute-done.2.above, ...), custom_call_target="tpu_custom_call" | custom-call | flops 553648128 | bytes 1179648 | tf_op jit(solution)/shard_map/pallas_call | solution.py:25
  107.8 1.9 %collective-permute-start.11 = (bf16[2,32,256]{2,1,0:T(8,128)(2,1)S(1)}, bf16[2,32,256]{2,1,0:T(8,128)(2,1)S(1)}, u32[]{:S(2)}, u32[]{:S(2)}) collective-permute-start(bf16[2,32,256]{2,1,0:T(8,128)(2,1)S(1)} %get-tuple-element.34.w_own), channel_id=1, source_target_pairs={{1,0},{2,1},{3,2},{4,3},{5,4},{6,5},{7,6},{8,7},{9,8},{10,9},{11,1... | collective-permute-start | bytes 98312 | tf_op jit(solution)/shard_map/ppermute | solution.py:258
  109.7 3.4 %collective-permute-start.10 = (bf16[2,32,256]{2,1,0:T(8,128)(2,1)S(1)}, bf16[2,32,256]{2,1,0:T(8,128)(2,1)S(1)}, u32[]{:S(2)}, u32[]{:S(2)}) collective-permute-start(bf16[2,32,256]{2,1,0:T(8,128)(2,1)S(1)} %get-tuple-element.34.w_own), channel_id=1, source_target_pairs={{0,1},{1,2},{2,3},{3,4},{4,5},{5,6},{6,7},{7,8},{8,9},{9,10},{10,1... | collective-permute-start | bytes 98312 | tf_op jit(solution)/shard_map/ppermute | solution.py:258
  113.1 0.0 collective-permute-done.11.w_below
  113.1 4.6 %collective-permute-done.10.w_above = bf16[2,32,256]{2,1,0:T(8,128)(2,1)S(1)} collective-permute-done((bf16[2,32,256]{2,1,0:T(8,128)(2,1)S(1)}, bf16[2,32,256]{2,1,0:T(8,128)(2,1)S(1)}, u32[]{:S(2)}, u32[]{:S(2)}) %collective-permute-start.10) | collective-permute-done | bytes 32800 | tf_op jit(solution)/shard_map/ppermute | solution.py:258
  117.7 3.3 %shard_map.60 = bf16[16,2,32,128]{3,2,1,0:T(8,128)(2,1)S(1)} custom-call(bf16[192,96]{1,0:T(8,128)(2,1)S(1)} %get-tuple-element.21.row_mat, bf16[512,512]{1,0:T(8,128)(2,1)S(1)} %get-tuple-element.22.col_mat, bf16[9,2,32,256]{3,2,1,0:T(8,128)(2,1)S(1)} %collective-permute-done.above, bf16[9,2,32,256]{3,2,1,0:T(8,128)(2,1)S(1)} %pad_maximum_fusion.own, ...), custom_call_target="tpu_custom_call" | custom-call | flops 553648128 | bytes 1179648 | tf_op jit(solution)/shard_map/pallas_call | solution.py:25
  121.0 18.0 %all_to_all.11.terms = bf16[16,2,32,128]{3,2,1,0:T(8,128)(2,1)S(1)} all-to-all(bf16[16,2,32,128]{3,2,1,0:T(8,128)(2,1)S(1)} %shard_map.60), channel_id=1, replica_groups=mesh['depth'=16,'lat'=32] {'depth'}, dimensions={0} | all-to-all | bytes 524288 | tf_op jit(solution)/shard_map/all_to_all | solution.py:358
  139.0 1.9 %shard_map.61 = f32[2,2,32,2048]{3,2,1,0:T(8,128)} custom-call(s32[7]{0:T(128)S(1)} %concatenate.6.meta, bf16[16,2,32,128]{3,2,1,0:T(8,128)(2,1)S(1)} %all_to_all.11.terms), custom_call_target="tpu_custom_call" | custom-call | flops 1000000 | bytes 2000000 | tf_op jit(solution)/shard_map/pallas_call | solution.py:25
  (5 shorter events, 0.1 us)
Async XLA Ops:
  0.0 0.7 copy-start.3
  2.8 1.2 copy-start
  4.1 1.0 copy-start.1
  5.1 0.9 copy-start.2
  35.0 30.7 %copy-start.4 = (bf16[2,9]{1,0:T(2,128)(2,1)S(1)}, bf16[2,9]{1,0:T(2,128)(2,1)}, u32[]{:S(2)}) copy-start(bf16[2,9]{1,0:T(2,128)(2,1)} %param.9) | copy-start | bytes 112
  35.0 18.0 %collective-permute-start.1 = (bf16[9,2,32,256]{3,2,1,0:T(8,128)(2,1)S(1)}, bf16[9,2,32,256]{3,2,1,0:T(8,128)(2,1)S(1)}, u32[]{:S(2)}, u32[]{:S(2)}) collective-permute-start(bf16[9,2,32,256]{3,2,1,0:T(8,128)(2,1)S(1)} %pad_maximum_fusion.own), channel_id=1, source_target_pairs={{1,0},{2,1},{3,2},{4,3},{5,4},{6,5},{7,6},{8,7},{9,8},{10,9},{11,1... | collective-permute-start | bytes 884744 | tf_op jit(solution)/shard_map/ppermute | solution.py:258
  46.9 13.5 %collective-permute-start = (bf16[9,2,32,256]{3,2,1,0:T(8,128)(2,1)S(1)}, bf16[9,2,32,256]{3,2,1,0:T(8,128)(2,1)S(1)}, u32[]{:S(2)}, u32[]{:S(2)}) collective-permute-start(bf16[9,2,32,256]{3,2,1,0:T(8,128)(2,1)S(1)} %pad_maximum_fusion.own), channel_id=1, source_target_pairs={{0,1},{1,2},{2,3},{3,4},{4,5},{5,6},{6,7},{7,8},{8,9},{9,10},{10,1... | collective-permute-start | bytes 884744 | tf_op jit(solution)/shard_map/ppermute | solution.py:258
  60.4 22.9 %collective-permute-start.3 = (bf16[8,2,32,256]{3,2,1,0:T(8,128)(2,1)S(1)}, bf16[8,2,32,256]{3,2,1,0:T(8,128)(2,1)S(1)}, u32[]{:S(2)}, u32[]{:S(2)}) collective-permute-start(bf16[8,2,32,256]{3,2,1,0:T(8,128)(2,1)S(1)} %get-tuple-element.27.own), channel_id=1, source_target_pairs={{1,0},{2,1},{3,2},{4,3},{5,4},{6,5},{7,6},{8,7},{9,8},{10,9},{11,1... | collective-permute-start | bytes 786440 | tf_op jit(solution)/shard_map/ppermute | solution.py:258
  62.3 20.9 %collective-permute-start.2 = (bf16[8,2,32,256]{3,2,1,0:T(8,128)(2,1)S(1)}, bf16[8,2,32,256]{3,2,1,0:T(8,128)(2,1)S(1)}, u32[]{:S(2)}, u32[]{:S(2)}) collective-permute-start(bf16[8,2,32,256]{3,2,1,0:T(8,128)(2,1)S(1)} %get-tuple-element.27.own), channel_id=1, source_target_pairs={{0,1},{1,2},{2,3},{3,4},{4,5},{5,6},{6,7},{7,8},{8,9},{9,10},{10,1... | collective-permute-start | bytes 786440 | tf_op jit(solution)/shard_map/ppermute | solution.py:258
  70.0 7.2 %collective-permute-start.5 = (bf16[2,32,256]{2,1,0:T(8,128)(2,1)S(1)}, bf16[2,32,256]{2,1,0:T(8,128)(2,1)S(1)}, u32[]{:S(2)}, u32[]{:S(2)}) collective-permute-start(bf16[2,32,256]{2,1,0:T(8,128)(2,1)S(1)} %get-tuple-element.30.w_own), channel_id=1, source_target_pairs={{1,0},{2,1},{3,2},{4,3},{5,4},{6,5},{7,6},{8,7},{9,8},{10,9},{11,1... | collective-permute-start | bytes 98312 | tf_op jit(solution)/shard_map/ppermute | solution.py:258
  75.3 8.0 %collective-permute-start.4 = (bf16[2,32,256]{2,1,0:T(8,128)(2,1)S(1)}, bf16[2,32,256]{2,1,0:T(8,128)(2,1)S(1)}, u32[]{:S(2)}, u32[]{:S(2)}) collective-permute-start(bf16[2,32,256]{2,1,0:T(8,128)(2,1)S(1)} %get-tuple-element.30.w_own), channel_id=1, source_target_pairs={{0,1},{1,2},{2,3},{3,4},{4,5},{5,6},{6,7},{7,8},{8,9},{9,10},{10,1... | collective-permute-start | bytes 98312 | tf_op jit(solution)/shard_map/ppermute | solution.py:258
  86.5 5.3 %collective-permute-start.7 = (bf16[32,256]{1,0:T(8,128)(2,1)S(1)}, bf16[32,256]{1,0:T(8,128)(2,1)S(1)}, u32[]{:S(2)}, u32[]{:S(2)}) collective-permute-start(bf16[32,256]{1,0:T(8,128)(2,1)S(1)} %get-tuple-element.32), channel_id=1, source_target_pairs={{1,0},{2,1},{3,2},{4,3},{5,4},{6,5},{7,6},{8,7},{9,8},{10,9},{11,1... | collective-permute-start | bytes 49160 | tf_op jit(solution)/shard_map/ppermute | solution.py:258
  88.4 7.8 %collective-permute-start.6 = (bf16[32,256]{1,0:T(8,128)(2,1)S(1)}, bf16[32,256]{1,0:T(8,128)(2,1)S(1)}, u32[]{:S(2)}, u32[]{:S(2)}) collective-permute-start(bf16[32,256]{1,0:T(8,128)(2,1)S(1)} %get-tuple-element.32), channel_id=1, source_target_pairs={{0,1},{1,2},{2,3},{3,4},{4,5},{5,6},{6,7},{7,8},{8,9},{9,10},{10,1... | collective-permute-start | bytes 49160 | tf_op jit(solution)/shard_map/ppermute | solution.py:258
  96.3 7.0 %collective-permute-start.9 = (bf16[3,32,128]{2,1,0:T(8,128)(2,1)S(1)}, bf16[3,32,128]{2,1,0:T(8,128)(2,1)S(1)}, u32[]{:S(2)}, u32[]{:S(2)}) collective-permute-start(bf16[3,32,128]{2,1,0:T(8,128)(2,1)S(1)} %get-tuple-element.43), channel_id=1, source_target_pairs={{32,0},{64,32},{96,64},{128,96},{160,128},{192,160},{224,192},{288... | collective-permute-start | bytes 73736 | tf_op jit(solution)/shard_map/ppermute | solution.py:319
  101.4 3.1 %collective-permute-start.8 = (bf16[3,32,128]{2,1,0:T(8,128)(2,1)S(1)}, bf16[3,32,128]{2,1,0:T(8,128)(2,1)S(1)}, u32[]{:S(2)}, u32[]{:S(2)}) collective-permute-start(bf16[3,32,128]{2,1,0:T(8,128)(2,1)S(1)} %get-tuple-element.44), channel_id=1, source_target_pairs={{0,32},{32,64},{64,96},{96,128},{128,160},{160,192},{192,224},{256... | collective-permute-start | bytes 73736 | tf_op jit(solution)/shard_map/ppermute | solution.py:318
  107.8 5.3 %collective-permute-start.11 = (bf16[2,32,256]{2,1,0:T(8,128)(2,1)S(1)}, bf16[2,32,256]{2,1,0:T(8,128)(2,1)S(1)}, u32[]{:S(2)}, u32[]{:S(2)}) collective-permute-start(bf16[2,32,256]{2,1,0:T(8,128)(2,1)S(1)} %get-tuple-element.34.w_own), channel_id=1, source_target_pairs={{1,0},{2,1},{3,2},{4,3},{5,4},{6,5},{7,6},{8,7},{9,8},{10,9},{11,1... | collective-permute-start | bytes 98312 | tf_op jit(solution)/shard_map/ppermute | solution.py:258
  109.7 8.0 %collective-permute-start.10 = (bf16[2,32,256]{2,1,0:T(8,128)(2,1)S(1)}, bf16[2,32,256]{2,1,0:T(8,128)(2,1)S(1)}, u32[]{:S(2)}, u32[]{:S(2)}) collective-permute-start(bf16[2,32,256]{2,1,0:T(8,128)(2,1)S(1)} %get-tuple-element.34.w_own), channel_id=1, source_target_pairs={{0,1},{1,2},{2,3},{3,4},{4,5},{5,6},{6,7},{7,8},{8,9},{9,10},{10,1... | collective-permute-start | bytes 98312 | tf_op jit(solution)/shard_map/ppermute | solution.py:258

commit v2 on v0

v2 whole, which is shorter than its diff:
```python
import functools

import jax
import jax.numpy as jnp
from jax import lax
from jax.experimental import pallas as pl
from jax.experimental.pallas import tpu as pltpu
from jax.sharding import Mesh
from jax.sharding import PartitionSpec as P

F32 = jnp.float32
BF16 = jnp.bfloat16
LANES = 128
PIECE = 64
CORES = 2
GROUP = 4
TAIL = 8
VMEM_BYTES = 48 * 1024 * 1024


def vmem_spec():
    return pl.BlockSpec(memory_space=pltpu.VMEM)


def smem_spec():
    return pl.BlockSpec(memory_space=pltpu.SMEM)


def call(body, outs, scalars, arrays, cost, scratch=(), outside=0):
    in_specs = [smem_spec()] * len(scalars)
    in_specs += [pl.BlockSpec(memory_space=pl.ANY)] * outside
    in_specs += [vmem_spec()] * (len(arrays) - outside)
    return pl.pallas_call(
        body,
        out_shape=outs,
        in_specs=in_specs,
        out_specs=jax.tree.map(lambda _: vmem_spec(), outs),
        scratch_shapes=list(scratch),
        compiler_params=pltpu.CompilerParams(vmem_limit_bytes=VMEM_BYTES),
        cost_estimate=pl.CostEstimate(flops=cost[0], bytes_accessed=cost[1], transcendentals=0),
    )(*scalars, *arrays)


def tile_at(x, y, y_count, probes):
    rows = y_count // probes
    probe, row = y // rows, y % rows
    return probe, row * GROUP + (x if row % 2 == 0 else GROUP - 1 - x)


def low_lanes(rows):
    return lax.broadcasted_iota(jnp.int32, (rows, LANES), 1) < PIECE


def swap_halves(cells):
    return pltpu.roll(cells, PIECE, 1)


def half_of(offsets, probe, band, lat, lat_count):
    first = offsets[probe, 0] // band
    return (first + lax.rem(lat - first + lat_count, lat_count)) // lat_count


def packed(real, imag, tiles):
    span = real.shape[1]
    real_on = pltpu.roll(real, span - PIECE, 1)
    imag_on = pltpu.roll(imag, span - PIECE, 1)
    low = low_lanes(real.shape[0])
    out = []
    for tile in range(tiles):
        base = tile // 2 * LANES
        here, there = slice(base, base + LANES), slice(base + LANES, base + 2 * LANES)
        if tile % 2 == 0:
            middle = jnp.where(low, real[:, there], imag_on[:, here])
            out.append((real[:, here], middle, imag[:, here]))
        else:
            middle = jnp.where(low, real_on[:, there], imag[:, there])
            out.append((real_on[:, here], middle, imag_on[:, here]))
    return out


def prepare_body(
    dims, offsets, potential, incident, measured, sent, pot_buf, inc_buf, mea_buf, sems
):
    probes, tiles, halo, y_count, lat_count = dims
    band, columns = pot_buf.shape[2], pot_buf.shape[3]
    window = inc_buf.shape[3]
    span = window + 2 * halo
    y = lax.axis_index("y")
    lat = lax.axis_index("z") * GROUP + lax.axis_index("x")
    strip = TAIL // 2
    first = pl.multiple_of(y // 2 * TAIL, TAIL)
    copies = []
    for probe in range(probes):
        half = half_of(offsets, probe, band, lat, lat_count)
        copies.append(
            pltpu.make_async_copy(potential.at[:, half], pot_buf.at[probe], sems.at[probe])
        )
    copies.append(
        pltpu.make_async_copy(incident.at[:, :, pl.ds(first, TAIL)], inc_buf, sems.at[probes])
    )
    copies.append(
        pltpu.make_async_copy(measured.at[:, pl.ds(first, TAIL)], mea_buf, sems.at[probes + 1])
    )
    for copy in copies:
        copy.start()
    slots = {}
    for spot in range(y_count * GROUP):
        slots[tile_at(spot // y_count, spot % y_count, y_count, probes)] = spot
    lane = lax.broadcasted_iota(jnp.int32, (band, span), 1)
    inside = (lane >= halo) & (lane < window + halo)
    for probe in range(probes):
        copies[probe].wait()
        turn = lax.rem(columns + halo - offsets[probe, 1], columns)
        phase = pltpu.roll(pot_buf[probe, 0], turn, 1)[:, :span]
        absorb = pltpu.roll(pot_buf[probe, 1], turn, 1)[:, :span]
        damping = jnp.where(inside, jnp.exp(-absorb), 0.0)
        for tile, parts in enumerate(
            packed(damping * jnp.cos(phase), damping * jnp.sin(phase), tiles)
        ):
            for at, part in enumerate(parts):
                cols = slice(at * LANES, (at + 1) * LANES)
                sent[slots[probe, tile], :band, cols] = part.astype(BF16)
    copies[probes].wait()
    copies[probes + 1].wait()
    odd = lax.rem(y, 2) == 1
    rest = jnp.zeros((TAIL, 2 * halo), F32)
    upper = lax.broadcasted_iota(jnp.int32, (TAIL, LANES), 0) < strip
    low = low_lanes(TAIL)
    for probe in range(probes):
        wide = []
        for part in range(2):
            rows = inc_buf[part, probe]
            rows = jnp.where(odd, pltpu.roll(rows, strip, 0), rows)
            wide.append(pltpu.roll(jnp.concatenate([rows, rest], axis=1), halo, 1))
        rows = mea_buf[probe]
        rows = jnp.where(odd, rows, pltpu.roll(rows, strip, 0))
        coarse = rows.astype(BF16).astype(F32)
        fine = rows - coarse
        coarse_on = pltpu.roll(coarse, window - PIECE, 1)
        fine_back = pltpu.roll(fine, PIECE, 1)
        for tile, parts in enumerate(packed(wide[0], wide[1], tiles)):
            here = slice(tile // 2 * LANES, tile // 2 * LANES + LANES)
            if tile % 2 == 0:
                both = jnp.where(low, coarse[:, here], fine_back[:, here])
            else:
                both = jnp.where(low, coarse_on[:, here], fine[:, here])
            for at, part in enumerate(parts):
                cols = slice(at * LANES, (at + 1) * LANES)
                under = both if at == 0 else jnp.zeros_like(both)
                sent[slots[probe, tile], band:, cols] = jnp.where(upper, part, under).astype(BF16)


def banded(taps, diff, half_width, conj):
    count = 2 * half_width + 1
    real = jnp.zeros(diff.shape, F32)
    imag = jnp.zeros(diff.shape, F32)
    for tap in range(count):
        hit = diff == tap - half_width
        source = count - 1 - tap if conj else tap
        real = jnp.where(hit, taps[source], real)
        value = taps[count + source]
        imag = jnp.where(hit, -value if conj else value, imag)
    return real, imag


def matrices_body(dims, offsets, taps, row_fwd, row_bwd, col_fwd, col_bwd):
    band, half_width, y_count, probes, lat_count = dims
    rows, lanes = row_fwd.shape[0], col_fwd.shape[0]
    reach = rows // band // 2 - GROUP // 2
    own = lax.axis_index("y") // (y_count // probes)
    base = lax.axis_index("z") * GROUP - reach - offsets[own, 0] // band + 2 * lat_count
    base = lax.rem(base, lat_count)

    def window_row(axis):
        index = lax.broadcasted_iota(jnp.int32, (rows, rows), axis)
        return jnp.where(
            index // band + base >= lat_count, index + (base - lat_count) * band, index + base * band
        )

    def column(axis):
        index = lax.broadcasted_iota(jnp.int32, (lanes, lanes), axis)
        edge = LANES + PIECE
        other = index >= edge
        return jnp.where(index >= 2 * LANES, index - 2 * LANES, jnp.where(other, index - PIECE, index)), other

    row_diff = window_row(1) - window_row(0)
    in_col, in_imag = column(0)
    out_col, out_imag = column(1)
    for conj, row_out, col_out in ((False, row_fwd, col_fwd), (True, row_bwd, col_bwd)):
        real, imag = banded(taps, row_diff, half_width, conj)
        row_out[:, :rows] = real.astype(BF16)
        row_out[:, rows:] = imag.astype(BF16)
        real, imag = banded(taps, in_col - out_col, half_width, conj)
        signed = jnp.where(in_imag, -imag, imag)
        col_out[...] = jnp.where(in_imag == out_imag, real, signed).astype(BF16)


def three(cells):
    return cells[:, :LANES], cells[:, LANES : 2 * LANES], cells[:, 2 * LANES :]


def fill_layer(layer, source, y, band):
    at = 0
    for part in source:
        for index in range(part.shape[0]):
            layer[at : at + band] = part[index, y, :band]
            at += band


def turning(middle, low):
    turned = swap_halves(middle)
    return jnp.where(low, middle, turned), jnp.where(low, -turned, middle)


def with_quarter_turn(parts, low):
    first, middle, last = parts
    turned = swap_halves(middle)
    direct = jnp.concatenate([first, middle, last], axis=1)
    crossed = jnp.concatenate([-last, jnp.where(low, -turned, turned), first], axis=1)
    return jnp.concatenate([direct, crossed], axis=0).astype(BF16)


def forward_body(
    dims, row_mat, col_mat, above, own, below, o_above, o_own, o_below, kept, seed, psi, layer, goal
):
    band, strip = dims
    near, far = (above, own, below), (o_above, o_own, o_below)
    core = lax.axis_index("core")
    rows = psi.shape[0]
    own_rows = own.shape[0] * band
    head = (rows - own_rows) // 2
    y_count = own.shape[1]
    low = low_lanes(rows)
    upper = lax.broadcasted_iota(jnp.int32, (TAIL, 3 * LANES), 0) < strip
    at = 0
    for part in near:
        for index in range(part.shape[0]):
            for pair in range(y_count // 2):
                one = part[index, 2 * pair, band:].astype(F32)
                two = part[index, 2 * pair + 1, band:].astype(F32)
                psi[at : at + TAIL] = jnp.where(upper, one, pltpu.roll(two, strip, 0))
                if part is own:
                    both = jnp.where(upper, pltpu.roll(one, strip, 0), two)[:, :LANES]
                    goal[at - head : at - head + TAIL] = both + swap_halves(both)
                at += TAIL

    def two_slices(y, _):
        for parity in range(CORES):
            mine = core == parity
            pl.when(mine)(lambda: fill_layer(layer, near, y, band))
            pl.when(jnp.logical_not(mine))(lambda: fill_layer(layer, far, y, band))
            t_first, t_middle, t_last = three(layer[...].astype(F32))
            t_real, t_turn = turning(t_middle, low)
            first, middle, last = three(psi[...])
            u_first = t_first * first - t_last * last
            u_last = t_first * last + t_last * first
            u_middle = t_real * middle + t_turn * swap_halves(middle)
            kept[CORES * y + parity, :, :LANES] = u_first[head : head + own_rows].astype(BF16)
            kept[CORES * y + parity, :, LANES:] = u_last[head : head + own_rows].astype(BF16)
            field = with_quarter_turn((u_first, u_middle, u_last), low)
            spread = jnp.dot(row_mat[...], field, preferred_element_type=F32).astype(BF16)
            psi[...] = jnp.dot(spread, col_mat[...], preferred_element_type=F32)
        return 0

    lax.fori_loop(0, y_count, two_slices, 0)
    real = psi[head : head + own_rows, :LANES]
    imag = psi[head : head + own_rows, 2 * LANES :]
    low = low_lanes(own_rows)
    twice = 2.0 * (real * real + imag * imag - goal[...])
    seed[...] = jnp.where(low, swap_halves(twice * real), twice * imag).astype(BF16)


def backward_body(
    dims,
    row_mat,
    col_mat,
    above,
    own,
    below,
    o_above,
    o_own,
    o_below,
    kept,
    seeds,
    left,
    right,
    terms,
    field,
    layer,
):
    (band,) = dims
    near, far = (above, own, below), (o_above, o_own, o_below)
    core = lax.axis_index("core")
    rows = field.shape[0]
    own_rows = own.shape[0] * band
    head = (rows - own_rows) // 2
    y_count = own.shape[1]
    low = low_lanes(rows)
    low_own = low_lanes(own_rows)
    middle = seeds[...].astype(F32)
    beside = left[...].astype(F32)
    field[:, :LANES] = jnp.where(low, beside, swap_halves(middle)).astype(BF16)
    field[:, LANES : 2 * LANES] = right[...]
    field[:, 2 * LANES :] = jnp.where(low, swap_halves(beside), middle).astype(BF16)

    def two_slices(step, _):
        y = y_count - 1 - step
        for parity in reversed(range(CORES)):
            mine = core == parity
            pl.when(mine)(lambda: fill_layer(layer, near, y, band))
            pl.when(jnp.logical_not(mine))(lambda: fill_layer(layer, far, y, band))
            spread = jnp.dot(field[...], col_mat[...], preferred_element_type=F32)
            both = with_quarter_turn(three(spread), low)
            first, centre, last = three(
                jnp.dot(row_mat[...], both, preferred_element_type=F32)
            )

            @pl.when(mine)
            def _():
                u_re = kept[CORES * y + parity, :, :LANES].astype(F32)
                u_im = kept[CORES * y + parity, :, LANES:].astype(F32)
                v_re, v_im = first[head : head + own_rows], last[head : head + own_rows]
                phase = swap_halves(u_re * v_im - u_im * v_re)
                term = jnp.where(low_own, phase, -(u_re * v_re + u_im * v_im)).astype(BF16)
                for index in range(own.shape[0]):
                    terms[index, y] = term[index * band : (index + 1) * band]

            t_first, t_middle, t_last = three(layer[...].astype(F32))
            t_real, t_turn = turning(t_middle, low)
            field[:, :LANES] = (t_first * first + t_last * last).astype(BF16)
            turned = t_real * centre - t_turn * swap_halves(centre)
            field[:, LANES : 2 * LANES] = turned.astype(BF16)
            field[:, 2 * LANES :] = (t_first * last - t_last * first).astype(BF16)
        return 0

    lax.fori_loop(0, y_count, two_slices, 0)


def collect_body(dims, offsets, terms, gradient):
    probes, tiles, y_count, lat_count, window, columns = dims
    band = terms.shape[1]
    lat = lax.axis_index("z") * GROUP + lax.axis_index("x")
    slots = {}
    for spot in range(y_count * GROUP):
        slots[tile_at(spot // y_count, spot % y_count, y_count, probes)] = spot
    low = low_lanes(band)
    rest = jnp.zeros((band, columns - window), F32)
    moved = []
    for probe in range(probes):
        parts = ([], [])
        for pair in range(tiles // 2):
            one = terms[slots[probe, 2 * pair]].astype(F32)
            two = terms[slots[probe, 2 * pair + 1]].astype(F32)
            parts[0].append(jnp.where(low, one, swap_halves(two)))
            parts[1].append(jnp.where(low, swap_halves(one), two))
        half = half_of(offsets, probe, band, lat, lat_count)
        for part in range(2):
            row = pltpu.roll(jnp.concatenate(parts[part] + [rest], axis=1), offsets[probe, 1], 1)
            moved.append((part, half, row))
    for part in range(2):
        for at in range(2):
            total = jnp.zeros((band, columns), F32)
            for which, half, row in moved:
                if which == part:
                    total = total + jnp.where(half == at, row, 0.0)
            gradient[part, at] = total


def local(potential, incident, measured, offsets, kernel):
    y_count = lax.axis_size("y")
    z_count = lax.axis_size("z")
    lat_count = z_count * GROUP
    band = potential.shape[3]
    columns = potential.shape[4]
    window = incident.shape[3]
    probes = incident.shape[1]
    half_width = (kernel.shape[1] - 1) // 2
    slices = y_count * CORES
    halo = slices * half_width
    tiles = y_count * GROUP // probes
    spots = y_count * GROUP
    reach = halo // band
    rows = (GROUP + 2 * reach) * band
    own_rows = GROUP * band
    lanes = 3 * LANES
    taps = kernel.astype(F32).reshape(-1)

    def shape(*dims, dtype=BF16):
        return jax.ShapeDtypeStruct(dims, dtype)

    sent = call(
        functools.partial(prepare_body, (probes, tiles, halo, y_count, lat_count)),
        shape(spots, band + TAIL, lanes),
        [offsets],
        [potential[:, 0], incident, measured],
        (20_000_000, 3_000_000),
        [
            pltpu.VMEM((probes, 2, band, columns), F32),
            pltpu.VMEM((2, probes, TAIL, window), F32),
            pltpu.VMEM((probes, TAIL, window), F32),
            pltpu.SemaphoreType.DMA((probes + 2,)),
        ],
        outside=3,
    )
    row_fwd, row_bwd, col_fwd, col_bwd = call(
        functools.partial(matrices_body, (band, half_width, y_count, probes, lat_count)),
        (
            shape(rows, 2 * rows),
            shape(rows, 2 * rows),
            shape(lanes, lanes),
            shape(lanes, lanes),
        ),
        [offsets, taps],
        [],
        (20_000_000, 1_500_000),
    )

    down_z = [(i, (i + 1) % z_count) for i in range(z_count)]
    up_z = [((i + 1) % z_count, i) for i in range(z_count)]

    def row_halo(last, first):
        return lax.ppermute(last, "z", down_z), lax.ppermute(first, "z", up_z)

    def other_core(cells):
        return lax.ppermute(cells, "core", [(i, CORES - 1 - i) for i in range(CORES)])

    own = lax.all_to_all(sent, ("x", "y"), 0, 0, tiled=False)
    own = own.reshape(GROUP, y_count, band + TAIL, lanes)
    above, below = row_halo(own[GROUP - reach :], own[:reach])
    layers = (above, own, below)
    layers = layers + tuple(other_core(part) for part in layers)

    flops = 2 * slices * rows * lanes * (2 * rows + lanes)
    kept, seed = call(
        functools.partial(forward_body, (band, TAIL // 2)),
        (shape(slices, own_rows, 2 * LANES), shape(own_rows, LANES)),
        [],
        [row_fwd, col_fwd, *layers],
        (flops, 6_000_000),
        [
            pltpu.VMEM((rows, lanes), F32),
            pltpu.VMEM((rows, lanes), BF16),
            pltpu.VMEM((own_rows, LANES), F32),
        ],
    )
    seed_above, seed_below = row_halo(seed[own_rows - halo :], seed[:halo])
    seeds = jnp.concatenate([seed_above, seed, seed_below], axis=0)
    at = {}
    for y in range(y_count):
        for x in range(GROUP):
            at[tile_at(x, y, y_count, probes)] = y * GROUP + x
    right = [(at[p, c], at[p, c + 1]) for p in range(probes) for c in range(tiles - 1)]
    from_left = lax.ppermute(seeds, ("y", "x"), right)
    from_right = lax.ppermute(seeds, ("y", "x"), [(b, a) for a, b in right])
    terms = call(
        functools.partial(backward_body, (band,)),
        shape(GROUP, y_count, band, LANES),
        [],
        [row_bwd, col_bwd, *layers, kept, seeds, from_left, from_right],
        (flops, 6_000_000),
        [pltpu.VMEM((rows, lanes), BF16), pltpu.VMEM((rows, lanes), BF16)],
    )
    gathered = lax.all_to_all(
        terms.reshape(spots, band, LANES), ("x", "y"), 0, 0, tiled=False
    )
    gradient = call(
        functools.partial(collect_body, (probes, tiles, y_count, lat_count, window, columns)),
        shape(2, 2, band, columns, dtype=F32),
        [offsets],
        [gathered],
        (1_000_000, 2_000_000),
    )
    return gradient[:, None]


def solution(mesh):
    depth_count, lat_count = mesh.devices.shape
    grid = mesh.devices.reshape(depth_count // CORES, CORES, lat_count // GROUP, GROUP)
    fine = Mesh(grid, ("y", "core", "z", "x"))
    depth, lat = ("y", "core"), ("z", "x")
    in_specs = (
        P(None, depth, None, lat, None),
        P(None, None, lat, None),
        P(None, lat, None),
        P(),
        P(),
    )
    out_specs = P(None, depth, None, lat, None)
    return jax.shard_map(local, mesh=fine, in_specs=in_specs, out_specs=out_specs, check_vma=False)
```

time: 694 us -> 133 us (0.19)
  the two profiles are of different devices: /device:TPU:25 before, /device:TPU:8 now
where the time goes in v2:
time: 133 us; the launch traced here: 132 us
  blocking collectives  54.5 us (41%)
  starting transfers between devices  32 us (24%)
  Pallas kernels  31.2 us (23%)
  waiting for transfers between devices  10.2 us (8%)
  local copies, waits for them, and re-layouts  4.11 us (3%)
    all_to_all x1, blocking collectives, local(): own = lax.all_to_all(sent, ('x', 'y'), 0, 0, tiled=False)  37.2 us
    pallas_call x5, Pallas kernels, call(): pl.pallas_call(body, out_shape=outs, in_specs=in_specs, out_specs=jax.tre...  31.2 us
    ppermute x4, starting transfers between devices, row_halo(): return (lax.ppermute(last, 'z', down_z), lax.ppermute(first, 'z', up_z))  19.9 us
    all_to_all x1, blocking collectives, local(): lax.all_to_all(terms.reshape(spots, band, LANES), ('x', 'y'), 0, 0, tiled...  17.3 us
    ppermute x4, waiting for transfers between devices, row_halo(): return (lax.ppermute(last, 'z', down_z), lax.ppermute(first, 'z', up_z))  6.58 us
    ppermute x3, starting transfers between devices, other_core(): lax.ppermute(cells, 'core', [(i, CORES - 1 - i) for i in range(CORES)])  6.24 us
    unnamed x12, local copies, waits for them, and re-layouts  3.91 us
    ppermute x1, waiting for transfers between devices, local(): from_left = lax.ppermute(seeds, ('y', 'x'), right)  3.36 us
  transfers between devices with their start and end apart: 9, of which 4 were waited for; matrix products, arithmetic and copies ran while one was open for 0% of the time, Pallas kernels for 1%

profile of v2, /device:TPU:8, one launch (start us, length us, event | category | flops | bytes accessed | tf_op | source)
XLA Modules:
  0.0 132.2 jit_solution(12202075093359668308)
XLA Ops:
  0.0 0.0 copy-start.3
  0.0 0.7 copy-done.3
  0.7 0.0 copy-start
  0.7 1.2 copy-done
  1.9 0.0 copy-start.1
  1.9 1.0 copy-done.1
  2.9 0.0 copy-start.2
  2.9 0.9 copy-done.2
  3.9 2.8 %shard_map.56 = bf16[32,40,384]{2,1,0:T(8,128)(2,1)S(1)} custom-call(s32[2,2]{1,0:T(2,128)S(1)} %copy-done.3, f32[2,2,32,2048]{3,2,1,0:T(8,128)S(1)} %bitcast.11, f32[2,2,32,1024]{3,2,1,0:T(8,128)S(1)} %copy-done.1, f32[2,32,1024]{2,1,0:T(8,128)S(1)} %copy-done.2), custom_call_target="tpu_custom_call" | custom-call | flops 20000000 | bytes 3000000 | tf_op jit(solution)/shard_map/pallas_call | solution.py:33
  6.7 37.2 %all_to_all.10 = bf16[32,40,384]{2,1,0:T(8,128)(2,1)S(1)} all-to-all(bf16[32,40,384]{2,1,0:T(8,128)(2,1)S(1)} %shard_map.56), channel_id=1, replica_groups=mesh['y'=8,'core'=2,'z'=8,'x'=4] {'x','y'}, dimensions={0} | all-to-all | bytes 1966080 | tf_op jit(solution)/shard_map/all_to_all | solution.py:427
  43.9 0.1 fusion
  44.0 4.3 %collective-permute-start = (bf16[2,8,40,384]{3,2,1,0:T(8,128)(2,1)S(1)}, bf16[2,8,40,384]{3,2,1,0:T(8,128)(2,1)S(1)}, u32[]{:S(2)}, u32[]{:S(2)}) collective-permute-start(bf16[2,8,40,384]{3,2,1,0:T(8,128)(2,1)S(1)} %bitcast.14), channel_id=1, source_target_pairs={{0,4},{4,8},{8,12},{12,16},{16,20},{20,24},{24,28},{28,0},{1,5},{5... | collective-permute-start | bytes 1474568 | tf_op jit(solution)/shard_map/ppermute | solution.py:422
  48.2 0.0 copy-start.4
  48.3 8.6 %collective-permute-start.1 = (bf16[2,8,40,384]{3,2,1,0:T(8,128)(2,1)S(1)}, bf16[2,8,40,384]{3,2,1,0:T(8,128)(2,1)S(1)}, u32[]{:S(2)}, u32[]{:S(2)}) collective-permute-start(bf16[2,8,40,384]{3,2,1,0:T(8,128)(2,1)S(1)} %bitcast.13), channel_id=1, source_target_pairs={{4,0},{8,4},{12,8},{16,12},{20,16},{24,20},{28,24},{0,28},{5,1},{9... | collective-permute-start | bytes 1474568 | tf_op jit(solution)/shard_map/ppermute | solution.py:422
  56.9 1.9 %collective-permute-start.3 = (bf16[4,8,40,384]{3,2,1,0:T(8,128)(2,1)S(1)}, bf16[4,8,40,384]{3,2,1,0:T(8,128)(2,1)S(1)}, u32[]{:S(2)}, u32[]{:S(2)}) collective-permute-start(bf16[4,8,40,384]{3,2,1,0:T(8,128)(2,1)S(1)} %bitcast.8), channel_id=1, source_target_pairs={{0,32},{32,0},{1,33},{33,1},{2,34},{34,2},{3,35},{35,3},{4,36},{36... | collective-permute-start | bytes 2949128 | tf_op jit(solution)/shard_map/ppermute | solution.py:425
  58.8 5.2 %collective-permute-done.above = bf16[2,8,40,384]{3,2,1,0:T(8,128)(2,1)S(1)} collective-permute-done((bf16[2,8,40,384]{3,2,1,0:T(8,128)(2,1)S(1)}, bf16[2,8,40,384]{3,2,1,0:T(8,128)(2,1)S(1)}, u32[]{:S(2)}, u32[]{:S(2)}) %collective-permute-start) | collective-permute-done | bytes 491552 | tf_op jit(solution)/shard_map/ppermute | solution.py:422
  64.0 1.9 %collective-permute-start.2 = (bf16[2,8,40,384]{3,2,1,0:T(8,128)(2,1)S(1)}, bf16[2,8,40,384]{3,2,1,0:T(8,128)(2,1)S(1)}, u32[]{:S(2)}, u32[]{:S(2)}) collective-permute-start(bf16[2,8,40,384]{3,2,1,0:T(8,128)(2,1)S(1)} %collective-permute-done.above), channel_id=1, source_target_pairs={{0,32},{32,0},{1,33},{33,1},{2,34},{34,2},{3,35},{35,3},{4,36},{36... | collective-permute-start | bytes 1474568 | tf_op jit(solution)/shard_map/ppermute | solution.py:425
  65.9 0.0 collective-permute-done.1.below
  65.9 2.4 %collective-permute-start.4 = (bf16[2,8,40,384]{3,2,1,0:T(8,128)(2,1)S(1)}, bf16[2,8,40,384]{3,2,1,0:T(8,128)(2,1)}, u32[]{:S(2)}, u32[]{:S(2)}) collective-permute-start(bf16[2,8,40,384]{3,2,1,0:T(8,128)(2,1)S(1)} %collective-permute-done.1.below), channel_id=1, source_target_pairs={{0,32},{32,0},{1,33},{33,1},{2,34},{34,2},{3,35},{35,3},{4,36},{36... | collective-permute-start | bytes 1474568 | tf_op jit(solution)/shard_map/ppermute | solution.py:425
  68.3 0.0 copy-done.4
  68.3 0.1 reshape.18.taps
  68.4 1.9 %shard_map.55 = (bf16[256,512]{1,0:T(8,128)(2,1)S(1)}, bf16[256,512]{1,0:T(8,128)(2,1)S(1)}, bf16[384,384]{1,0:T(8,128)(2,1)S(1)}, bf16[384,384]{1,0:T(8,128)(2,1)S(1)}) custom-call(s32[2,2]{1,0:T(2,128)S(1)} %copy-done.3, f32[18]{0:T(128)S(1)} %reshape.18.taps), custom_call_target="tpu_custom_call" | custom-call | flops 20000000 | bytes 1500000 | tf_op jit(solution)/shard_map/pallas_call | solution.py:33
  70.4 0.0 collective-permute-done.2.o_above
  70.4 0.0 collective-permute-done.4.o_below
  70.4 0.0 collective-permute-done.3.o_own
  70.4 11.1 %shard_map.57 = (bf16[16,128,256]{2,1,0:T(8,128)(2,1)S(1)}, bf16[128,128]{1,0:T(8,128)(2,1)S(1)}) custom-call(bf16[256,512]{1,0:T(8,128)(2,1)S(1)} %get-tuple-element.13.row_mat, bf16[384,384]{1,0:T(8,128)(2,1)S(1)} %get-tuple-element.14.col_mat, bf16[2,8,40,384]{3,2,1,0:T(8,128)(2,1)S(1)} %collective-permute-done.above, ...), custom_call_target="tpu_custom_call" | custom-call | flops 2818572288 | bytes 6000000 | tf_op jit(solution)/shard_map/pallas_call | solution.py:33
  81.5 1.9 %collective-permute-start.5 = (bf16[64,128]{1,0:T(8,128)(2,1)S(1)}, bf16[64,128]{1,0:T(8,128)(2,1)S(1)}, u32[]{:S(2)}, u32[]{:S(2)}) collective-permute-start(bf16[64,128]{1,0:T(8,128)(2,1)S(1)} %get-tuple-element.20), channel_id=1, source_target_pairs={{0,4},{4,8},{8,12},{12,16},{16,20},{20,24},{24,28},{28,0},{1,5},{5... | collective-permute-start | bytes 49160 | tf_op jit(solution)/shard_map/ppermute | solution.py:422
  83.4 5.1 %collective-permute-start.6 = (bf16[64,128]{1,0:T(8,128)(2,1)S(1)}, bf16[64,128]{1,0:T(8,128)(2,1)S(1)}, u32[]{:S(2)}, u32[]{:S(2)}) collective-permute-start(bf16[64,128]{1,0:T(8,128)(2,1)S(1)} %get-tuple-element.19), channel_id=1, source_target_pairs={{4,0},{8,4},{12,8},{16,12},{20,16},{24,20},{28,24},{0,28},{5,1},{9... | collective-permute-start | bytes 49160 | tf_op jit(solution)/shard_map/ppermute | solution.py:422
  88.5 0.0 collective-permute-done.5
  88.6 1.4 %collective-permute-done.6 = bf16[64,128]{1,0:T(8,128)(2,1)S(1)} collective-permute-done((bf16[64,128]{1,0:T(8,128)(2,1)S(1)}, bf16[64,128]{1,0:T(8,128)(2,1)S(1)}, u32[]{:S(2)}, u32[]{:S(2)}) %collective-permute-start.6) | collective-permute-done | bytes 16416 | tf_op jit(solution)/shard_map/ppermute | solution.py:422
  90.0 3.3 %collective-permute-start.8 = (bf16[256,128]{1,0:T(8,128)(2,1)S(1)}, bf16[256,128]{1,0:T(8,128)(2,1)S(1)}, u32[]{:S(2)}, u32[]{:S(2)}) collective-permute-start(bf16[256,128]{1,0:T(8,128)(2,1)S(1)} %constant_dynamic-update-slice_fusion.seeds), channel_id=1, source_target_pairs={{1,0},{2,1},{3,2},{67,3},{66,67},{65,66},{64,65},{128,64},{129,128... | collective-permute-start | bytes 196616 | tf_op jit(solution)/shard_map/ppermute | solution.py:454
  93.3 2.5 %collective-permute-start.7 = (bf16[256,128]{1,0:T(8,128)(2,1)S(1)}, bf16[256,128]{1,0:T(8,128)(2,1)S(1)}, u32[]{:S(2)}, u32[]{:S(2)}) collective-permute-start(bf16[256,128]{1,0:T(8,128)(2,1)S(1)} %constant_dynamic-update-slice_fusion.seeds), channel_id=1, source_target_pairs={{0,1},{1,2},{2,3},{3,67},{67,66},{66,65},{65,64},{64,128},{128,129... | collective-permute-start | bytes 196616 | tf_op jit(solution)/shard_map/ppermute | solution.py:453
  95.8 0.3 collective-permute-done.8.right
  96.1 3.4 %collective-permute-done.7.left = bf16[256,128]{1,0:T(8,128)(2,1)S(1)} collective-permute-done((bf16[256,128]{1,0:T(8,128)(2,1)S(1)}, bf16[256,128]{1,0:T(8,128)(2,1)S(1)}, u32[]{:S(2)}, u32[]{:S(2)}) %collective-permute-start.7) | collective-permute-done | bytes 65568 | tf_op jit(solution)/shard_map/ppermute | solution.py:453
  99.5 13.4 %shard_map.58 = bf16[4,8,32,128]{3,2,1,0:T(8,128)(2,1)S(1)} custom-call(bf16[256,512]{1,0:T(8,128)(2,1)S(1)} %get-tuple-element.11.row_mat, bf16[384,384]{1,0:T(8,128)(2,1)S(1)} %get-tuple-element.12.col_mat, bf16[2,8,40,384]{3,2,1,0:T(8,128)(2,1)S(1)} %collective-permute-done.above, bf16[4,8,40,384]{3,2,1,0:T(8,128)(2,1)S(1)} %bitcast.10, ...), custom_call_target="tpu_custom_call" | custom-call | flops 2818572288 | bytes 6000000 | tf_op jit(solution)/shard_map/pallas_call | solution.py:33
  112.9 17.3 %all_to_all.11.terms = bf16[32,32,128]{2,1,0:T(8,128)(2,1)S(1)} all-to-all(bf16[32,32,128]{2,1,0:T(8,128)(2,1)S(1)} %bitcast.12), channel_id=1, replica_groups=mesh['y'=8,'core'=2,'z'=8,'x'=4] {'x','y'}, dimensions={0} | all-to-all | bytes 524288 | tf_op jit(solution)/shard_map/all_to_all | solution.py:463
  130.2 2.0 %shard_map.59 = f32[2,2,32,2048]{3,2,1,0:T(8,128)} custom-call(s32[2,2]{1,0:T(2,128)S(1)} %copy-done.3, bf16[32,32,128]{2,1,0:T(8,128)(2,1)S(1)} %all_to_all.11.terms), custom_call_target="tpu_custom_call" | custom-call | flops 1000000 | bytes 2000000 | tf_op jit(solution)/shard_map/pallas_call | solution.py:33
  (4 shorter events, 0.0 us)
Async XLA Ops:
  0.0 0.7 copy-start.3
  0.7 1.2 copy-start
  1.9 1.0 copy-start.1
  2.9 0.9 copy-start.2
  44.0 20.0 %collective-permute-start = (bf16[2,8,40,384]{3,2,1,0:T(8,128)(2,1)S(1)}, bf16[2,8,40,384]{3,2,1,0:T(8,128)(2,1)S(1)}, u32[]{:S(2)}, u32[]{:S(2)}) collective-permute-start(bf16[2,8,40,384]{3,2,1,0:T(8,128)(2,1)S(1)} %bitcast.14), channel_id=1, source_target_pairs={{0,4},{4,8},{8,12},{12,16},{16,20},{20,24},{24,28},{28,0},{1,5},{5... | collective-permute-start | bytes 1474568 | tf_op jit(solution)/shard_map/ppermute | solution.py:422
  48.2 20.1 %copy-start.4 = (bf16[2,9]{1,0:T(2,128)(2,1)S(1)}, bf16[2,9]{1,0:T(2,128)(2,1)}, u32[]{:S(2)}) copy-start(bf16[2,9]{1,0:T(2,128)(2,1)} %param.9) | copy-start | bytes 112
  48.3 17.6 %collective-permute-start.1 = (bf16[2,8,40,384]{3,2,1,0:T(8,128)(2,1)S(1)}, bf16[2,8,40,384]{3,2,1,0:T(8,128)(2,1)S(1)}, u32[]{:S(2)}, u32[]{:S(2)}) collective-permute-start(bf16[2,8,40,384]{3,2,1,0:T(8,128)(2,1)S(1)} %bitcast.13), channel_id=1, source_target_pairs={{4,0},{8,4},{12,8},{16,12},{20,16},{24,20},{28,24},{0,28},{5,1},{9... | collective-permute-start | bytes 1474568 | tf_op jit(solution)/shard_map/ppermute | solution.py:422
  56.9 13.5 %collective-permute-start.3 = (bf16[4,8,40,384]{3,2,1,0:T(8,128)(2,1)S(1)}, bf16[4,8,40,384]{3,2,1,0:T(8,128)(2,1)S(1)}, u32[]{:S(2)}, u32[]{:S(2)}) collective-permute-start(bf16[4,8,40,384]{3,2,1,0:T(8,128)(2,1)S(1)} %bitcast.8), channel_id=1, source_target_pairs={{0,32},{32,0},{1,33},{33,1},{2,34},{34,2},{3,35},{35,3},{4,36},{36... | collective-permute-start | bytes 2949128 | tf_op jit(solution)/shard_map/ppermute | solution.py:425
  64.0 6.4 %collective-permute-start.2 = (bf16[2,8,40,384]{3,2,1,0:T(8,128)(2,1)S(1)}, bf16[2,8,40,384]{3,2,1,0:T(8,128)(2,1)S(1)}, u32[]{:S(2)}, u32[]{:S(2)}) collective-permute-start(bf16[2,8,40,384]{3,2,1,0:T(8,128)(2,1)S(1)} %collective-permute-done.above), channel_id=1, source_target_pairs={{0,32},{32,0},{1,33},{33,1},{2,34},{34,2},{3,35},{35,3},{4,36},{36... | collective-permute-start | bytes 1474568 | tf_op jit(solution)/shard_map/ppermute | solution.py:425
  65.9 4.5 %collective-permute-start.4 = (bf16[2,8,40,384]{3,2,1,0:T(8,128)(2,1)S(1)}, bf16[2,8,40,384]{3,2,1,0:T(8,128)(2,1)}, u32[]{:S(2)}, u32[]{:S(2)}) collective-permute-start(bf16[2,8,40,384]{3,2,1,0:T(8,128)(2,1)S(1)} %collective-permute-done.1.below), channel_id=1, source_target_pairs={{0,32},{32,0},{1,33},{33,1},{2,34},{34,2},{3,35},{35,3},{4,36},{36... | collective-permute-start | bytes 1474568 | tf_op jit(solution)/shard_map/ppermute | solution.py:425
  81.5 7.1 %collective-permute-start.5 = (bf16[64,128]{1,0:T(8,128)(2,1)S(1)}, bf16[64,128]{1,0:T(8,128)(2,1)S(1)}, u32[]{:S(2)}, u32[]{:S(2)}) collective-permute-start(bf16[64,128]{1,0:T(8,128)(2,1)S(1)} %get-tuple-element.20), channel_id=1, source_target_pairs={{0,4},{4,8},{8,12},{12,16},{16,20},{20,24},{24,28},{28,0},{1,5},{5... | collective-permute-start | bytes 49160 | tf_op jit(solution)/shard_map/ppermute | solution.py:422
  83.4 6.6 %collective-permute-start.6 = (bf16[64,128]{1,0:T(8,128)(2,1)S(1)}, bf16[64,128]{1,0:T(8,128)(2,1)S(1)}, u32[]{:S(2)}, u32[]{:S(2)}) collective-permute-start(bf16[64,128]{1,0:T(8,128)(2,1)S(1)} %get-tuple-element.19), channel_id=1, source_target_pairs={{4,0},{8,4},{12,8},{16,12},{20,16},{24,20},{28,24},{0,28},{5,1},{9... | collective-permute-start | bytes 49160 | tf_op jit(solution)/shard_map/ppermute | solution.py:422
  90.0 6.1 %collective-permute-start.8 = (bf16[256,128]{1,0:T(8,128)(2,1)S(1)}, bf16[256,128]{1,0:T(8,128)(2,1)S(1)}, u32[]{:S(2)}, u32[]{:S(2)}) collective-permute-start(bf16[256,128]{1,0:T(8,128)(2,1)S(1)} %constant_dynamic-update-slice_fusion.seeds), channel_id=1, source_target_pairs={{1,0},{2,1},{3,2},{67,3},{66,67},{65,66},{64,65},{128,64},{129,128... | collective-permute-start | bytes 196616 | tf_op jit(solution)/shard_map/ppermute | solution.py:454
  93.3 6.2 %collective-permute-start.7 = (bf16[256,128]{1,0:T(8,128)(2,1)S(1)}, bf16[256,128]{1,0:T(8,128)(2,1)S(1)}, u32[]{:S(2)}, u32[]{:S(2)}) collective-permute-start(bf16[256,128]{1,0:T(8,128)(2,1)S(1)} %constant_dynamic-update-slice_fusion.seeds), channel_id=1, source_target_pairs={{0,1},{1,2},{2,3},{3,67},{67,66},{66,65},{65,64},{64,128},{128,129... | collective-permute-start | bytes 196616 | tf_op jit(solution)/shard_map/ppermute | solution.py:453

commit v3 on v2

v3 whole, which is shorter than its diff:
```python
import functools

import jax
import jax.numpy as jnp
from jax import lax
from jax.experimental import pallas as pl
from jax.experimental.pallas import tpu as pltpu
from jax.sharding import Mesh
from jax.sharding import PartitionSpec as P

F32 = jnp.float32
BF16 = jnp.bfloat16
LANES = 128
PIECE = 64
CORES = 2
GROUP = 4
TAIL = 8
VMEM_BYTES = 16 * 1024 * 1024
WIDE_BYTES = 60 * 1024 * 1024


def vmem_spec():
    return pl.BlockSpec(memory_space=pltpu.VMEM)


def smem_spec():
    return pl.BlockSpec(memory_space=pltpu.SMEM)


def call(body, outs, scalars, arrays, cost, scratch=(), outside=0, grant=VMEM_BYTES):
    in_specs = [smem_spec()] * len(scalars)
    in_specs += [pl.BlockSpec(memory_space=pltpu.HBM)] * outside
    in_specs += [vmem_spec()] * (len(arrays) - outside)
    return pl.pallas_call(
        body,
        out_shape=outs,
        in_specs=in_specs,
        out_specs=jax.tree.map(lambda _: vmem_spec(), outs),
        scratch_shapes=list(scratch),
        compiler_params=pltpu.CompilerParams(vmem_limit_bytes=grant),
        cost_estimate=pl.CostEstimate(flops=cost[0], bytes_accessed=cost[1], transcendentals=0),
    )(*scalars, *arrays)


def tile_at(x, y, y_count, probes):
    rows = y_count // probes
    probe, row = y // rows, y % rows
    return probe, row * GROUP + (x if row % 2 == 0 else GROUP - 1 - x)


def low_lanes(rows):
    return lax.broadcasted_iota(jnp.int32, (rows, LANES), 1) < PIECE


def swap_halves(cells):
    return pltpu.roll(cells, PIECE, 1)


def half_of(offsets, probe, band, lat, lat_count):
    first = offsets[probe, 0] // band
    return (first + lax.rem(lat - first + lat_count, lat_count)) // lat_count


def packed(real, imag, tiles):
    span = real.shape[1]
    real_on = pltpu.roll(real, span - PIECE, 1)
    imag_on = pltpu.roll(imag, span - PIECE, 1)
    low = low_lanes(real.shape[0])
    out = []
    for tile in range(tiles):
        base = tile // 2 * LANES
        here, there = slice(base, base + LANES), slice(base + LANES, base + 2 * LANES)
        if tile % 2 == 0:
            middle = jnp.where(low, real[:, there], imag_on[:, here])
            out.append((real[:, here], middle, imag[:, here]))
        else:
            middle = jnp.where(low, real_on[:, there], imag[:, there])
            out.append((real_on[:, here], middle, imag_on[:, here]))
    return out


def prepare_body(
    dims, offsets, potential, incident, measured, sent, pot_buf, inc_buf, mea_buf, sems
):
    probes, tiles, halo, y_count, lat_count = dims
    band, columns = pot_buf.shape[2], pot_buf.shape[3]
    window = inc_buf.shape[3]
    span = window + 2 * halo
    y = lax.axis_index("y")
    lat = lax.axis_index("z") * GROUP + lax.axis_index("x")
    strip = TAIL // 2
    first = pl.multiple_of(y // 2 * TAIL, TAIL)
    copies = []
    for probe in range(probes):
        half = half_of(offsets, probe, band, lat, lat_count)
        copies.append(
            pltpu.make_async_copy(potential.at[:, half], pot_buf.at[probe], sems.at[probe])
        )
    copies.append(
        pltpu.make_async_copy(incident.at[:, :, pl.ds(first, TAIL)], inc_buf, sems.at[probes])
    )
    copies.append(
        pltpu.make_async_copy(measured.at[:, pl.ds(first, TAIL)], mea_buf, sems.at[probes + 1])
    )
    for copy in copies:
        copy.start()
    slots = {}
    for spot in range(y_count * GROUP):
        slots[tile_at(spot // y_count, spot % y_count, y_count, probes)] = spot
    lane = lax.broadcasted_iota(jnp.int32, (band, span), 1)
    inside = (lane >= halo) & (lane < window + halo)
    for probe in range(probes):
        copies[probe].wait()
        turn = lax.rem(columns + halo - offsets[probe, 1], columns)
        phase = pltpu.roll(pot_buf[probe, 0], turn, 1)[:, :span]
        absorb = pltpu.roll(pot_buf[probe, 1], turn, 1)[:, :span]
        damping = jnp.where(inside, jnp.exp(-absorb), 0.0)
        for tile, parts in enumerate(
            packed(damping * jnp.cos(phase), damping * jnp.sin(phase), tiles)
        ):
            for at, part in enumerate(parts):
                cols = slice(at * LANES, (at + 1) * LANES)
                sent[slots[probe, tile], :band, cols] = part.astype(BF16)
    copies[probes].wait()
    copies[probes + 1].wait()
    odd = lax.rem(y, 2) == 1
    rest = jnp.zeros((TAIL, 2 * halo), F32)
    upper = lax.broadcasted_iota(jnp.int32, (TAIL, LANES), 0) < strip
    low = low_lanes(TAIL)
    for probe in range(probes):
        wide = []
        for part in range(2):
            rows = inc_buf[part, probe]
            rows = jnp.where(odd, pltpu.roll(rows, strip, 0), rows)
            wide.append(pltpu.roll(jnp.concatenate([rows, rest], axis=1), halo, 1))
        rows = mea_buf[probe]
        rows = jnp.where(odd, rows, pltpu.roll(rows, strip, 0))
        coarse = rows.astype(BF16).astype(F32)
        fine = rows - coarse
        coarse_on = pltpu.roll(coarse, window - PIECE, 1)
        fine_back = pltpu.roll(fine, PIECE, 1)
        for tile, parts in enumerate(packed(wide[0], wide[1], tiles)):
            here = slice(tile // 2 * LANES, tile // 2 * LANES + LANES)
            if tile % 2 == 0:
                both = jnp.where(low, coarse[:, here], fine_back[:, here])
            else:
                both = jnp.where(low, coarse_on[:, here], fine[:, here])
            for at, part in enumerate(parts):
                cols = slice(at * LANES, (at + 1) * LANES)
                under = both if at == 0 else jnp.zeros_like(both)
                sent[slots[probe, tile], band:, cols] = jnp.where(upper, part, under).astype(BF16)


def banded(taps, diff, half_width, conj):
    count = 2 * half_width + 1
    real = jnp.zeros(diff.shape, F32)
    imag = jnp.zeros(diff.shape, F32)
    for tap in range(count):
        hit = diff == tap - half_width
        source = count - 1 - tap if conj else tap
        real = jnp.where(hit, taps[source], real)
        value = taps[count + source]
        imag = jnp.where(hit, -value if conj else value, imag)
    return real, imag


def matrices_body(dims, offsets, taps, *outs):
    band, half_width, y_count, probes, lat_count, reach, phase_rows = dims
    own = lax.axis_index("y") // (y_count // probes)
    start = lax.axis_index("z") * GROUP + lax.axis_index("core") * (GROUP // CORES) - reach
    base = lax.rem(start - offsets[own, 0] // band + 2 * lat_count, lat_count)

    def window_row(rows, axis):
        skip = (phase_rows[0] - rows) // 2
        index = lax.broadcasted_iota(jnp.int32, (rows, rows), axis) + skip
        at = index + base * band
        return jnp.where(at >= lat_count * band, at - lat_count * band, at)

    def column(lanes, axis):
        index = lax.broadcasted_iota(jnp.int32, (lanes, lanes), axis)
        if lanes == 2 * LANES:
            return jnp.where(index >= LANES, index - LANES, index), index >= LANES
        imag = index >= LANES + PIECE
        inner = jnp.where(imag, index - PIECE, index)
        return jnp.where(index >= 2 * LANES, index - 2 * LANES, inner), imag

    count = len(phase_rows)
    for at, rows in enumerate(phase_rows):
        diff = window_row(rows, 1) - window_row(rows, 0)
        for conj in (False, True):
            real, imag = banded(taps, diff, half_width, conj)
            out = outs[at + count * conj]
            out[...] = jnp.concatenate([real, imag], axis=1).astype(BF16)
    for at in range(2):
        lanes = outs[2 * count + at].shape[0]
        in_col, in_imag = column(lanes, 0)
        out_col, out_imag = column(lanes, 1)
        for conj in (False, True):
            real, imag = banded(taps, in_col - out_col, half_width, conj)
            signed = jnp.where(in_imag, -imag, imag)
            outs[2 * count + at + 2 * conj][...] = jnp.where(
                in_imag == out_imag, real, signed
            ).astype(BF16)


def parts_of(cells):
    return tuple(cells[:, at : at + LANES] for at in range(0, cells.shape[1], LANES))


def fill_layer(layer, own, halo, y, band, core):
    reach = halo.shape[0] * band
    for index in range(own.shape[0]):
        layer[reach + index * band : reach + (index + 1) * band] = own[index, y, :band]
    base = core * (reach + own.shape[0] * band)
    for index in range(halo.shape[0]):
        at = pl.multiple_of(base + index * band, band)
        layer[pl.ds(at, band)] = halo[index, y, :band]


def narrowed(wide):
    first, middle, last = wide
    edge = lax.broadcasted_iota(jnp.int32, first.shape, 1) < LANES - PIECE // 2
    on, back = LANES - PIECE // 2, PIECE // 2
    real = jnp.where(edge, pltpu.roll(first, on, 1), pltpu.roll(middle, on, 1))
    imag = jnp.where(edge, pltpu.roll(last, on, 1), pltpu.roll(middle, back, 1))
    return real, imag


def own_columns(parts, rows):
    low = low_lanes(rows)
    if len(parts) == 3:
        return jnp.where(low, swap_halves(parts[0]), parts[2])
    real = pltpu.roll(parts[0], LANES - PIECE // 2, 1)
    return jnp.where(low, real, pltpu.roll(parts[1], PIECE // 2, 1))


def times(t, field, conj):
    sign = -1.0 if conj else 1.0
    if len(t) == 2:
        return (
            t[0] * field[0] - sign * (t[1] * field[1]),
            t[0] * field[1] + sign * (t[1] * field[0]),
        )
    low = low_lanes(t[0].shape[0])
    turned = swap_halves(t[1])
    real = jnp.where(low, t[1], turned)
    imag = jnp.where(low, -turned, t[1])
    return (
        t[0] * field[0] - sign * (t[2] * field[2]),
        real * field[1] + sign * (imag * swap_halves(field[1])),
        t[0] * field[2] + sign * (t[2] * field[0]),
    )


def with_quarter_turn(parts):
    if len(parts) == 2:
        crossed = (-parts[1], parts[0])
    else:
        low = low_lanes(parts[1].shape[0])
        turned = swap_halves(parts[1])
        crossed = (-parts[2], jnp.where(low, -turned, turned), parts[0])
    both = [jnp.concatenate(rows, axis=1) for rows in (parts, crossed)]
    return jnp.concatenate(both, axis=0).astype(BF16)


def phases(dims):
    phase_rows, y_count = dims
    each = y_count // len(phase_rows)
    for at, rows in enumerate(phase_rows):
        skip = (phase_rows[0] - rows) // 2
        yield at, at * each, each, skip, rows, at < len(phase_rows) // 2


def narrow_state(state, skip, rows):
    here = slice(skip, skip + rows)
    real, imag = narrowed(parts_of(state[here].astype(F32)))
    state[here, :LANES] = real.astype(state.dtype)
    state[here, LANES : 2 * LANES] = imag.astype(state.dtype)


def layer_parts(layer, core, reach, skip, rows, wide):
    at = pl.multiple_of(core * reach + skip, 16)
    parts = parts_of(layer[pl.ds(at, rows)].astype(F32))
    return parts if wide else narrowed(parts)


def forward_body(dims, *refs):
    band, phase_rows = dims
    count = len(phase_rows)
    row_mats, col_mats = refs[:count], refs[count : count + 2]
    own, halo, o_own, o_halo, kept, seed, psi, layer, goal, wave = refs[count + 2 :]
    core = lax.axis_index("core")
    strip = TAIL // 2
    total = phase_rows[0]
    own_rows = own.shape[0] * band // CORES
    head = (total - own_rows) // 2
    reach = halo.shape[0] * band
    y_count = own.shape[1]
    upper = lax.broadcasted_iota(jnp.int32, (TAIL, 3 * LANES), 0) < strip

    def tails(part, index, pair):
        one = part[index, 2 * pair, band:].astype(F32)
        two = part[index, 2 * pair + 1, band:].astype(F32)
        return one, two

    for part, base in ((own, reach), (halo, core * (reach + own.shape[0] * band))):
        for index in range(part.shape[0]):
            for pair in range(y_count // 2):
                one, two = tails(part, index, pair)
                at = base + index * band + pair * TAIL
                at = at if part is own else pl.multiple_of(at, TAIL)
                wave[pl.ds(at, TAIL)] = jnp.where(upper, one, pltpu.roll(two, strip, 0))
    psi[...] = wave[pl.ds(pl.multiple_of(core * reach, band), total)]
    for index in range(own.shape[0] // CORES):
        for pair in range(y_count // 2):
            one, two = tails(own, core * (own.shape[0] // CORES) + index, pair)
            both = jnp.where(upper, pltpu.roll(one, strip, 0), two)[:, :LANES]
            at = index * band + pair * TAIL
            goal[at : at + TAIL] = both + swap_halves(both)

    for phase, y_first, each, skip, rows, wide in phases((phase_rows, y_count)):
        lanes = (3 if wide else 2) * LANES
        here = slice(skip, skip + rows)
        mine_rows = slice(head - skip, head - skip + own_rows)
        if phase == count // 2:
            narrow_state(psi, skip, rows)

        def two_slices(step, _):
            y = y_first + step
            for parity in range(CORES):
                mine = core == parity
                pl.when(mine)(lambda: fill_layer(layer, own, halo, y, band, core))
                pl.when(jnp.logical_not(mine))(
                    lambda: fill_layer(layer, o_own, o_halo, y, band, core)
                )
                t = layer_parts(layer, core, reach, skip, rows, wide)
                product = times(t, parts_of(psi[here, :lanes]), False)
                inner = [part[mine_rows] for part in product]
                kept[CORES * y + parity] = own_columns(inner, own_rows).astype(BF16)
                field = with_quarter_turn(product)
                spread = jnp.dot(row_mats[phase][...], field, preferred_element_type=F32)
                col_mat = col_mats[0 if wide else 1][...]
                psi[here, :lanes] = jnp.dot(
                    spread.astype(BF16), col_mat, preferred_element_type=F32
                )
            return 0

        lax.fori_loop(0, each, two_slices, 0)
    wave_out = own_columns(parts_of(psi[head : head + own_rows, : 2 * LANES]), own_rows)
    square = wave_out * wave_out
    residual = square + swap_halves(square) - goal[...]
    seed[...] = (2.0 * residual * wave_out).astype(BF16)


def backward_body(dims, *refs):
    band, phase_rows = dims
    count = len(phase_rows)
    row_mats, col_mats = refs[:count], refs[count : count + 2]
    own, halo, o_own, o_halo, kept, seeds, left, right = refs[count + 2 : count + 10]
    terms, o_terms, field, layer = refs[count + 10 :]
    core = lax.axis_index("core")
    own_rows = own.shape[0] * band // CORES
    head = (phase_rows[0] - own_rows) // 2
    reach = halo.shape[0] * band
    y_count = own.shape[1]
    low = low_lanes(phase_rows[0])
    low_own = low_lanes(own_rows)
    middle = seeds[...].astype(F32)
    beside = left[...].astype(F32)
    field[:, :LANES] = jnp.where(low, beside, swap_halves(middle)).astype(BF16)
    field[:, LANES : 2 * LANES] = right[...]
    field[:, 2 * LANES :] = jnp.where(low, swap_halves(beside), middle).astype(BF16)

    for phase, y_first, each, skip, rows, wide in phases((phase_rows, y_count)):
        lanes = (3 if wide else 2) * LANES
        here = slice(skip, skip + rows)
        mine_rows = slice(head - skip, head - skip + own_rows)
        if phase == count // 2:
            narrow_state(field, skip, rows)

        def two_slices(step, _):
            y = y_count - 1 - y_first - step
            for parity in reversed(range(CORES)):
                mine = core == parity
                other = jnp.logical_not(mine)
                pl.when(mine)(lambda: fill_layer(layer, own, halo, y, band, core))
                pl.when(other)(lambda: fill_layer(layer, o_own, o_halo, y, band, core))
                col_mat = col_mats[0 if wide else 1][...]
                spread = jnp.dot(field[here, :lanes], col_mat, preferred_element_type=F32)
                both = with_quarter_turn(parts_of(spread))
                back = parts_of(
                    jnp.dot(row_mats[phase][...], both, preferred_element_type=F32)
                )
                u = kept[CORES * y + parity].astype(F32)
                v = own_columns([part[mine_rows] for part in back], own_rows)
                u_turn, v_turn = swap_halves(u), swap_halves(v)
                phase_term = u * v_turn - u_turn * v
                term = jnp.where(low_own, phase_term, -(u * v + u_turn * v_turn)).astype(BF16)

                def put(out):
                    for index in range(out.shape[0]):
                        out[index, y] = term[index * band : (index + 1) * band]

                pl.when(mine)(lambda: put(terms))
                pl.when(other)(lambda: put(o_terms))
                t = layer_parts(layer, core, reach, skip, rows, wide)
                earlier = times(t, back, True)
                field[here, :lanes] = jnp.concatenate(earlier, axis=1).astype(BF16)
            return 0

        lax.fori_loop(0, each, two_slices, 0)


def collect_body(dims, offsets, terms, gradient):
    probes, tiles, y_count, lat_count, window, columns = dims
    band = terms.shape[1]
    lat = lax.axis_index("z") * GROUP + lax.axis_index("x")
    slots = {}
    for spot in range(y_count * GROUP):
        slots[tile_at(spot // y_count, spot % y_count, y_count, probes)] = spot
    low = low_lanes(band)
    rest = jnp.zeros((band, columns - window), F32)
    moved = []
    for probe in range(probes):
        parts = ([], [])
        for pair in range(tiles // 2):
            one = terms[slots[probe, 2 * pair]].astype(F32)
            two = terms[slots[probe, 2 * pair + 1]].astype(F32)
            parts[0].append(jnp.where(low, one, swap_halves(two)))
            parts[1].append(jnp.where(low, swap_halves(one), two))
        half = half_of(offsets, probe, band, lat, lat_count)
        for part in range(2):
            row = pltpu.roll(jnp.concatenate(parts[part] + [rest], axis=1), offsets[probe, 1], 1)
            moved.append((part, half, row))
    for part in range(2):
        for at in range(2):
            total = jnp.zeros((band, columns), F32)
            for which, half, row in moved:
                if which == part:
                    total = total + jnp.where(half == at, row, 0.0)
            gradient[part, at] = total


def local(potential, incident, measured, offsets, kernel):
    y_count = lax.axis_size("y")
    z_count = lax.axis_size("z")
    lat_count = z_count * GROUP
    band = potential.shape[3]
    columns = potential.shape[4]
    window = incident.shape[3]
    probes = incident.shape[1]
    half_width = (kernel.shape[1] - 1) // 2
    slices = y_count * CORES
    halo = slices * half_width
    tiles = y_count * GROUP // probes
    spots = y_count * GROUP
    reach = halo // band
    own_rows = GROUP // CORES * band
    phase_rows = tuple(own_rows + 2 * halo - at for at in range(0, 2 * halo, band))
    lanes = 3 * LANES
    taps = kernel.astype(F32).reshape(-1)
    core = lax.axis_index("core")

    def shape(*dims, dtype=BF16):
        return jax.ShapeDtypeStruct(dims, dtype)

    sent = call(
        functools.partial(prepare_body, (probes, tiles, halo, y_count, lat_count)),
        shape(spots, band + TAIL, lanes),
        [offsets],
        [potential[:, 0], incident, measured],
        (20_000_000, 3_000_000),
        [
            pltpu.VMEM((probes, 2, band, columns), F32),
            pltpu.VMEM((2, probes, TAIL, window), F32),
            pltpu.VMEM((probes, TAIL, window), F32),
            pltpu.SemaphoreType.DMA((probes + 2,)),
        ],
        outside=3,
        grant=WIDE_BYTES,
    )
    row_shapes = tuple(shape(rows, 2 * rows) for rows in phase_rows)
    col_shapes = (shape(lanes, lanes), shape(2 * LANES, 2 * LANES))
    matrices = call(
        functools.partial(
            matrices_body, (band, half_width, y_count, probes, lat_count, reach, phase_rows)
        ),
        row_shapes + row_shapes + col_shapes + col_shapes,
        [offsets, taps],
        [],
        (20_000_000, 1_500_000),
    )

    def spot_of(z, at_core):
        return at_core * z_count + z % z_count

    steps_z = range(z_count)
    same = [(spot_of(i, 0), spot_of(i + 1, 0)) for i in steps_z]
    same += [(spot_of(i + 1, 1), spot_of(i, 1)) for i in steps_z]
    cross = [(spot_of(i, 1), spot_of(i + 1, 0)) for i in steps_z]
    cross += [(spot_of(i + 1, 0), spot_of(i, 1)) for i in steps_z]

    def other_core(cells):
        return lax.ppermute(cells, "core", [(i, CORES - 1 - i) for i in range(CORES)])

    own = lax.all_to_all(sent, ("x", "y"), 0, 0, tiled=False)
    own = own.reshape(GROUP, y_count, band + TAIL, lanes)
    last_for_zero = lax.dynamic_slice_in_dim(own, (GROUP - reach) * (1 - core), reach, 0)
    last_for_one = lax.dynamic_slice_in_dim(own, (GROUP - reach) * core, reach, 0)
    edge = lax.ppermute(last_for_zero, ("core", "z"), same)
    o_edge = lax.ppermute(last_for_one, ("core", "z"), cross)
    o_own = other_core(own)
    edge, o_edge, o_own, *matrices = lax.optimization_barrier((edge, o_edge, o_own, *matrices))
    layers = (own, edge, o_own, o_edge)
    count = len(phase_rows)
    forward_mats = matrices[:count] + matrices[2 * count : 2 * count + 2]
    backward_mats = matrices[count : 2 * count] + matrices[2 * count + 2 :]

    flops = slices * phase_rows[1] * lanes * (4 * phase_rows[1] + 2 * lanes)
    kept, seed = call(
        functools.partial(forward_body, (band, phase_rows)),
        (shape(slices, own_rows, LANES), shape(own_rows, LANES)),
        [],
        [*forward_mats, *layers],
        (flops, 6_000_000),
        [
            pltpu.VMEM((phase_rows[0], lanes), F32),
            pltpu.VMEM(((GROUP + 2 * reach) * band, lanes), BF16),
            pltpu.VMEM((own_rows, LANES), F32),
            pltpu.VMEM(((GROUP + 2 * reach) * band, lanes), F32),
        ],
    )
    beyond = lax.ppermute(seed, ("core", "z"), cross)
    beside = other_core(seed)
    first_core = core == 0
    seeds = jnp.concatenate(
        [jnp.where(first_core, beyond, beside), seed, jnp.where(first_core, beside, beyond)],
        axis=0,
    )
    at = {}
    for y in range(y_count):
        for x in range(GROUP):
            at[tile_at(x, y, y_count, probes)] = y * GROUP + x
    right = [(at[p, c], at[p, c + 1]) for p in range(probes) for c in range(tiles - 1)]
    from_left = lax.ppermute(seeds, ("y", "x"), right)
    from_right = lax.ppermute(seeds, ("y", "x"), [(b, a) for a, b in right])
    terms, o_terms = call(
        functools.partial(backward_body, (band, phase_rows)),
        (
            shape(GROUP // CORES, y_count, band, LANES),
            shape(GROUP // CORES, y_count, band, LANES),
        ),
        [],
        [*backward_mats, *layers, kept, seeds, from_left, from_right],
        (flops, 6_000_000),
        [
            pltpu.VMEM((phase_rows[0], lanes), BF16),
            pltpu.VMEM(((GROUP + 2 * reach) * band, lanes), BF16),
        ],
    )
    o_terms = other_core(o_terms)
    terms = jnp.concatenate(
        [jnp.where(first_core, terms, o_terms), jnp.where(first_core, o_terms, terms)], axis=0
    )
    gathered = lax.all_to_all(
        terms.reshape(spots, band, LANES), ("x", "y"), 0, 0, tiled=False
    )
    gradient = call(
        functools.partial(collect_body, (probes, tiles, y_count, lat_count, window, columns)),
        shape(2, 2, band, columns, dtype=F32),
        [offsets],
        [gathered],
        (1_000_000, 2_000_000),
    )
    return gradient[:, None]


def solution(mesh):
    depth_count, lat_count = mesh.devices.shape
    grid = mesh.devices.reshape(depth_count // CORES, CORES, lat_count // GROUP, GROUP)
    fine = Mesh(grid, ("y", "core", "z", "x"))
    depth, lat = ("y", "core"), ("z", "x")
    in_specs = (
        P(None, depth, None, lat, None),
        P(None, None, lat, None),
        P(None, lat, None),
        P(),
        P(),
    )
    out_specs = P(None, depth, None, lat, None)
    return jax.shard_map(local, mesh=fine, in_specs=in_specs, out_specs=out_specs, check_vma=False)
```

time: 133 us -> 132 us (level)
  starting transfers between devices: 32 us -> 29.2 us
  waiting for transfers between devices: 10.2 us -> 12.7 us
  Pallas kernels: 31.2 us -> 29.1 us
    ppermute x4 -> x3, starting transfers between devices: 19.9 us -> 17.6 us  [the longest x1 11.2 us: local(): o_edge = lax.ppermute(last_for_one, ('core', 'z'), cross)]
    ppermute x4 -> x3, waiting for transfers between devices: 6.58 us -> 8.72 us  [the longest x1 5.24 us: local(): o_edge = lax.ppermute(last_for_one, ('core', 'z'), cross)]
    pallas_call x5, Pallas kernels: 31.2 us -> 29.1 us  [call(): pl.pallas_call(body, out_shape=outs, in_specs=in_specs, out_specs=jax.tre...]
    unnamed x12 -> x20, local copies, waits for them, and re-layouts: 3.91 us -> 3.31 us
  transfers between devices with their start and end apart: 9 -> 8, of which waited for: 4 -> 6; matrix products, arithmetic and copies ran while one was open for 0% -> 1% of each run, Pallas kernels for 1% -> 2%
where the time goes in v3:
time: 132 us
  blocking collectives  55.3 us (42%)
  starting transfers between devices  29.2 us (22%)
  Pallas kernels  29.1 us (22%)
  waiting for transfers between devices  12.7 us (10%)
  local copies, waits for them, and re-layouts  4.45 us (3%)
    all_to_all x1, blocking collectives, local(): own = lax.all_to_all(sent, ('x', 'y'), 0, 0, tiled=False)  37.4 us
    pallas_call x5, Pallas kernels, call(): pl.pallas_call(body, out_shape=outs, in_specs=in_specs, out_specs=jax.tre...  29.1 us
    all_to_all x1, blocking collectives, local(): lax.all_to_all(terms.reshape(spots, band, LANES), ('x', 'y'), 0, 0, tiled...  18 us
    ppermute x1, starting transfers between devices, local(): o_edge = lax.ppermute(last_for_one, ('core', 'z'), cross)  11.2 us
    ppermute x3, starting transfers between devices, other_core(): lax.ppermute(cells, 'core', [(i, CORES - 1 - i) for i in range(CORES)])  5.74 us
    ppermute x1, waiting for transfers between devices, local(): o_edge = lax.ppermute(last_for_one, ('core', 'z'), cross)  5.24 us
    ppermute x1, starting transfers between devices, local(): beyond = lax.ppermute(seed, ('core', 'z'), cross)  4.53 us
    ppermute x1, starting transfers between devices, local(): from_left = lax.ppermute(seeds, ('y', 'x'), right)  3.31 us
  transfers between devices with their start and end apart: 8, of which 6 were waited for; matrix products, arithmetic and copies ran while one was open for 1% of the time, Pallas kernels for 2%

profile of v3, /device:TPU:8, one launch (start us, length us, event | category | flops | bytes accessed | tf_op | source)
XLA Modules:
  0.0 131.8 jit_solution(5535430251497894374)
XLA Ops:
  0.0 4.8 %shard_map.55 = bf16[32,40,384]{2,1,0:T(8,128)(2,1)} custom-call(s32[2,2]{1,0:T(2,128)} %offsets.5, f32[2,2,32,2048]{3,2,1,0:T(8,128)} %bitcast.10, f32[2,2,32,1024]{3,2,1,0:T(8,128)} %incident.1, f32[2,32,1024]{2,1,0:T(8,128)} %measured.1), custom_call_target="tpu_custom_call" | custom-call | flops 20000000 | bytes 3000000 | tf_op jit(solution)/shard_map/pallas_call | solution.py:34
  4.8 37.4 %all_to_all.10 = bf16[32,40,384]{2,1,0:T(8,128)(2,1)S(1)} all-to-all(bf16[32,40,384]{2,1,0:T(8,128)(2,1)} %shard_map.55), channel_id=1, replica_groups=mesh['y'=8,'core'=2,'z'=8,'x'=4] {'x','y'}, dimensions={0} | all-to-all | bytes 1966080 | tf_op jit(solution)/shard_map/all_to_all | solution.py:506
  42.1 1.9 %collective-permute-start.2 = (bf16[4,8,40,384]{3,2,1,0:T(8,128)(2,1)S(1)}, bf16[4,8,40,384]{3,2,1,0:T(8,128)(2,1)S(1)}, u32[]{:S(2)}, u32[]{:S(2)}) collective-permute-start(bf16[4,8,40,384]{3,2,1,0:T(8,128)(2,1)S(1)} %bitcast.6), channel_id=1, source_target_pairs={{0,32},{32,0},{1,33},{33,1},{2,34},{34,2},{3,35},{35,3},{4,36},{36... | collective-permute-start | bytes 2949128 | tf_op jit(solution)/shard_map/ppermute | solution.py:504
  44.1 1.1 constant_dynamic-slice_fusion
  45.1 0.0 copy-start.9
  45.1 11.2 %collective-permute-start.1 = (bf16[2,8,40,384]{3,2,1,0:T(8,128)(2,1)}, bf16[2,8,40,384]{3,2,1,0:T(8,128)(2,1)S(1)}, u32[]{:S(2)}, u32[]{:S(2)}) collective-permute-start(bf16[2,8,40,384]{3,2,1,0:T(8,128)(2,1)} %get-tuple-element.67), channel_id=1, source_target_pairs={{32,4},{36,8},{40,12},{44,16},{48,20},{52,24},{56,28},{60,0},{4,32... | collective-permute-start | bytes 1474568 | tf_op jit(solution)/shard_map/ppermute | solution.py:511
  56.3 0.0 copy-start
  56.3 1.9 %collective-permute-start = (bf16[2,8,40,384]{3,2,1,0:T(8,128)(2,1)}, bf16[2,8,40,384]{3,2,1,0:T(8,128)(2,1)S(1)}, u32[]{:S(2)}, u32[]{:S(2)}) collective-permute-start(bf16[2,8,40,384]{3,2,1,0:T(8,128)(2,1)} %get-tuple-element.68), channel_id=1, source_target_pairs={{0,4},{4,8},{8,12},{12,16},{16,20},{20,24},{24,28},{28,0},{36,32},... | collective-permute-start | bytes 1474568 | tf_op jit(solution)/shard_map/ppermute | solution.py:510
  58.2 0.0 copy-done.9
  58.2 0.1 reshape.16.taps
  58.3 0.0 copy-done
  58.3 3.2 %shard_map.56 = (bf16[192,384]{1,0:T(8,128)(2,1)S(1)}, bf16[160,320]{1,0:T(8,128)(2,1)S(1)}, bf16[128,256]{1,0:T(8,128)(2,1)S(1)}, bf16[96,192]{1,0:T(8,128)(2,1...) custom-call(s32[2,2]{1,0:T(2,128)S(1)} %copy-done, ...), custom_call_target="tpu_custom_call" | custom-call | flops 20000000 | bytes 1500000 | tf_op jit(solution)/shard_map/pallas_call | solution.py:34
  61.5 0.0 copy-start.1
  61.5 0.0 copy-start.3
  61.5 0.0 copy-start.5
  61.5 5.2 %collective-permute-done.1.refs_9_ = bf16[2,8,40,384]{3,2,1,0:T(8,128)(2,1)S(1)} collective-permute-done((bf16[2,8,40,384]{3,2,1,0:T(8,128)(2,1)}, bf16[2,8,40,384]{3,2,1,0:T(8,128)(2,1)S(1)}, u32[]{:S(2)}, u32[]{:S(2)}) %collective-permute-start.1) | collective-permute-done | bytes 491552 | tf_op jit(solution)/shard_map/ppermute | solution.py:511
  66.8 1.7 %collective-permute-done.refs_7_ = bf16[2,8,40,384]{3,2,1,0:T(8,128)(2,1)S(1)} collective-permute-done((bf16[2,8,40,384]{3,2,1,0:T(8,128)(2,1)}, bf16[2,8,40,384]{3,2,1,0:T(8,128)(2,1)S(1)}, u32[]{:S(2)}, u32[]{:S(2)}) %collective-permute-start) | collective-permute-done | bytes 491552 | tf_op jit(solution)/shard_map/ppermute | solution.py:510
  68.4 0.0 collective-permute-done.2.refs_8_
  68.5 8.1 %shard_map.57 = (bf16[16,64,128]{2,1,0:T(8,128)(2,1)S(1)}, bf16[64,128]{1,0:T(8,128)(2,1)S(1)}) custom-call(bf16[192,384]{1,0:T(8,128)(2,1)S(1)} %get-tuple-element.57.refs_0_, bf16[160,320]{1,0:T(8,128)(2,1)S(1)} %get-tuple-element.58.refs_1_, bf16[128,256]{1,0:T(8,128)(2,1)S(1)} %get-tuple-element.59.refs_2_, ...), custom_call_target="tpu_custom_call" | custom-call | flops 1384120320 | bytes 6000000 | tf_op jit(solution)/shard_map/pallas_call | solution.py:34
  76.6 0.0 copy-done.1
  76.6 0.0 copy-done.3
  76.6 0.0 copy-done.5
  76.6 0.0 copy-start.7
  76.6 0.7 copy-done.7
  77.3 1.9 %collective-permute-start.4 = (bf16[64,128]{1,0:T(8,128)(2,1)S(1)}, bf16[64,128]{1,0:T(8,128)(2,1)}, u32[]{:S(2)}, u32[]{:S(2)}) collective-permute-start(bf16[64,128]{1,0:T(8,128)(2,1)S(1)} %get-tuple-element.64), channel_id=1, source_target_pairs={{0,32},{32,0},{1,33},{33,1},{2,34},{34,2},{3,35},{35,3},{4,36},{36... | collective-permute-start | bytes 49160 | tf_op jit(solution)/shard_map/ppermute | solution.py:504
  79.2 4.5 %collective-permute-start.3 = (bf16[64,128]{1,0:T(8,128)(2,1)S(1)}, bf16[64,128]{1,0:T(8,128)(2,1)}, u32[]{:S(2)}, u32[]{:S(2)}) collective-permute-start(bf16[64,128]{1,0:T(8,128)(2,1)S(1)} %get-tuple-element.64), channel_id=1, source_target_pairs={{32,4},{36,8},{40,12},{44,16},{48,20},{52,24},{56,28},{60,0},{4,32... | collective-permute-start | bytes 49160 | tf_op jit(solution)/shard_map/ppermute | solution.py:533
  83.8 0.0 copy-start.2
  83.8 0.0 collective-permute-done.4
  83.8 1.8 %collective-permute-done.3 = bf16[64,128]{1,0:T(8,128)(2,1)} collective-permute-done((bf16[64,128]{1,0:T(8,128)(2,1)S(1)}, bf16[64,128]{1,0:T(8,128)(2,1)}, u32[]{:S(2)}, u32[]{:S(2)}) %collective-permute-start.3) | collective-permute-done | bytes 16416 | tf_op jit(solution)/shard_map/ppermute | solution.py:533
  85.6 0.7 broadcast_select_fusion.3
  86.4 2.5 %collective-permute-start.6 = (bf16[192,128]{1,0:T(8,128)(2,1)S(1)}, bf16[192,128]{1,0:T(8,128)(2,1)S(1)}, u32[]{:S(2)}, u32[]{:S(2)}) collective-permute-start(bf16[192,128]{1,0:T(8,128)(2,1)S(1)} %pad_maximum_fusion.1.refs_11_), channel_id=1, source_target_pairs={{1,0},{2,1},{3,2},{67,3},{66,67},{65,66},{64,65},{128,64},{129,128... | collective-permute-start | bytes 147464 | tf_op jit(solution)/shard_map/ppermute | solution.py:546
  88.9 3.3 %collective-permute-start.5 = (bf16[192,128]{1,0:T(8,128)(2,1)S(1)}, bf16[192,128]{1,0:T(8,128)(2,1)S(1)}, u32[]{:S(2)}, u32[]{:S(2)}) collective-permute-start(bf16[192,128]{1,0:T(8,128)(2,1)S(1)} %pad_maximum_fusion.1.refs_11_), channel_id=1, source_target_pairs={{0,1},{1,2},{2,3},{3,67},{67,66},{66,65},{65,64},{64,128},{128,129... | collective-permute-start | bytes 147464 | tf_op jit(solution)/shard_map/ppermute | solution.py:545
  92.2 0.1 collective-permute-done.6.refs_13_
  92.4 2.5 %collective-permute-done.5.refs_12_ = bf16[192,128]{1,0:T(8,128)(2,1)S(1)} collective-permute-done((bf16[192,128]{1,0:T(8,128)(2,1)S(1)}, bf16[192,128]{1,0:T(8,128)(2,1)S(1)}, u32[]{:S(2)}, u32[]{:S(2)}) %collective-permute-start.5) | collective-permute-done | bytes 49184 | tf_op jit(solution)/shard_map/ppermute | solution.py:545
  94.9 0.0 copy-done.2
  94.9 0.0 copy-start.4
  94.9 0.8 copy-done.4
  95.7 0.0 copy-start.6
  95.7 0.8 copy-done.6
  96.5 0.0 copy-start.8
  96.5 0.9 copy-done.8
  97.5 11.0 %shard_map.58 = (bf16[2,8,32,128]{3,2,1,0:T(8,128)(2,1)S(1)}, bf16[2,8,32,128]{3,2,1,0:T(8,128)(2,1)S(1)}) custom-call(bf16[192,384]{1,0:T(8,128)(2,1)S(1)} %get-tuple-element.48.refs_0_, bf16[160,320]{1,0:T(8,128)(2,1)S(1)} %copy-done.2, bf16[128,256]{1,0:T(8,128)(2,1)S(1)} %copy-done.4, bf16[96,192]{1,0:T(8,128)(2,1)S(1)} %copy-done.6, ...), custom_call_target="tpu_custom_call" | custom-call | flops 1384120320 | bytes 6000000 | tf_op jit(solution)/shard_map/pallas_call | solution.py:34
  108.5 1.9 %collective-permute-start.7 = (bf16[2,8,32,128]{3,2,1,0:T(8,128)(2,1)S(1)}, bf16[2,8,32,128]{3,2,1,0:T(8,128)(2,1)S(1)}, u32[]{:S(2)}, u32[]{:S(2)}) collective-permute-start(bf16[2,8,32,128]{3,2,1,0:T(8,128)(2,1)S(1)} %get-tuple-element.66), channel_id=1, source_target_pairs={{0,32},{32,0},{1,33},{33,1},{2,34},{34,2},{3,35},{35,3},{4,36},{36... | collective-permute-start | bytes 393224 | tf_op jit(solution)/shard_map/ppermute | solution.py:504
  110.4 1.3 collective-permute-done.7
  111.8 18.0 %all_to_all.11.terms = bf16[32,32,128]{2,1,0:T(8,128)(2,1)S(1)} all-to-all(bf16[32,32,128]{2,1,0:T(8,128)(2,1)S(1)} %bitcast.11), channel_id=1, replica_groups=mesh['y'=8,'core'=2,'z'=8,'x'=4] {'x','y'}, dimensions={0} | all-to-all | bytes 524288 | tf_op jit(solution)/shard_map/all_to_all | solution.py:565
  129.8 2.0 %shard_map.59 = f32[2,2,32,2048]{3,2,1,0:T(8,128)} custom-call(s32[2,2]{1,0:T(2,128)S(1)} %copy-done, bf16[32,32,128]{2,1,0:T(8,128)(2,1)S(1)} %all_to_all.11.terms), custom_call_target="tpu_custom_call" | custom-call | flops 1000000 | bytes 2000000 | tf_op jit(solution)/shard_map/pallas_call | solution.py:34
  (3 shorter events, 0.1 us)
Async XLA Ops:
  42.1 26.3 %collective-permute-start.2 = (bf16[4,8,40,384]{3,2,1,0:T(8,128)(2,1)S(1)}, bf16[4,8,40,384]{3,2,1,0:T(8,128)(2,1)S(1)}, u32[]{:S(2)}, u32[]{:S(2)}) collective-permute-start(bf16[4,8,40,384]{3,2,1,0:T(8,128)(2,1)S(1)} %bitcast.6), channel_id=1, source_target_pairs={{0,32},{32,0},{1,33},{33,1},{2,34},{34,2},{3,35},{35,3},{4,36},{36... | collective-permute-start | bytes 2949128 | tf_op jit(solution)/shard_map/ppermute | solution.py:504
  45.1 13.1 %copy-start.9 = (bf16[2,9]{1,0:T(2,128)(2,1)S(1)}, bf16[2,9]{1,0:T(2,128)(2,1)}, u32[]{:S(2)}) copy-start(bf16[2,9]{1,0:T(2,128)(2,1)} %param.9) | copy-start | bytes 112
  45.1 21.7 %collective-permute-start.1 = (bf16[2,8,40,384]{3,2,1,0:T(8,128)(2,1)}, bf16[2,8,40,384]{3,2,1,0:T(8,128)(2,1)S(1)}, u32[]{:S(2)}, u32[]{:S(2)}) collective-permute-start(bf16[2,8,40,384]{3,2,1,0:T(8,128)(2,1)} %get-tuple-element.67), channel_id=1, source_target_pairs={{32,4},{36,8},{40,12},{44,16},{48,20},{52,24},{56,28},{60,0},{4,32... | collective-permute-start | bytes 1474568 | tf_op jit(solution)/shard_map/ppermute | solution.py:511
  56.3 2.0 %copy-start = (s32[2,2]{1,0:T(2,128)S(1)}, s32[2,2]{1,0:T(2,128)}, u32[]{:S(2)}) copy-start(s32[2,2]{1,0:T(2,128)} %offsets.5) | copy-start | bytes 52
  56.3 12.1 %collective-permute-start = (bf16[2,8,40,384]{3,2,1,0:T(8,128)(2,1)}, bf16[2,8,40,384]{3,2,1,0:T(8,128)(2,1)S(1)}, u32[]{:S(2)}, u32[]{:S(2)}) collective-permute-start(bf16[2,8,40,384]{3,2,1,0:T(8,128)(2,1)} %get-tuple-element.68), channel_id=1, source_target_pairs={{0,4},{4,8},{8,12},{12,16},{16,20},{20,24},{24,28},{28,0},{36,32},... | collective-permute-start | bytes 1474568 | tf_op jit(solution)/shard_map/ppermute | solution.py:510
  61.5 15.1 %copy-start.1 = (bf16[160,320]{1,0:T(8,128)(2,1)}, bf16[160,320]{1,0:T(8,128)(2,1)S(1)}, u32[]{:S(2)}) copy-start(bf16[160,320]{1,0:T(8,128)(2,1)S(1)} %get-tuple-element.49.refs_1_) | copy-start | bytes 307204
  61.5 15.1 %copy-start.3 = (bf16[128,256]{1,0:T(8,128)(2,1)}, bf16[128,256]{1,0:T(8,128)(2,1)S(1)}, u32[]{:S(2)}) copy-start(bf16[128,256]{1,0:T(8,128)(2,1)S(1)} %get-tuple-element.50.refs_2_) | copy-start | bytes 196612
  61.5 15.1 %copy-start.5 = (bf16[96,192]{1,0:T(8,128)(2,1)}, bf16[96,192]{1,0:T(8,128)(2,1)S(1)}, u32[]{:S(2)}) copy-start(bf16[96,192]{1,0:T(8,128)(2,1)S(1)} %get-tuple-element.51.refs_3_) | copy-start | bytes 110596
  76.6 0.7 copy-start.7
  77.3 6.5 %collective-permute-start.4 = (bf16[64,128]{1,0:T(8,128)(2,1)S(1)}, bf16[64,128]{1,0:T(8,128)(2,1)}, u32[]{:S(2)}, u32[]{:S(2)}) collective-permute-start(bf16[64,128]{1,0:T(8,128)(2,1)S(1)} %get-tuple-element.64), channel_id=1, source_target_pairs={{0,32},{32,0},{1,33},{33,1},{2,34},{34,2},{3,35},{35,3},{4,36},{36... | collective-permute-start | bytes 49160 | tf_op jit(solution)/shard_map/ppermute | solution.py:504
  79.2 6.4 %collective-permute-start.3 = (bf16[64,128]{1,0:T(8,128)(2,1)S(1)}, bf16[64,128]{1,0:T(8,128)(2,1)}, u32[]{:S(2)}, u32[]{:S(2)}) collective-permute-start(bf16[64,128]{1,0:T(8,128)(2,1)S(1)} %get-tuple-element.64), channel_id=1, source_target_pairs={{32,4},{36,8},{40,12},{44,16},{48,20},{52,24},{56,28},{60,0},{4,32... | collective-permute-start | bytes 49160 | tf_op jit(solution)/shard_map/ppermute | solution.py:533
  83.8 11.1 %copy-start.2 = (bf16[160,320]{1,0:T(8,128)(2,1)S(1)}, bf16[160,320]{1,0:T(8,128)(2,1)}, u32[]{:S(2)}) copy-start(bf16[160,320]{1,0:T(8,128)(2,1)} %copy-done.1) | copy-start | bytes 307204
  86.4 6.0 %collective-permute-start.6 = (bf16[192,128]{1,0:T(8,128)(2,1)S(1)}, bf16[192,128]{1,0:T(8,128)(2,1)S(1)}, u32[]{:S(2)}, u32[]{:S(2)}) collective-permute-start(bf16[192,128]{1,0:T(8,128)(2,1)S(1)} %pad_maximum_fusion.1.refs_11_), channel_id=1, source_target_pairs={{1,0},{2,1},{3,2},{67,3},{66,67},{65,66},{64,65},{128,64},{129,128... | collective-permute-start | bytes 147464 | tf_op jit(solution)/shard_map/ppermute | solution.py:546
  88.9 6.0 %collective-permute-start.5 = (bf16[192,128]{1,0:T(8,128)(2,1)S(1)}, bf16[192,128]{1,0:T(8,128)(2,1)S(1)}, u32[]{:S(2)}, u32[]{:S(2)}) collective-permute-start(bf16[192,128]{1,0:T(8,128)(2,1)S(1)} %pad_maximum_fusion.1.refs_11_), channel_id=1, source_target_pairs={{0,1},{1,2},{2,3},{3,67},{67,66},{66,65},{65,64},{64,128},{128,129... | collective-permute-start | bytes 147464 | tf_op jit(solution)/shard_map/ppermute | solution.py:545
  94.9 0.8 copy-start.4
  95.7 0.8 copy-start.6
  96.5 0.9 copy-start.8
  108.5 3.2 %collective-permute-start.7 = (bf16[2,8,32,128]{3,2,1,0:T(8,128)(2,1)S(1)}, bf16[2,8,32,128]{3,2,1,0:T(8,128)(2,1)S(1)}, u32[]{:S(2)}, u32[]{:S(2)}) collective-permute-start(bf16[2,8,32,128]{3,2,1,0:T(8,128)(2,1)S(1)} %get-tuple-element.66), channel_id=1, source_target_pairs={{0,32},{32,0},{1,33},{33,1},{2,34},{34,2},{3,35},{35,3},{4,36},{36... | collective-permute-start | bytes 393224 | tf_op jit(solution)/shard_map/ppermute | solution.py:504

commit v4 on v3

--- a/solution.py
+++ b/solution.py
@@ -77,6 +77,18 @@
             middle = jnp.where(low, real_on[:, there], imag[:, there])
             out.append((real_on[:, here], middle, imag_on[:, here]))
     return out
+
+
+def cos_sin(phase):
+    half = 0.5 * phase
+    square = half * half
+    sin, cos = 1.0 / 6227020800.0, 1.0 / 479001600.0
+    for term in (-39916800.0, 362880.0, -5040.0, 120.0, -6.0, 1.0):
+        sin = sin * square + 1.0 / term
+    for term in (-3628800.0, 40320.0, -720.0, 24.0, -2.0, 1.0):
+        cos = cos * square + 1.0 / term
+    sin = sin * half
+    return 1.0 - 2.0 * (sin * sin), 2.0 * (sin * cos)
 
 
 def prepare_body(
@@ -115,9 +127,8 @@
         phase = pltpu.roll(pot_buf[probe, 0], turn, 1)[:, :span]
         absorb = pltpu.roll(pot_buf[probe, 1], turn, 1)[:, :span]
         damping = jnp.where(inside, jnp.exp(-absorb), 0.0)
-        for tile, parts in enumerate(
-            packed(damping * jnp.cos(phase), damping * jnp.sin(phase), tiles)
-        ):
+        cos, sin = cos_sin(phase)
+        for tile, parts in enumerate(packed(damping * cos, damping * sin, tiles)):
             for at, part in enumerate(parts):
                 cols = slice(at * LANES, (at + 1) * LANES)
                 sent[slots[probe, tile], :band, cols] = part.astype(BF16)
@@ -164,7 +175,7 @@
     return real, imag
 
 
-def matrices_body(dims, offsets, taps, *outs):
+def matrices_body(dims, conj, offsets, taps, *outs):
     band, half_width, y_count, probes, lat_count, reach, phase_rows = dims
     own = lax.axis_index("y") // (y_count // probes)
     start = lax.axis_index("z") * GROUP + lax.axis_index("core") * (GROUP // CORES) - reach
@@ -185,36 +196,32 @@
         return jnp.where(index >= 2 * LANES, index - 2 * LANES, inner), imag
 
     count = len(phase_rows)
-    for at, rows in enumerate(phase_rows):
+    for out, rows in zip(outs[:count], phase_rows):
         diff = window_row(rows, 1) - window_row(rows, 0)
-        for conj in (False, True):
-            real, imag = banded(taps, diff, half_width, conj)
-            out = outs[at + count * conj]
-            out[...] = jnp.concatenate([real, imag], axis=1).astype(BF16)
-    for at in range(2):
-        lanes = outs[2 * count + at].shape[0]
-        in_col, in_imag = column(lanes, 0)
-        out_col, out_imag = column(lanes, 1)
-        for conj in (False, True):
-            real, imag = banded(taps, in_col - out_col, half_width, conj)
-            signed = jnp.where(in_imag, -imag, imag)
-            outs[2 * count + at + 2 * conj][...] = jnp.where(
-                in_imag == out_imag, real, signed
-            ).astype(BF16)
+        real, imag = banded(taps, diff, half_width, conj)
+        out[...] = jnp.concatenate([real, imag], axis=1).astype(BF16)
+    for out in outs[count:]:
+        in_col, in_imag = column(out.shape[0], 0)
+        out_col, out_imag = column(out.shape[0], 1)
+        real, imag = banded(taps, in_col - out_col, half_width, conj)
+        signed = jnp.where(in_imag, -imag, imag)
+        out[...] = jnp.where(in_imag == out_imag, real, signed).astype(BF16)
 
 
 def parts_of(cells):
     return tuple(cells[:, at : at + LANES] for at in range(0, cells.shape[1], LANES))
 
 
-def fill_layer(layer, own, halo, y, band, core):
-    reach = halo.shape[0] * band
-    for index in range(own.shape[0]):
-        layer[reach + index * band : reach + (index + 1) * band] = own[index, y, :band]
-    base = core * (reach + own.shape[0] * band)
-    for index in range(halo.shape[0]):
-        at = pl.multiple_of(base + index * band, band)
-        layer[pl.ds(at, band)] = halo[index, y, :band]
+def fill_layers(layers, sources, y, band, core):
+    for parity, (own, halo) in ((core, sources[:2]), (CORES - 1 - core, sources[2:])):
+        reach = halo.shape[0] * band
+        for index in range(own.shape[0]):
+            rows = slice(reach + index * band, reach + (index + 1) * band)
+            layers[CORES * y + parity, rows] = own[index, y, :band]
+        base = core * (reach + own.shape[0] * band)
+        for index in range(halo.shape[0]):
+            rows = pl.ds(pl.multiple_of(base + index * band, band), band)
+            layers[CORES * y + parity, rows] = halo[index, y, :band]
 
 
 def narrowed(wide):
@@ -278,9 +285,9 @@
     state[here, LANES : 2 * LANES] = imag.astype(state.dtype)
 
 
-def layer_parts(layer, core, reach, skip, rows, wide):
+def layer_parts(layers, index, core, reach, skip, rows, wide):
     at = pl.multiple_of(core * reach + skip, 16)
-    parts = parts_of(layer[pl.ds(at, rows)].astype(F32))
+    parts = parts_of(layers[index, pl.ds(at, rows)].astype(F32))
     return parts if wide else narrowed(parts)
 
 
@@ -288,7 +295,8 @@
     band, phase_rows = dims
     count = len(phase_rows)
     row_mats, col_mats = refs[:count], refs[count : count + 2]
-    own, halo, o_own, o_halo, kept, seed, psi, layer, goal, wave = refs[count + 2 :]
+    own, halo, o_own, o_halo, kept, seed, psi, layers, goal, wave = refs[count + 2 :]
+    sources = (own, halo, o_own, o_halo)
     core = lax.axis_index("core")
     strip = TAIL // 2
     total = phase_rows[0]
@@ -318,6 +326,7 @@
             at = index * band + pair * TAIL
             goal[at : at + TAIL] = both + swap_halves(both)
 
+    fill_layers(layers, sources, 0, band, core)
     for phase, y_first, each, skip, rows, wide in phases((phase_rows, y_count)):
         lanes = (3 if wide else 2) * LANES
         here = slice(skip, skip + rows)
@@ -327,13 +336,9 @@
 
         def two_slices(step, _):
             y = y_first + step
+            fill_layers(layers, sources, jnp.minimum(y + 1, y_count - 1), band, core)
             for parity in range(CORES):
-                mine = core == parity
-                pl.when(mine)(lambda: fill_layer(layer, own, halo, y, band, core))
-                pl.when(jnp.logical_not(mine))(
-                    lambda: fill_layer(layer, o_own, o_halo, y, band, core)
-                )
-                t = layer_parts(layer, core, reach, skip, rows, wide)
+                t = layer_parts(layers, CORES * y + parity, core, reach, skip, rows, wide)
                 product = times(t, parts_of(psi[here, :lanes]), False)
                 inner = [part[mine_rows] for part in product]
                 kept[CORES * y + parity] = own_columns(inner, own_rows).astype(BF16)
@@ -356,21 +361,25 @@
     band, phase_rows = dims
     count = len(phase_rows)
     row_mats, col_mats = refs[:count], refs[count : count + 2]
-    own, halo, o_own, o_halo, kept, seeds, left, right = refs[count + 2 : count + 10]
-    terms, o_terms, field, layer = refs[count + 10 :]
+    own, halo, o_own, o_halo, kept, seeds, beside, beyond = refs[count + 2 : count + 10]
+    terms, field, layers = refs[count + 10 :]
+    sources = (own, halo, o_own, o_halo)
     core = lax.axis_index("core")
     own_rows = own.shape[0] * band // CORES
     head = (phase_rows[0] - own_rows) // 2
     reach = halo.shape[0] * band
     y_count = own.shape[1]
-    low = low_lanes(phase_rows[0])
     low_own = low_lanes(own_rows)
-    middle = seeds[...].astype(F32)
-    beside = left[...].astype(F32)
-    field[:, :LANES] = jnp.where(low, beside, swap_halves(middle)).astype(BF16)
-    field[:, LANES : 2 * LANES] = right[...]
-    field[:, 2 * LANES :] = jnp.where(low, swap_halves(beside), middle).astype(BF16)
-
+    tail = phase_rows[0] - own_rows
+
+    for part, base in ((seeds, head), (beside, (1 - core) * tail), (beyond, core * tail)):
+        left, middle = part[0].astype(F32), part[1].astype(F32)
+        rows = pl.ds(base if part is seeds else pl.multiple_of(base, band), own_rows)
+        field[rows, :LANES] = jnp.where(low_own, left, swap_halves(middle)).astype(BF16)
+        field[rows, LANES : 2 * LANES] = part[2]
+        field[rows, 2 * LANES :] = jnp.where(low_own, swap_halves(left), middle).astype(BF16)
+
+    fill_layers(layers, sources, y_count - 1, band, core)
     for phase, y_first, each, skip, rows, wide in phases((phase_rows, y_count)):
         lanes = (3 if wide else 2) * LANES
         here = slice(skip, skip + rows)
@@ -380,32 +389,25 @@
 
         def two_slices(step, _):
             y = y_count - 1 - y_first - step
+            fill_layers(layers, sources, jnp.maximum(y - 1, 0), band, core)
             for parity in reversed(range(CORES)):
-                mine = core == parity
-                other = jnp.logical_not(mine)
-                pl.when(mine)(lambda: fill_layer(layer, own, halo, y, band, core))
-                pl.when(other)(lambda: fill_layer(layer, o_own, o_halo, y, band, core))
                 col_mat = col_mats[0 if wide else 1][...]
                 spread = jnp.dot(field[here, :lanes], col_mat, preferred_element_type=F32)
                 both = with_quarter_turn(parts_of(spread))
                 back = parts_of(
                     jnp.dot(row_mats[phase][...], both, preferred_element_type=F32)
                 )
+                t = layer_parts(layers, CORES * y + parity, core, reach, skip, rows, wide)
+                earlier = times(t, back, True)
+                field[here, :lanes] = jnp.concatenate(earlier, axis=1).astype(BF16)
                 u = kept[CORES * y + parity].astype(F32)
                 v = own_columns([part[mine_rows] for part in back], own_rows)
                 u_turn, v_turn = swap_halves(u), swap_halves(v)
                 phase_term = u * v_turn - u_turn * v
                 term = jnp.where(low_own, phase_term, -(u * v + u_turn * v_turn)).astype(BF16)
-
-                def put(out):
-                    for index in range(out.shape[0]):
-                        out[index, y] = term[index * band : (index + 1) * band]
-
-                pl.when(mine)(lambda: put(terms))
-                pl.when(other)(lambda: put(o_terms))
-                t = layer_parts(layer, core, reach, skip, rows, wide)
-                earlier = times(t, back, True)
-                field[here, :lanes] = jnp.concatenate(earlier, axis=1).astype(BF16)
+                owner = lax.rem(core + parity, CORES)
+                for index in range(terms.shape[1]):
+                    terms[owner, index, y] = term[index * band : (index + 1) * band]
             return 0
 
         lax.fori_loop(0, each, two_slices, 0)
@@ -479,17 +481,13 @@
         outside=3,
         grant=WIDE_BYTES,
     )
-    row_shapes = tuple(shape(rows, 2 * rows) for rows in phase_rows)
-    col_shapes = (shape(lanes, lanes), shape(2 * LANES, 2 * LANES))
-    matrices = call(
-        functools.partial(
-            matrices_body, (band, half_width, y_count, probes, lat_count, reach, phase_rows)
-        ),
-        row_shapes + row_shapes + col_shapes + col_shapes,
-        [offsets, taps],
-        [],
-        (20_000_000, 1_500_000),
-    )
+    mat_shapes = tuple(shape(rows, 2 * rows) for rows in phase_rows)
+    mat_shapes += (shape(lanes, lanes), shape(2 * LANES, 2 * LANES))
+    mat_dims = (band, half_width, y_count, probes, lat_count, reach, phase_rows)
+
+    def matrices(conj, taps):
+        body = functools.partial(matrices_body, mat_dims, conj)
+        return call(body, mat_shapes, [offsets, taps], [], (20_000_000, 700_000))
 
     def spot_of(z, at_core):
         return at_core * z_count + z % z_count
@@ -510,11 +508,10 @@
     edge = lax.ppermute(last_for_zero, ("core", "z"), same)
     o_edge = lax.ppermute(last_for_one, ("core", "z"), cross)
     o_own = other_core(own)
-    edge, o_edge, o_own, *matrices = lax.optimization_barrier((edge, o_edge, o_own, *matrices))
+    edge, o_edge, o_own, *forward_mats = lax.optimization_barrier(
+        (edge, o_edge, o_own, *matrices(False, taps))
+    )
     layers = (own, edge, o_own, o_edge)
-    count = len(phase_rows)
-    forward_mats = matrices[:count] + matrices[2 * count : 2 * count + 2]
-    backward_mats = matrices[count : 2 * count] + matrices[2 * count + 2 :]
 
     flops = slices * phase_rows[1] * lanes * (4 * phase_rows[1] + 2 * lanes)
     kept, seed = call(
@@ -525,42 +522,40 @@
         (flops, 6_000_000),
         [
             pltpu.VMEM((phase_rows[0], lanes), F32),
-            pltpu.VMEM(((GROUP + 2 * reach) * band, lanes), BF16),
+            pltpu.VMEM((slices, (GROUP + 2 * reach) * band, lanes), BF16),
             pltpu.VMEM((own_rows, LANES), F32),
             pltpu.VMEM(((GROUP + 2 * reach) * band, lanes), F32),
         ],
-    )
-    beyond = lax.ppermute(seed, ("core", "z"), cross)
-    beside = other_core(seed)
-    first_core = core == 0
-    seeds = jnp.concatenate(
-        [jnp.where(first_core, beyond, beside), seed, jnp.where(first_core, beside, beyond)],
-        axis=0,
     )
     at = {}
     for y in range(y_count):
         for x in range(GROUP):
             at[tile_at(x, y, y_count, probes)] = y * GROUP + x
     right = [(at[p, c], at[p, c + 1]) for p in range(probes) for c in range(tiles - 1)]
-    from_left = lax.ppermute(seeds, ("y", "x"), right)
-    from_right = lax.ppermute(seeds, ("y", "x"), [(b, a) for a, b in right])
-    terms, o_terms = call(
+    seed, late_taps = lax.optimization_barrier((seed, taps))
+    from_left = lax.ppermute(seed, ("y", "x"), right)
+    from_right = lax.ppermute(seed, ("y", "x"), [(b, a) for a, b in right])
+    from_left, from_right, *backward_mats = lax.optimization_barrier(
+        (from_left, from_right, *matrices(True, late_taps))
+    )
+    seeds = jnp.stack([from_left, seed, from_right])
+    beyond = lax.ppermute(seeds, ("core", "z"), cross)
+    beside = other_core(seeds)
+    terms = call(
         functools.partial(backward_body, (band, phase_rows)),
-        (
-            shape(GROUP // CORES, y_count, band, LANES),
-            shape(GROUP // CORES, y_count, band, LANES),
-        ),
+        shape(CORES, GROUP // CORES, y_count, band, LANES),
         [],
-        [*backward_mats, *layers, kept, seeds, from_left, from_right],
+        [*backward_mats, *layers, kept, seeds, beside, beyond],
         (flops, 6_000_000),
         [
             pltpu.VMEM((phase_rows[0], lanes), BF16),
-            pltpu.VMEM(((GROUP + 2 * reach) * band, lanes), BF16),
+            pltpu.VMEM((slices, (GROUP + 2 * reach) * band, lanes), BF16),
         ],
     )
-    o_terms = other_core(o_terms)
+    mine, others = terms[0], other_core(terms[1])
+    first_core = core == 0
     terms = jnp.concatenate(
-        [jnp.where(first_core, terms, o_terms), jnp.where(first_core, o_terms, terms)], axis=0
+        [jnp.where(first_core, mine, others), jnp.where(first_core, others, mine)], axis=0
     )
     gathered = lax.all_to_all(
         terms.reshape(spots, band, LANES), ("x", "y"), 0, 0, tiled=False

time: 132 us -> 121 us (0.917)
  Pallas kernels: 29.1 us -> 25.1 us
  local copies, waits for them, and re-layouts: 4.45 us -> 0.99 us
  waiting for transfers between devices: 12.7 us -> 10.8 us
    pallas_call x5 -> x6, Pallas kernels: 29.1 us -> 25.1 us  [call(): pl.pallas_call(body, out_shape=outs, in_specs=in_specs, out_specs=jax.tre...]
    ppermute x3, waiting for transfers between devices: 4.47 us -> 1.13 us  [the longest x1 0.75 us: local(): beyond = lax.ppermute(seeds, ('core', 'z'), cross)]
    unnamed x20 -> x4, local copies, waits for them, and re-layouts: 3.31 us -> 0.01 us
    ppermute x1, waiting for transfers between devices: 5.24 us -> 6.77 us  [local(): o_edge = lax.ppermute(last_for_one, ('core', 'z'), cross)]
  transfers between devices with their start and end apart: 8 -> 8, of which waited for: 6 -> 6; matrix products, arithmetic and copies ran while one was open for 1% -> 1% of each run, Pallas kernels for 2% -> 3%
where the time goes in v4:
time: 121 us
  blocking collectives  54.9 us (45%)
  starting transfers between devices  28.8 us (24%)
  Pallas kernels  25.1 us (21%)
  waiting for transfers between devices  10.8 us (9%)
    all_to_all x1, blocking collectives, local(): own = lax.all_to_all(sent, ('x', 'y'), 0, 0, tiled=False)  37.4 us
    pallas_call x6, Pallas kernels, call(): pl.pallas_call(body, out_shape=outs, in_specs=in_specs, out_specs=jax.tre...  25.1 us
    all_to_all x1, blocking collectives, local(): lax.all_to_all(terms.reshape(spots, band, LANES), ('x', 'y'), 0, 0, tiled...  17.5 us
    ppermute x1, starting transfers between devices, local(): o_edge = lax.ppermute(last_for_one, ('core', 'z'), cross)  11.2 us
    ppermute x1, waiting for transfers between devices, local(): o_edge = lax.ppermute(last_for_one, ('core', 'z'), cross)  6.77 us
    ppermute x3, starting transfers between devices, other_core(): lax.ppermute(cells, 'core', [(i, CORES - 1 - i) for i in range(CORES)])  5.9 us
    ppermute x1, starting transfers between devices, local(): beyond = lax.ppermute(seeds, ('core', 'z'), cross)  3.93 us
    ppermute x1, starting transfers between devices, local(): from_left = lax.ppermute(seed, ('y', 'x'), right)  3.32 us
  transfers between devices with their start and end apart: 8, of which 6 were waited for; matrix products, arithmetic and copies ran while one was open for 1% of the time, Pallas kernels for 3%

profile of v4, /device:TPU:8, one launch (start us, length us, event | category | flops | bytes accessed | tf_op | source)
XLA Modules:
  0.0 120.7 jit_solution(18008457910154167309)
XLA Ops:
  0.0 3.9 %shard_map.55 = bf16[32,40,384]{2,1,0:T(8,128)(2,1)} custom-call(s32[2,2]{1,0:T(2,128)} %offsets.7, f32[2,2,32,2048]{3,2,1,0:T(8,128)} %bitcast.22, f32[2,2,32,1024]{3,2,1,0:T(8,128)} %incident.1, f32[2,32,1024]{2,1,0:T(8,128)} %measured.1), custom_call_target="tpu_custom_call" | custom-call | flops 20000000 | bytes 3000000 | tf_op jit(solution)/shard_map/pallas_call | solution.py:34
  3.9 37.4 %all_to_all.10 = bf16[32,40,384]{2,1,0:T(8,128)(2,1)S(1)} all-to-all(bf16[32,40,384]{2,1,0:T(8,128)(2,1)} %shard_map.55), channel_id=1, replica_groups=mesh['y'=8,'core'=2,'z'=8,'x'=4] {'x','y'}, dimensions={0} | all-to-all | bytes 1966080 | tf_op jit(solution)/shard_map/all_to_all | solution.py:504
  41.3 1.9 %collective-permute-start.2 = (bf16[4,8,40,384]{3,2,1,0:T(8,128)(2,1)S(1)}, bf16[4,8,40,384]{3,2,1,0:T(8,128)(2,1)S(1)}, u32[]{:S(2)}, u32[]{:S(2)}) collective-permute-start(bf16[4,8,40,384]{3,2,1,0:T(8,128)(2,1)S(1)} %bitcast.17), channel_id=1, source_target_pairs={{0,32},{32,0},{1,33},{33,1},{2,34},{34,2},{3,35},{35,3},{4,36},{36... | collective-permute-start | bytes 2949128 | tf_op jit(solution)/shard_map/ppermute | solution.py:502
  43.2 0.9 constant_dynamic-slice_fusion
  44.1 0.0 copy-start.1
  44.1 11.2 %collective-permute-start.1 = (bf16[2,8,40,384]{3,2,1,0:T(8,128)(2,1)}, bf16[2,8,40,384]{3,2,1,0:T(8,128)(2,1)S(1)}, u32[]{:S(2)}, u32[]{:S(2)}) collective-permute-start(bf16[2,8,40,384]{3,2,1,0:T(8,128)(2,1)} %get-tuple-element.71), channel_id=1, source_target_pairs={{32,4},{36,8},{40,12},{44,16},{48,20},{52,24},{56,28},{60,0},{4,32... | collective-permute-start | bytes 1474568 | tf_op jit(solution)/shard_map/ppermute | solution.py:509
  55.3 0.0 copy-start
  55.3 1.9 %collective-permute-start = (bf16[2,8,40,384]{3,2,1,0:T(8,128)(2,1)S(1)}, bf16[2,8,40,384]{3,2,1,0:T(8,128)(2,1)S(1)}, u32[]{:S(2)}, u32[]{:S(2)}) collective-permute-start(bf16[2,8,40,384]{3,2,1,0:T(8,128)(2,1)S(1)} %get-tuple-element.72), channel_id=1, source_target_pairs={{0,4},{4,8},{8,12},{12,16},{16,20},{20,24},{24,28},{28,0},{36,32},... | collective-permute-start | bytes 1474568 | tf_op jit(solution)/shard_map/ppermute | solution.py:508
  57.2 0.0 copy-done.1
  57.2 0.1 reshape.16.taps
  57.3 0.0 copy-done
  57.3 1.9 %shard_map.56 = (bf16[192,384]{1,0:T(8,128)(2,1)S(1)}, bf16[160,320]{1,0:T(8,128)(2,1)S(1)}, bf16[128,256]{1,0:T(8,128)(2,1)S(1)}, bf16[96,192]{1,0:T(8,128)(2,1...) custom-call(s32[2,2]{1,0:T(2,128)S(1)} %copy-done, f32[18]{0:T(128)S(1)} %reshape.16.taps), custom_call_target="tpu_custom_call" | custom-call | flops 20000000 | bytes 700000 | tf_op jit(solution)/shard_map/pallas_call | solution.py:34
  59.2 6.8 %collective-permute-done.1.refs_9_ = bf16[2,8,40,384]{3,2,1,0:T(8,128)(2,1)S(1)} collective-permute-done((bf16[2,8,40,384]{3,2,1,0:T(8,128)(2,1)}, bf16[2,8,40,384]{3,2,1,0:T(8,128)(2,1)S(1)}, u32[]{:S(2)}, u32[]{:S(2)}) %collective-permute-start.1) | collective-permute-done | bytes 491552 | tf_op jit(solution)/shard_map/ppermute | solution.py:509
  66.0 1.2 %collective-permute-done.refs_7_ = bf16[2,8,40,384]{3,2,1,0:T(8,128)(2,1)S(1)} collective-permute-done((bf16[2,8,40,384]{3,2,1,0:T(8,128)(2,1)S(1)}, bf16[2,8,40,384]{3,2,1,0:T(8,128)(2,1)S(1)}, u32[]{:S(2)}, u32[]{:S(2)}) %collective-permute-start) | collective-permute-done | bytes 491552 | tf_op jit(solution)/shard_map/ppermute | solution.py:508
  67.2 0.0 collective-permute-done.2.refs_8_
  67.2 7.5 %shard_map.57 = (bf16[16,64,128]{2,1,0:T(8,128)(2,1)S(1)}, bf16[64,128]{1,0:T(8,128)(2,1)S(1)}) custom-call(bf16[192,384]{1,0:T(8,128)(2,1)S(1)} %get-tuple-element.44.refs_0_, bf16[160,320]{1,0:T(8,128)(2,1)S(1)} %get-tuple-element.45.refs_1_, bf16[128,256]{1,0:T(8,128)(2,1)S(1)} %get-tuple-element.46.refs_2_, ...), custom_call_target="tpu_custom_call" | custom-call | flops 1384120320 | bytes 6000000 | tf_op jit(solution)/shard_map/pallas_call | solution.py:34
  74.8 2.5 %collective-permute-start.4 = (bf16[64,128]{1,0:T(8,128)(2,1)S(1)}, bf16[64,128]{1,0:T(8,128)(2,1)S(1)}, u32[]{:S(2)}, u32[]{:S(2)}) collective-permute-start(bf16[64,128]{1,0:T(8,128)(2,1)S(1)} %get-tuple-element.54), channel_id=1, source_target_pairs={{1,0},{2,1},{3,2},{67,3},{66,67},{65,66},{64,65},{128,64},{129,128... | collective-permute-start | bytes 49160 | tf_op jit(solution)/shard_map/ppermute | solution.py:537
  77.3 3.3 %collective-permute-start.3 = (bf16[64,128]{1,0:T(8,128)(2,1)S(1)}, bf16[64,128]{1,0:T(8,128)(2,1)S(1)}, u32[]{:S(2)}, u32[]{:S(2)}) collective-permute-start(bf16[64,128]{1,0:T(8,128)(2,1)S(1)} %get-tuple-element.54), channel_id=1, source_target_pairs={{0,1},{1,2},{2,3},{3,67},{67,66},{66,65},{65,64},{64,128},{128,129... | collective-permute-start | bytes 49160 | tf_op jit(solution)/shard_map/ppermute | solution.py:536
  80.6 1.9 %shard_map.58 = (bf16[192,384]{1,0:T(8,128)(2,1)S(1)}, bf16[160,320]{1,0:T(8,128)(2,1)S(1)}, bf16[128,256]{1,0:T(8,128)(2,1)S(1)}, bf16[96,192]{1,0:T(8,128)(2,1...) custom-call(s32[2,2]{1,0:T(2,128)S(1)} %copy-done, f32[18]{0:T(128)S(1)} %reshape.16.taps), custom_call_target="tpu_custom_call" | custom-call | flops 20000000 | bytes 700000 | tf_op jit(solution)/shard_map/pallas_call | solution.py:34
  82.5 0.0 collective-permute-done.4
  82.6 0.4 collective-permute-done.3
  82.9 3.9 %collective-permute-start.6 = (bf16[3,64,128]{2,1,0:T(8,128)(2,1)S(1)}, bf16[3,64,128]{2,1,0:T(8,128)(2,1)S(1)}, u32[]{:S(2)}, u32[]{:S(2)}) collective-permute-start(bf16[3,64,128]{2,1,0:T(8,128)(2,1)S(1)} %pad_maximum_fusion.1.refs_11_), channel_id=1, source_target_pairs={{32,4},{36,8},{40,12},{44,16},{48,20},{52,24},{56,28},{60,0},{4,32... | collective-permute-start | bytes 147464 | tf_op jit(solution)/shard_map/ppermute | solution.py:542
  86.9 1.9 %collective-permute-start.5 = (bf16[3,64,128]{2,1,0:T(8,128)(2,1)S(1)}, bf16[3,64,128]{2,1,0:T(8,128)(2,1)S(1)}, u32[]{:S(2)}, u32[]{:S(2)}) collective-permute-start(bf16[3,64,128]{2,1,0:T(8,128)(2,1)S(1)} %pad_maximum_fusion.1.refs_11_), channel_id=1, source_target_pairs={{0,32},{32,0},{1,33},{33,1},{2,34},{34,2},{3,35},{35,3},{4,36},{36... | collective-permute-start | bytes 147464 | tf_op jit(solution)/shard_map/ppermute | solution.py:502
  88.8 0.8 collective-permute-done.6.refs_13_
  89.6 0.4 collective-permute-done.5.refs_12_
  90.0 7.8 %shard_map.59 = bf16[2,2,8,32,128]{4,3,2,1,0:T(8,128)(2,1)S(1)} custom-call(bf16[192,384]{1,0:T(8,128)(2,1)S(1)} %get-tuple-element.62.refs_0_, bf16[160,320]{1,0:T(8,128)(2,1)S(1)} %get-tuple-element.63.refs_1_, bf16[128,256]{1,0:T(8,128)(2,1)S(1)} %get-tuple-element.64.refs_2_, bf16[96,192]{1,0:T(8,128)(2,1)S(1)} %get-tuple-element.65.refs_3_, ...), custom_call_target="tpu_custom_call" | custom-call | flops 1384120320 | bytes 6000000 | tf_op jit(solution)/shard_map/pallas_call | solution.py:34
  97.9 2.1 %collective-permute-start.7 = (bf16[2,8,32,128]{3,2,1,0:T(8,128)(2,1)S(1)}, bf16[2,8,32,128]{3,2,1,0:T(8,128)(2,1)S(1)}, u32[]{:S(2)}, u32[]{:S(2)}) collective-permute-start(bf16[2,8,32,128]{3,2,1,0:T(8,128)(2,1)S(1)} %slice_bitcast_fusion), channel_id=1, source_target_pairs={{0,32},{32,0},{1,33},{33,1},{2,34},{34,2},{3,35},{35,3},{4,36},{36... | collective-permute-start | bytes 393224 | tf_op jit(solution)/shard_map/ppermute | solution.py:502
  99.9 1.2 collective-permute-done.7
  101.2 17.5 %all_to_all.11.terms = bf16[32,32,128]{2,1,0:T(8,128)(2,1)S(1)} all-to-all(bf16[32,32,128]{2,1,0:T(8,128)(2,1)S(1)} %bitcast.23), channel_id=1, replica_groups=mesh['y'=8,'core'=2,'z'=8,'x'=4] {'x','y'}, dimensions={0} | all-to-all | bytes 524288 | tf_op jit(solution)/shard_map/all_to_all | solution.py:560
  118.7 2.0 %shard_map.60 = f32[2,2,32,2048]{3,2,1,0:T(8,128)} custom-call(s32[2,2]{1,0:T(2,128)S(1)} %copy-done, bf16[32,32,128]{2,1,0:T(8,128)(2,1)S(1)} %all_to_all.11.terms), custom_call_target="tpu_custom_call" | custom-call | flops 1000000 | bytes 2000000 | tf_op jit(solution)/shard_map/pallas_call | solution.py:34
  (4 shorter events, 0.1 us)
Async XLA Ops:
  41.3 26.0 %collective-permute-start.2 = (bf16[4,8,40,384]{3,2,1,0:T(8,128)(2,1)S(1)}, bf16[4,8,40,384]{3,2,1,0:T(8,128)(2,1)S(1)}, u32[]{:S(2)}, u32[]{:S(2)}) collective-permute-start(bf16[4,8,40,384]{3,2,1,0:T(8,128)(2,1)S(1)} %bitcast.17), channel_id=1, source_target_pairs={{0,32},{32,0},{1,33},{33,1},{2,34},{34,2},{3,35},{35,3},{4,36},{36... | collective-permute-start | bytes 2949128 | tf_op jit(solution)/shard_map/ppermute | solution.py:502
  44.1 13.1 %copy-start.1 = (bf16[2,9]{1,0:T(2,128)(2,1)S(1)}, bf16[2,9]{1,0:T(2,128)(2,1)}, u32[]{:S(2)}) copy-start(bf16[2,9]{1,0:T(2,128)(2,1)} %param.9) | copy-start | bytes 112
  44.1 21.9 %collective-permute-start.1 = (bf16[2,8,40,384]{3,2,1,0:T(8,128)(2,1)}, bf16[2,8,40,384]{3,2,1,0:T(8,128)(2,1)S(1)}, u32[]{:S(2)}, u32[]{:S(2)}) collective-permute-start(bf16[2,8,40,384]{3,2,1,0:T(8,128)(2,1)} %get-tuple-element.71), channel_id=1, source_target_pairs={{32,4},{36,8},{40,12},{44,16},{48,20},{52,24},{56,28},{60,0},{4,32... | collective-permute-start | bytes 1474568 | tf_op jit(solution)/shard_map/ppermute | solution.py:509
  55.3 2.0 %copy-start = (s32[2,2]{1,0:T(2,128)S(1)}, s32[2,2]{1,0:T(2,128)}, u32[]{:S(2)}) copy-start(s32[2,2]{1,0:T(2,128)} %offsets.7) | copy-start | bytes 52
  55.3 12.0 %collective-permute-start = (bf16[2,8,40,384]{3,2,1,0:T(8,128)(2,1)S(1)}, bf16[2,8,40,384]{3,2,1,0:T(8,128)(2,1)S(1)}, u32[]{:S(2)}, u32[]{:S(2)}) collective-permute-start(bf16[2,8,40,384]{3,2,1,0:T(8,128)(2,1)S(1)} %get-tuple-element.72), channel_id=1, source_target_pairs={{0,4},{4,8},{8,12},{12,16},{16,20},{20,24},{24,28},{28,0},{36,32},... | collective-permute-start | bytes 1474568 | tf_op jit(solution)/shard_map/ppermute | solution.py:508
  74.8 7.8 %collective-permute-start.4 = (bf16[64,128]{1,0:T(8,128)(2,1)S(1)}, bf16[64,128]{1,0:T(8,128)(2,1)S(1)}, u32[]{:S(2)}, u32[]{:S(2)}) collective-permute-start(bf16[64,128]{1,0:T(8,128)(2,1)S(1)} %get-tuple-element.54), channel_id=1, source_target_pairs={{1,0},{2,1},{3,2},{67,3},{66,67},{65,66},{64,65},{128,64},{129,128... | collective-permute-start | bytes 49160 | tf_op jit(solution)/shard_map/ppermute | solution.py:537
  77.3 5.6 %collective-permute-start.3 = (bf16[64,128]{1,0:T(8,128)(2,1)S(1)}, bf16[64,128]{1,0:T(8,128)(2,1)S(1)}, u32[]{:S(2)}, u32[]{:S(2)}) collective-permute-start(bf16[64,128]{1,0:T(8,128)(2,1)S(1)} %get-tuple-element.54), channel_id=1, source_target_pairs={{0,1},{1,2},{2,3},{3,67},{67,66},{66,65},{65,64},{64,128},{128,129... | collective-permute-start | bytes 49160 | tf_op jit(solution)/shard_map/ppermute | solution.py:536
  82.9 6.6 %collective-permute-start.6 = (bf16[3,64,128]{2,1,0:T(8,128)(2,1)S(1)}, bf16[3,64,128]{2,1,0:T(8,128)(2,1)S(1)}, u32[]{:S(2)}, u32[]{:S(2)}) collective-permute-start(bf16[3,64,128]{2,1,0:T(8,128)(2,1)S(1)} %pad_maximum_fusion.1.refs_11_), channel_id=1, source_target_pairs={{32,4},{36,8},{40,12},{44,16},{48,20},{52,24},{56,28},{60,0},{4,32... | collective-permute-start | bytes 147464 | tf_op jit(solution)/shard_map/ppermute | solution.py:542
  86.9 3.1 %collective-permute-start.5 = (bf16[3,64,128]{2,1,0:T(8,128)(2,1)S(1)}, bf16[3,64,128]{2,1,0:T(8,128)(2,1)S(1)}, u32[]{:S(2)}, u32[]{:S(2)}) collective-permute-start(bf16[3,64,128]{2,1,0:T(8,128)(2,1)S(1)} %pad_maximum_fusion.1.refs_11_), channel_id=1, source_target_pairs={{0,32},{32,0},{1,33},{33,1},{2,34},{34,2},{3,35},{35,3},{4,36},{36... | collective-permute-start | bytes 147464 | tf_op jit(solution)/shard_map/ppermute | solution.py:502
  97.9 3.2 %collective-permute-start.7 = (bf16[2,8,32,128]{3,2,1,0:T(8,128)(2,1)S(1)}, bf16[2,8,32,128]{3,2,1,0:T(8,128)(2,1)S(1)}, u32[]{:S(2)}, u32[]{:S(2)}) collective-permute-start(bf16[2,8,32,128]{3,2,1,0:T(8,128)(2,1)S(1)} %slice_bitcast_fusion), channel_id=1, source_target_pairs={{0,32},{32,0},{1,33},{33,1},{2,34},{34,2},{3,35},{35,3},{4,36},{36... | collective-permute-start | bytes 393224 | tf_op jit(solution)/shard_map/ppermute | solution.py:502

commit v5 on v4

--- a/solution.py
+++ b/solution.py
@@ -15,6 +15,7 @@
 CORES = 2
 GROUP = 4
 TAIL = 8
+STRIP = 2
 VMEM_BYTES = 16 * 1024 * 1024
 WIDE_BYTES = 60 * 1024 * 1024
 
@@ -46,6 +47,15 @@
     rows = y_count // probes
     probe, row = y // rows, y % rows
     return probe, row * GROUP + (x if row % 2 == 0 else GROUP - 1 - x)
+
+
+def tile_slots(y_count, probes, core):
+    slots = {}
+    for x in range(GROUP):
+        base = lax.rem(x + core * (GROUP // CORES), GROUP) * y_count
+        for y in range(y_count):
+            slots[tile_at(x, y, y_count, probes)] = base + y
+    return slots
 
 
 def low_lanes(rows):
@@ -98,10 +108,10 @@
     band, columns = pot_buf.shape[2], pot_buf.shape[3]
     window = inc_buf.shape[3]
     span = window + 2 * halo
-    y = lax.axis_index("y")
+    y, core = lax.axis_index("y"), lax.axis_index("core")
     lat = lax.axis_index("z") * GROUP + lax.axis_index("x")
-    strip = TAIL // 2
-    first = pl.multiple_of(y // 2 * TAIL, TAIL)
+    row = (y * CORES + core) * STRIP
+    first = pl.multiple_of(row // TAIL * TAIL, TAIL)
     copies = []
     for probe in range(probes):
         half = half_of(offsets, probe, band, lat, lat_count)
@@ -116,9 +126,7 @@
     )
     for copy in copies:
         copy.start()
-    slots = {}
-    for spot in range(y_count * GROUP):
-        slots[tile_at(spot // y_count, spot % y_count, y_count, probes)] = spot
+    slots = tile_slots(y_count, probes, core)
     lane = lax.broadcasted_iota(jnp.int32, (band, span), 1)
     inside = (lane >= halo) & (lane < window + halo)
     for probe in range(probes):
@@ -130,22 +138,20 @@
         cos, sin = cos_sin(phase)
         for tile, parts in enumerate(packed(damping * cos, damping * sin, tiles)):
             for at, part in enumerate(parts):
-                cols = slice(at * LANES, (at + 1) * LANES)
-                sent[slots[probe, tile], :band, cols] = part.astype(BF16)
+                rows = slice(at * band, (at + 1) * band)
+                sent[slots[probe, tile], rows] = part.astype(BF16)
     copies[probes].wait()
     copies[probes + 1].wait()
-    odd = lax.rem(y, 2) == 1
+    lift = lax.rem(first + TAIL - row, TAIL)
     rest = jnp.zeros((TAIL, 2 * halo), F32)
-    upper = lax.broadcasted_iota(jnp.int32, (TAIL, LANES), 0) < strip
+    place = lax.broadcasted_iota(jnp.int32, (TAIL, LANES), 0) // STRIP
     low = low_lanes(TAIL)
     for probe in range(probes):
         wide = []
         for part in range(2):
-            rows = inc_buf[part, probe]
-            rows = jnp.where(odd, pltpu.roll(rows, strip, 0), rows)
+            rows = pltpu.roll(inc_buf[part, probe], lift, 0)
             wide.append(pltpu.roll(jnp.concatenate([rows, rest], axis=1), halo, 1))
-        rows = mea_buf[probe]
-        rows = jnp.where(odd, rows, pltpu.roll(rows, strip, 0))
+        rows = pltpu.roll(pltpu.roll(mea_buf[probe], lift, 0), 3 * STRIP, 0)
         coarse = rows.astype(BF16).astype(F32)
         fine = rows - coarse
         coarse_on = pltpu.roll(coarse, window - PIECE, 1)
@@ -153,13 +159,13 @@
         for tile, parts in enumerate(packed(wide[0], wide[1], tiles)):
             here = slice(tile // 2 * LANES, tile // 2 * LANES + LANES)
             if tile % 2 == 0:
-                both = jnp.where(low, coarse[:, here], fine_back[:, here])
+                cells = jnp.where(low, coarse[:, here], fine_back[:, here])
             else:
-                both = jnp.where(low, coarse_on[:, here], fine[:, here])
+                cells = jnp.where(low, coarse_on[:, here], fine[:, here])
             for at, part in enumerate(parts):
-                cols = slice(at * LANES, (at + 1) * LANES)
-                under = both if at == 0 else jnp.zeros_like(both)
-                sent[slots[probe, tile], band:, cols] = jnp.where(upper, part, under).astype(BF16)
+                moved = pltpu.roll(part, at * STRIP, 0) if at else part
+                cells = jnp.where(place == at, moved, cells)
+            sent[slots[probe, tile], 3 * band :] = cells.astype(BF16)
 
 
 def banded(taps, diff, half_width, conj):
@@ -212,16 +218,27 @@
     return tuple(cells[:, at : at + LANES] for at in range(0, cells.shape[1], LANES))
 
 
+def band_rows(own, halo, band, core, index, of_other):
+    reach = halo.shape[0] * band
+    if index >= own.shape[0]:
+        at = core * (reach + own.shape[0] * band) + (index - own.shape[0]) * band
+    else:
+        half = own.shape[0] // CORES
+        later = core if (index < half) != of_other else CORES - 1 - core
+        at = reach + (later * half + index % half) * band
+    return pl.multiple_of(at, band)
+
+
 def fill_layers(layers, sources, y, band, core):
-    for parity, (own, halo) in ((core, sources[:2]), (CORES - 1 - core, sources[2:])):
-        reach = halo.shape[0] * band
-        for index in range(own.shape[0]):
-            rows = slice(reach + index * band, reach + (index + 1) * band)
-            layers[CORES * y + parity, rows] = own[index, y, :band]
-        base = core * (reach + own.shape[0] * band)
-        for index in range(halo.shape[0]):
-            rows = pl.ds(pl.multiple_of(base + index * band, band), band)
-            layers[CORES * y + parity, rows] = halo[index, y, :band]
+    for of_other, (own, halo) in enumerate((sources[:2], sources[2:])):
+        parity = CORES - 1 - core if of_other else core
+        for index in range(own.shape[0] + halo.shape[0]):
+            rows = pl.ds(band_rows(own, halo, band, core, index, bool(of_other)), band)
+            inner = index - own.shape[0]
+            cells = own[index, y, : 3 * band] if inner < 0 else halo[inner, y, : 3 * band]
+            for at in range(3):
+                cols = slice(at * LANES, (at + 1) * LANES)
+                layers[CORES * y + parity, rows, cols] = cells[at * band : (at + 1) * band]
 
 
 def narrowed(wide):
@@ -298,33 +315,47 @@
     own, halo, o_own, o_halo, kept, seed, psi, layers, goal, wave = refs[count + 2 :]
     sources = (own, halo, o_own, o_halo)
     core = lax.axis_index("core")
-    strip = TAIL // 2
     total = phase_rows[0]
     own_rows = own.shape[0] * band // CORES
     head = (total - own_rows) // 2
     reach = halo.shape[0] * band
     y_count = own.shape[1]
-    upper = lax.broadcasted_iota(jnp.int32, (TAIL, 3 * LANES), 0) < strip
-
-    def tails(part, index, pair):
-        one = part[index, 2 * pair, band:].astype(F32)
-        two = part[index, 2 * pair + 1, band:].astype(F32)
-        return one, two
-
-    for part, base in ((own, reach), (halo, core * (reach + own.shape[0] * band))):
-        for index in range(part.shape[0]):
-            for pair in range(y_count // 2):
-                one, two = tails(part, index, pair)
-                at = base + index * band + pair * TAIL
-                at = at if part is own else pl.multiple_of(at, TAIL)
-                wave[pl.ds(at, TAIL)] = jnp.where(upper, one, pltpu.roll(two, strip, 0))
+    row = lax.broadcasted_iota(jnp.int32, (TAIL, LANES), 0)
+    upper = row < TAIL // 2
+    mine = lax.rem(row // STRIP, CORES) == core
+
+    def both_strips(cells, o_cells):
+        one = pltpu.roll(cells[3 * band :].astype(F32), STRIP * core, 0)
+        two = pltpu.roll(o_cells[3 * band :].astype(F32), STRIP * (CORES - 1 - core), 0)
+        return jnp.where(mine, one, two), jnp.where(mine, two, one)
+
+    bands = own.shape[0] + halo.shape[0]
+    for index in range(bands):
+        base = band_rows(own, halo, band, core, index, False)
+        for pair in range(y_count // 2):
+            strips = []
+            for y in (2 * pair, 2 * pair + 1):
+                if index < own.shape[0]:
+                    across = (index + own.shape[0] // CORES) % own.shape[0]
+                    strips.append(both_strips(own[index, y], o_own[across, y]))
+                else:
+                    inner = index - own.shape[0]
+                    strips.append(both_strips(halo[inner, y], o_halo[inner, y]))
+            (even, even_mid), (odd, odd_mid) = strips
+            rows = pl.ds(pl.multiple_of(base + pair * TAIL, TAIL), TAIL)
+            turn = TAIL // 2
+            wave[rows, :LANES] = jnp.where(upper, even, pltpu.roll(odd, turn, 0))
+            wave[rows, LANES : 2 * LANES] = jnp.where(
+                upper, pltpu.roll(even_mid, TAIL - STRIP, 0), pltpu.roll(odd_mid, STRIP, 0)
+            )
+            wave[rows, 2 * LANES :] = jnp.where(upper, pltpu.roll(even, turn, 0), odd)
+            if index < own.shape[0] // CORES:
+                both = jnp.where(
+                    upper, pltpu.roll(even_mid, STRIP, 0), pltpu.roll(odd_mid, TAIL - STRIP, 0)
+                )
+                at = index * band + pair * TAIL
+                goal[at : at + TAIL] = both + swap_halves(both)
     psi[...] = wave[pl.ds(pl.multiple_of(core * reach, band), total)]
-    for index in range(own.shape[0] // CORES):
-        for pair in range(y_count // 2):
-            one, two = tails(own, core * (own.shape[0] // CORES) + index, pair)
-            both = jnp.where(upper, pltpu.roll(one, strip, 0), two)[:, :LANES]
-            at = index * band + pair * TAIL
-            goal[at : at + TAIL] = both + swap_halves(both)
 
     fill_layers(layers, sources, 0, band, core)
     for phase, y_first, each, skip, rows, wide in phases((phase_rows, y_count)):
@@ -417,9 +448,7 @@
     probes, tiles, y_count, lat_count, window, columns = dims
     band = terms.shape[1]
     lat = lax.axis_index("z") * GROUP + lax.axis_index("x")
-    slots = {}
-    for spot in range(y_count * GROUP):
-        slots[tile_at(spot // y_count, spot % y_count, y_count, probes)] = spot
+    slots = tile_slots(y_count, probes, lax.axis_index("core"))
     low = low_lanes(band)
     rest = jnp.zeros((band, columns - window), F32)
     moved = []
@@ -468,7 +497,7 @@
 
     sent = call(
         functools.partial(prepare_body, (probes, tiles, halo, y_count, lat_count)),
-        shape(spots, band + TAIL, lanes),
+        shape(spots, 3 * band + TAIL, LANES),
         [offsets],
         [potential[:, 0], incident, measured],
         (20_000_000, 3_000_000),
@@ -501,15 +530,29 @@
     def other_core(cells):
         return lax.ppermute(cells, "core", [(i, CORES - 1 - i) for i in range(CORES)])
 
-    own = lax.all_to_all(sent, ("x", "y"), 0, 0, tiled=False)
-    own = own.reshape(GROUP, y_count, band + TAIL, lanes)
-    last_for_zero = lax.dynamic_slice_in_dim(own, (GROUP - reach) * (1 - core), reach, 0)
-    last_for_one = lax.dynamic_slice_in_dim(own, (GROUP - reach) * core, reach, 0)
-    edge = lax.ppermute(last_for_zero, ("core", "z"), same)
-    o_edge = lax.ppermute(last_for_one, ("core", "z"), cross)
-    o_own = other_core(own)
+    groups = []
+    for at_core in range(CORES):
+        for z in range(z_count):
+            order = [(x + at_core * (GROUP // CORES)) % GROUP for x in range(GROUP)]
+            groups.append(
+                [
+                    ((y * CORES + at_core) * z_count + z) * GROUP + x
+                    for x in order
+                    for y in range(y_count)
+                ]
+            )
+
+    def exchange(blocks):
+        axes = ("y", "core", "z", "x")
+        return lax.all_to_all(blocks, axes, 0, 0, axis_index_groups=groups, tiled=False)
+
+    own = exchange(sent).reshape(GROUP, y_count, 3 * band + TAIL, LANES)
+    edge = lax.ppermute(own[GROUP - reach :], ("core", "z"), same)
+    o_edge = lax.ppermute(own[:reach], ("core", "z"), cross)
+    swapped, *forward_mats = lax.optimization_barrier((own, *matrices(False, taps)))
+    o_own = other_core(swapped)
     edge, o_edge, o_own, *forward_mats = lax.optimization_barrier(
-        (edge, o_edge, o_own, *matrices(False, taps))
+        (edge, o_edge, o_own, *forward_mats)
     )
     layers = (own, edge, o_own, o_edge)
 
@@ -552,14 +595,8 @@
             pltpu.VMEM((slices, (GROUP + 2 * reach) * band, lanes), BF16),
         ],
     )
-    mine, others = terms[0], other_core(terms[1])
-    first_core = core == 0
-    terms = jnp.concatenate(
-        [jnp.where(first_core, mine, others), jnp.where(first_core, others, mine)], axis=0
-    )
-    gathered = lax.all_to_all(
-        terms.reshape(spots, band, LANES), ("x", "y"), 0, 0, tiled=False
-    )
+    terms = jnp.concatenate([terms[0], other_core(terms[1])], axis=0)
+    gathered = exchange(terms.reshape(spots, band, LANES))
     gradient = call(
         functools.partial(collect_body, (probes, tiles, y_count, lat_count, window, columns)),
         shape(2, 2, band, columns, dtype=F32),

time: 121 us -> 115 us (0.950)
  the two profiles are of different devices: /device:TPU:8 before, /device:TPU:1 now
where the time goes in v5:
time: 115 us
  starting transfers between devices  42.9 us (37%)
  waiting for transfers between devices  27.6 us (24%)
  Pallas kernels  25.3 us (22%)
  blocking collectives  18.1 us (16%)
    pallas_call x6, Pallas kernels, call(): pl.pallas_call(body, out_shape=outs, in_specs=in_specs, out_specs=jax.tre...  25.3 us
    all_to_all x1, blocking collectives, exchange(): lax.all_to_all(blocks, axes, 0, 0, axis_index_groups=groups, tiled=False)  18.1 us
    all_to_all x1, waiting for transfers between devices, exchange(): lax.all_to_all(blocks, axes, 0, 0, axis_index_groups=groups, tiled=False)  18 us
    ppermute x3, starting transfers between devices, other_core(): lax.ppermute(cells, 'core', [(i, CORES - 1 - i) for i in range(CORES)])  11.7 us
    all_to_all x1, starting transfers between devices, exchange(): lax.all_to_all(blocks, axes, 0, 0, axis_index_groups=groups, tiled=False)  11.2 us
    ppermute x1, starting transfers between devices, local(): edge = lax.ppermute(own[GROUP - reach:], ('core', 'z'), same)  10.7 us
    ppermute x1, waiting for transfers between devices, local(): edge = lax.ppermute(own[GROUP - reach:], ('core', 'z'), same)  4.86 us
    ppermute x1, starting transfers between devices, local(): from_left = lax.ppermute(seed, ('y', 'x'), right)  3.99 us
  transfers between devices with their start and end apart: 9, of which 5 were waited for; matrix products, arithmetic and copies ran while one was open for 0% of the time, Pallas kernels for 3%

profile of v5, /device:TPU:1, one launch (start us, length us, event | category | flops | bytes accessed | tf_op | source)
XLA Modules:
  0.0 115.0 jit_solution(9748085252392450328)
XLA Ops:
  0.0 3.8 %shard_map.55 = bf16[32,104,128]{2,1,0:T(8,128)(2,1)} custom-call(s32[2,2]{1,0:T(2,128)} %offsets.7, f32[2,2,32,2048]{3,2,1,0:T(8,128)} %bitcast.19, f32[2,2,32,1024]{3,2,1,0:T(8,128)} %incident.1, f32[2,32,1024]{2,1,0:T(8,128)} %measured.1), custom_call_target="tpu_custom_call" | custom-call | flops 20000000 | bytes 3000000 | tf_op jit(solution)/shard_map/pallas_call | solution.py:35
  3.8 0.0 copy-start.1
  3.8 11.2 %all-to-all-start = ((bf16[32,104,128]{2,1,0:T(8,128)(2,1)}), bf16[32,104,128]{2,1,0:T(8,128)(2,1)S(1)}, u32[]{:S(2)}, u32[]{:S(2)}) async-start(bf16[32,104,128]{2,1,0:T(8,128)(2,1)} %shard_map.55), calls=%async_computation | async-start | bytes 1703936 | tf_op jit(solution)/shard_map/all_to_all | solution.py:547
  15.0 0.0 copy-done.1
  15.1 0.0 copy-start
  15.1 0.1 reshape.18.taps
  15.2 0.6 copy-done
  15.7 1.9 %shard_map.56 = (bf16[192,384]{1,0:T(8,128)(2,1)S(1)}, bf16[160,320]{1,0:T(8,128)(2,1)S(1)}, bf16[128,256]{1,0:T(8,128)(2,1)S(1)}, bf16[96,192]{1,0:T(8,128)(2,1...) custom-call(s32[2,2]{1,0:T(2,128)S(1)} %copy-done, f32[18]{0:T(128)S(1)} %reshape.18.taps), custom_call_target="tpu_custom_call" | custom-call | flops 20000000 | bytes 700000 | tf_op jit(solution)/shard_map/pallas_call | solution.py:35
  17.7 18.0 %all-to-all-done = bf16[32,104,128]{2,1,0:T(8,128)(2,1)S(1)} async-done(((bf16[32,104,128]{2,1,0:T(8,128)(2,1)}), bf16[32,104,128]{2,1,0:T(8,128)(2,1)S(1)}, u32[]{:S(2)}, u32[]{:S(2)}) %all-to-all-start) | async-done | bytes 852000 | tf_op jit(solution)/shard_map/all_to_all | solution.py:547
  35.7 4.4 %collective-permute-start.2 = (bf16[4,8,104,128]{3,2,1,0:T(8,128)(2,1)S(1)}, bf16[4,8,104,128]{3,2,1,0:T(8,128)(2,1)S(1)}, u32[]{:S(2)}, u32[]{:S(2)}) collective-permute-start(bf16[4,8,104,128]{3,2,1,0:T(8,128)(2,1)S(1)} %bitcast.15), channel_id=1, source_target_pairs={{0,32},{32,0},{1,33},{33,1},{2,34},{34,2},{3,35},{35,3},{4,36},{36... | collective-permute-start | bytes 2555912 | tf_op jit(solution)/shard_map/ppermute | solution.py:531
  40.1 0.1 fusion
  40.1 10.7 %collective-permute-start = (bf16[2,8,104,128]{3,2,1,0:T(8,128)(2,1)S(1)}, bf16[2,8,104,128]{3,2,1,0:T(8,128)(2,1)S(1)}, u32[]{:S(2)}, u32[]{:S(2)}) collective-permute-start(bf16[2,8,104,128]{3,2,1,0:T(8,128)(2,1)S(1)} %bitcast.22), channel_id=1, source_target_pairs={{0,4},{4,8},{8,12},{12,16},{16,20},{20,24},{24,28},{28,0},{36,32},... | collective-permute-start | bytes 1277960 | tf_op jit(solution)/shard_map/ppermute | solution.py:550
  50.8 1.9 %collective-permute-start.1 = (bf16[2,8,104,128]{3,2,1,0:T(8,128)(2,1)S(1)}, bf16[2,8,104,128]{3,2,1,0:T(8,128)(2,1)S(1)}, u32[]{:S(2)}, u32[]{:S(2)}) collective-permute-start(bf16[2,8,104,128]{3,2,1,0:T(8,128)(2,1)S(1)} %bitcast.21), channel_id=1, source_target_pairs={{32,4},{36,8},{40,12},{44,16},{48,20},{52,24},{56,28},{60,0},{4,32... | collective-permute-start | bytes 1277960 | tf_op jit(solution)/shard_map/ppermute | solution.py:551
  52.8 4.9 %collective-permute-done.refs_7_ = bf16[2,8,104,128]{3,2,1,0:T(8,128)(2,1)S(1)} collective-permute-done((bf16[2,8,104,128]{3,2,1,0:T(8,128)(2,1)S(1)}, bf16[2,8,104,128]{3,2,1,0:T(8,128)(2,1)S(1)}, u32[]{:S(2)}, u32[]{:S(2)}) %collective-permute-start) | collective-permute-done | bytes 426016 | tf_op jit(solution)/shard_map/ppermute | solution.py:550
  57.6 3.0 %collective-permute-done.1.refs_9_ = bf16[2,8,104,128]{3,2,1,0:T(8,128)(2,1)S(1)} collective-permute-done((bf16[2,8,104,128]{3,2,1,0:T(8,128)(2,1)S(1)}, bf16[2,8,104,128]{3,2,1,0:T(8,128)(2,1)S(1)}, u32[]{:S(2)}, u32[]{:S(2)}) %collective-permute-start.1) | collective-permute-done | bytes 426016 | tf_op jit(solution)/shard_map/ppermute | solution.py:551
  60.6 0.0 collective-permute-done.2.refs_8_
  60.6 7.8 %shard_map.57 = (bf16[16,64,128]{2,1,0:T(8,128)(2,1)S(1)}, bf16[64,128]{1,0:T(8,128)(2,1)S(1)}) custom-call(bf16[192,384]{1,0:T(8,128)(2,1)S(1)} %get-tuple-element.58.refs_0_, bf16[160,320]{1,0:T(8,128)(2,1)S(1)} %get-tuple-element.59.refs_1_, bf16[128,256]{1,0:T(8,128)(2,1)S(1)} %get-tuple-element.60.refs_2_, ...), custom_call_target="tpu_custom_call" | custom-call | flops 1384120320 | bytes 6000000 | tf_op jit(solution)/shard_map/pallas_call | solution.py:35
  68.3 1.3 %collective-permute-start.4 = (bf16[64,128]{1,0:T(8,128)(2,1)S(1)}, bf16[64,128]{1,0:T(8,128)(2,1)S(1)}, u32[]{:S(2)}, u32[]{:S(2)}) collective-permute-start(bf16[64,128]{1,0:T(8,128)(2,1)S(1)} %get-tuple-element.68), channel_id=1, source_target_pairs={{1,0},{2,1},{3,2},{67,3},{66,67},{65,66},{64,65},{128,64},{129,128... | collective-permute-start | bytes 49160 | tf_op jit(solution)/shard_map/ppermute | solution.py:580
  69.6 4.0 %collective-permute-start.3 = (bf16[64,128]{1,0:T(8,128)(2,1)S(1)}, bf16[64,128]{1,0:T(8,128)(2,1)S(1)}, u32[]{:S(2)}, u32[]{:S(2)}) collective-permute-start(bf16[64,128]{1,0:T(8,128)(2,1)S(1)} %get-tuple-element.68), channel_id=1, source_target_pairs={{0,1},{1,2},{2,3},{3,67},{67,66},{66,65},{65,64},{64,128},{128,129... | collective-permute-start | bytes 49160 | tf_op jit(solution)/shard_map/ppermute | solution.py:579
  73.6 1.9 %shard_map.58 = (bf16[192,384]{1,0:T(8,128)(2,1)S(1)}, bf16[160,320]{1,0:T(8,128)(2,1)S(1)}, bf16[128,256]{1,0:T(8,128)(2,1)S(1)}, bf16[96,192]{1,0:T(8,128)(2,1...) custom-call(s32[2,2]{1,0:T(2,128)S(1)} %copy-done, f32[18]{0:T(128)S(1)} %reshape.18.taps), custom_call_target="tpu_custom_call" | custom-call | flops 20000000 | bytes 700000 | tf_op jit(solution)/shard_map/pallas_call | solution.py:35
  75.5 0.0 collective-permute-done.4
  75.6 0.0 collective-permute-done.3
  75.6 2.2 %collective-permute-start.6 = (bf16[3,64,128]{2,1,0:T(8,128)(2,1)S(1)}, bf16[3,64,128]{2,1,0:T(8,128)(2,1)S(1)}, u32[]{:S(2)}, u32[]{:S(2)}) collective-permute-start(bf16[3,64,128]{2,1,0:T(8,128)(2,1)S(1)} %pad_maximum_fusion.1.refs_11_), channel_id=1, source_target_pairs={{32,4},{36,8},{40,12},{44,16},{48,20},{52,24},{56,28},{60,0},{4,32... | collective-permute-start | bytes 147464 | tf_op jit(solution)/shard_map/ppermute | solution.py:585
  77.8 5.0 %collective-permute-start.5 = (bf16[3,64,128]{2,1,0:T(8,128)(2,1)S(1)}, bf16[3,64,128]{2,1,0:T(8,128)(2,1)S(1)}, u32[]{:S(2)}, u32[]{:S(2)}) collective-permute-start(bf16[3,64,128]{2,1,0:T(8,128)(2,1)S(1)} %pad_maximum_fusion.1.refs_11_), channel_id=1, source_target_pairs={{0,32},{32,0},{1,33},{33,1},{2,34},{34,2},{3,35},{35,3},{4,36},{36... | collective-permute-start | bytes 147464 | tf_op jit(solution)/shard_map/ppermute | solution.py:531
  82.8 0.0 collective-permute-done.6.refs_13_
  82.8 0.8 collective-permute-done.5.refs_12_
  83.7 7.9 %shard_map.59 = bf16[2,2,8,32,128]{4,3,2,1,0:T(8,128)(2,1)S(1)} custom-call(bf16[192,384]{1,0:T(8,128)(2,1)S(1)} %get-tuple-element.76.refs_0_, bf16[160,320]{1,0:T(8,128)(2,1)S(1)} %get-tuple-element.77.refs_1_, bf16[128,256]{1,0:T(8,128)(2,1)S(1)} %get-tuple-element.78.refs_2_, bf16[96,192]{1,0:T(8,128)(2,1)S(1)} %get-tuple-element.79.refs_3_, ...), custom_call_target="tpu_custom_call" | custom-call | flops 1384120320 | bytes 6000000 | tf_op jit(solution)/shard_map/pallas_call | solution.py:35
  91.6 2.3 %collective-permute-start.7 = (bf16[2,8,32,128]{3,2,1,0:T(8,128)(2,1)S(1)}, bf16[2,8,32,128]{3,2,1,0:T(8,128)(2,1)S(1)}, u32[]{:S(2)}, u32[]{:S(2)}) collective-permute-start(bf16[2,8,32,128]{3,2,1,0:T(8,128)(2,1)S(1)} %get-tuple-element.88), channel_id=1, source_target_pairs={{0,32},{32,0},{1,33},{33,1},{2,34},{34,2},{3,35},{35,3},{4,36},{36... | collective-permute-start | bytes 393224 | tf_op jit(solution)/shard_map/ppermute | solution.py:531
  93.9 1.0 collective-permute-done.7
  94.9 18.1 %all_to_all.10.terms = bf16[32,32,128]{2,1,0:T(8,128)(2,1)S(1)} all-to-all(bf16[32,32,128]{2,1,0:T(8,128)(2,1)S(1)} %bitcast.20), channel_id=1, replica_groups={{0,64,128,192,256,320,384,448,1,65,129,193,257,321,385,449,2,66,130,194..., dimensions={0} | all-to-all | bytes 524288 | tf_op jit(solution)/shard_map/all_to_all | solution.py:547
  112.9 2.0 %shard_map.60 = f32[2,2,32,2048]{3,2,1,0:T(8,128)} custom-call(s32[2,2]{1,0:T(2,128)S(1)} %copy-done, bf16[32,32,128]{2,1,0:T(8,128)(2,1)S(1)} %all_to_all.10.terms), custom_call_target="tpu_custom_call" | custom-call | flops 1000000 | bytes 2000000 | tf_op jit(solution)/shard_map/pallas_call | solution.py:35
  (3 shorter events, 0.1 us)
Async XLA Ops:
  3.8 11.2 %copy-start.1 = (bf16[2,9]{1,0:T(2,128)(2,1)S(1)}, bf16[2,9]{1,0:T(2,128)(2,1)}, u32[]{:S(2)}) copy-start(bf16[2,9]{1,0:T(2,128)(2,1)} %param.9) | copy-start | bytes 112
  3.8 31.8 %all-to-all-start = ((bf16[32,104,128]{2,1,0:T(8,128)(2,1)}), bf16[32,104,128]{2,1,0:T(8,128)(2,1)S(1)}, u32[]{:S(2)}, u32[]{:S(2)}) async-start(bf16[32,104,128]{2,1,0:T(8,128)(2,1)} %shard_map.55), calls=%async_computation | async-start | bytes 1703936 | tf_op jit(solution)/shard_map/all_to_all | solution.py:547
  15.1 0.7 copy-start
  35.7 24.9 %collective-permute-start.2 = (bf16[4,8,104,128]{3,2,1,0:T(8,128)(2,1)S(1)}, bf16[4,8,104,128]{3,2,1,0:T(8,128)(2,1)S(1)}, u32[]{:S(2)}, u32[]{:S(2)}) collective-permute-start(bf16[4,8,104,128]{3,2,1,0:T(8,128)(2,1)S(1)} %bitcast.15), channel_id=1, source_target_pairs={{0,32},{32,0},{1,33},{33,1},{2,34},{34,2},{3,35},{35,3},{4,36},{36... | collective-permute-start | bytes 2555912 | tf_op jit(solution)/shard_map/ppermute | solution.py:531
  40.1 17.5 %collective-permute-start = (bf16[2,8,104,128]{3,2,1,0:T(8,128)(2,1)S(1)}, bf16[2,8,104,128]{3,2,1,0:T(8,128)(2,1)S(1)}, u32[]{:S(2)}, u32[]{:S(2)}) collective-permute-start(bf16[2,8,104,128]{3,2,1,0:T(8,128)(2,1)S(1)} %bitcast.22), channel_id=1, source_target_pairs={{0,4},{4,8},{8,12},{12,16},{16,20},{20,24},{24,28},{28,0},{36,32},... | collective-permute-start | bytes 1277960 | tf_op jit(solution)/shard_map/ppermute | solution.py:550
  50.8 9.7 %collective-permute-start.1 = (bf16[2,8,104,128]{3,2,1,0:T(8,128)(2,1)S(1)}, bf16[2,8,104,128]{3,2,1,0:T(8,128)(2,1)S(1)}, u32[]{:S(2)}, u32[]{:S(2)}) collective-permute-start(bf16[2,8,104,128]{3,2,1,0:T(8,128)(2,1)S(1)} %bitcast.21), channel_id=1, source_target_pairs={{32,4},{36,8},{40,12},{44,16},{48,20},{52,24},{56,28},{60,0},{4,32... | collective-permute-start | bytes 1277960 | tf_op jit(solution)/shard_map/ppermute | solution.py:551
  68.3 7.2 %collective-permute-start.4 = (bf16[64,128]{1,0:T(8,128)(2,1)S(1)}, bf16[64,128]{1,0:T(8,128)(2,1)S(1)}, u32[]{:S(2)}, u32[]{:S(2)}) collective-permute-start(bf16[64,128]{1,0:T(8,128)(2,1)S(1)} %get-tuple-element.68), channel_id=1, source_target_pairs={{1,0},{2,1},{3,2},{67,3},{66,67},{65,66},{64,65},{128,64},{129,128... | collective-permute-start | bytes 49160 | tf_op jit(solution)/shard_map/ppermute | solution.py:580
  69.6 5.9 %collective-permute-start.3 = (bf16[64,128]{1,0:T(8,128)(2,1)S(1)}, bf16[64,128]{1,0:T(8,128)(2,1)S(1)}, u32[]{:S(2)}, u32[]{:S(2)}) collective-permute-start(bf16[64,128]{1,0:T(8,128)(2,1)S(1)} %get-tuple-element.68), channel_id=1, source_target_pairs={{0,1},{1,2},{2,3},{3,67},{67,66},{66,65},{65,64},{64,128},{128,129... | collective-permute-start | bytes 49160 | tf_op jit(solution)/shard_map/ppermute | solution.py:579
  75.6 7.2 %collective-permute-start.6 = (bf16[3,64,128]{2,1,0:T(8,128)(2,1)S(1)}, bf16[3,64,128]{2,1,0:T(8,128)(2,1)S(1)}, u32[]{:S(2)}, u32[]{:S(2)}) collective-permute-start(bf16[3,64,128]{2,1,0:T(8,128)(2,1)S(1)} %pad_maximum_fusion.1.refs_11_), channel_id=1, source_target_pairs={{32,4},{36,8},{40,12},{44,16},{48,20},{52,24},{56,28},{60,0},{4,32... | collective-permute-start | bytes 147464 | tf_op jit(solution)/shard_map/ppermute | solution.py:585
  77.8 5.9 %collective-permute-start.5 = (bf16[3,64,128]{2,1,0:T(8,128)(2,1)S(1)}, bf16[3,64,128]{2,1,0:T(8,128)(2,1)S(1)}, u32[]{:S(2)}, u32[]{:S(2)}) collective-permute-start(bf16[3,64,128]{2,1,0:T(8,128)(2,1)S(1)} %pad_maximum_fusion.1.refs_11_), channel_id=1, source_target_pairs={{0,32},{32,0},{1,33},{33,1},{2,34},{34,2},{3,35},{35,3},{4,36},{36... | collective-permute-start | bytes 147464 | tf_op jit(solution)/shard_map/ppermute | solution.py:531
  91.6 3.2 %collective-permute-start.7 = (bf16[2,8,32,128]{3,2,1,0:T(8,128)(2,1)S(1)}, bf16[2,8,32,128]{3,2,1,0:T(8,128)(2,1)S(1)}, u32[]{:S(2)}, u32[]{:S(2)}) collective-permute-start(bf16[2,8,32,128]{3,2,1,0:T(8,128)(2,1)S(1)} %get-tuple-element.88), channel_id=1, source_target_pairs={{0,32},{32,0},{1,33},{33,1},{2,34},{34,2},{3,35},{35,3},{4,36},{36... | collective-permute-start | bytes 393224 | tf_op jit(solution)/shard_map/ppermute | solution.py:531

commit v6 on v5

--- a/solution.py
+++ b/solution.py
@@ -195,11 +195,7 @@
 
     def column(lanes, axis):
         index = lax.broadcasted_iota(jnp.int32, (lanes, lanes), axis)
-        if lanes == 2 * LANES:
-            return jnp.where(index >= LANES, index - LANES, index), index >= LANES
-        imag = index >= LANES + PIECE
-        inner = jnp.where(imag, index - PIECE, index)
-        return jnp.where(index >= 2 * LANES, index - 2 * LANES, inner), imag
+        return jnp.where(index >= LANES, index - LANES, index), index >= LANES
 
     count = len(phase_rows)
     for out, rows in zip(outs[:count], phase_rows):
@@ -241,8 +237,24 @@
                 layers[CORES * y + parity, rows, cols] = cells[at * band : (at + 1) * band]
 
 
-def narrowed(wide):
-    first, middle, last = wide
+def two_tiles(packed_parts):
+    first, middle, last = packed_parts
+    low = low_lanes(first.shape[0])
+    real = jnp.where(low, swap_halves(first), swap_halves(middle))
+    return first, last, real, jnp.where(low, swap_halves(last), middle)
+
+
+def one_tile(parts):
+    low = low_lanes(parts[0].shape[0])
+    on, back = LANES - PIECE // 2, PIECE // 2
+    return tuple(
+        jnp.where(low, pltpu.roll(parts[at], on, 1), pltpu.roll(parts[at + 2], back, 1))
+        for at in range(2)
+    )
+
+
+def narrowed(packed_parts):
+    first, middle, last = packed_parts
     edge = lax.broadcasted_iota(jnp.int32, first.shape, 1) < LANES - PIECE // 2
     on, back = LANES - PIECE // 2, PIECE // 2
     real = jnp.where(edge, pltpu.roll(first, on, 1), pltpu.roll(middle, on, 1))
@@ -251,40 +263,43 @@
 
 
 def own_columns(parts, rows):
-    low = low_lanes(rows)
-    if len(parts) == 3:
-        return jnp.where(low, swap_halves(parts[0]), parts[2])
+    lane = lax.broadcasted_iota(jnp.int32, (rows, LANES), 1)
+    low = lane < PIECE
+    if len(parts) == 4:
+        real = jnp.where(lane < PIECE // 2, swap_halves(parts[0]), parts[2])
+        imag = jnp.where(lane < PIECE + PIECE // 2, parts[1], swap_halves(parts[3]))
+        return jnp.where(low, real, imag)
     real = pltpu.roll(parts[0], LANES - PIECE // 2, 1)
     return jnp.where(low, real, pltpu.roll(parts[1], PIECE // 2, 1))
 
 
 def times(t, field, conj):
     sign = -1.0 if conj else 1.0
-    if len(t) == 2:
-        return (
-            t[0] * field[0] - sign * (t[1] * field[1]),
-            t[0] * field[1] + sign * (t[1] * field[0]),
-        )
-    low = low_lanes(t[0].shape[0])
-    turned = swap_halves(t[1])
-    real = jnp.where(low, t[1], turned)
-    imag = jnp.where(low, -turned, t[1])
-    return (
-        t[0] * field[0] - sign * (t[2] * field[2]),
-        real * field[1] + sign * (imag * swap_halves(field[1])),
-        t[0] * field[2] + sign * (t[2] * field[0]),
-    )
-
-
-def with_quarter_turn(parts):
-    if len(parts) == 2:
-        crossed = (-parts[1], parts[0])
-    else:
-        low = low_lanes(parts[1].shape[0])
-        turned = swap_halves(parts[1])
-        crossed = (-parts[2], jnp.where(low, -turned, turned), parts[0])
+    out = []
+    for at in range(0, len(t), 2):
+        out.append(t[at] * field[at] - sign * (t[at + 1] * field[at + 1]))
+        out.append(t[at] * field[at + 1] + sign * (t[at + 1] * field[at]))
+    return tuple(out)
+
+
+def along_rows(matrix, parts):
+    crossed = []
+    for at in range(0, len(parts), 2):
+        crossed += [-parts[at + 1], parts[at]]
     both = [jnp.concatenate(rows, axis=1) for rows in (parts, crossed)]
-    return jnp.concatenate(both, axis=0).astype(BF16)
+    field = jnp.concatenate(both, axis=0).astype(BF16)
+    return parts_of(jnp.dot(matrix, field, preferred_element_type=F32))
+
+
+def along_cols(matrix, parts):
+    rows = parts[0].shape[0]
+    tiles = [jnp.concatenate(parts[at : at + 2], axis=1) for at in range(0, len(parts), 2)]
+    field = jnp.concatenate(tiles, axis=0).astype(BF16)
+    out = jnp.dot(field, matrix, preferred_element_type=F32)
+    result = ()
+    for at in range(len(tiles)):
+        result += parts_of(out[at * rows : (at + 1) * rows])
+    return result
 
 
 def phases(dims):
@@ -295,24 +310,17 @@
         yield at, at * each, each, skip, rows, at < len(phase_rows) // 2
 
 
-def narrow_state(state, skip, rows):
-    here = slice(skip, skip + rows)
-    real, imag = narrowed(parts_of(state[here].astype(F32)))
-    state[here, :LANES] = real.astype(state.dtype)
-    state[here, LANES : 2 * LANES] = imag.astype(state.dtype)
-
-
 def layer_parts(layers, index, core, reach, skip, rows, wide):
     at = pl.multiple_of(core * reach + skip, 16)
     parts = parts_of(layers[index, pl.ds(at, rows)].astype(F32))
-    return parts if wide else narrowed(parts)
+    return two_tiles(parts) if wide else narrowed(parts)
 
 
 def forward_body(dims, *refs):
     band, phase_rows = dims
     count = len(phase_rows)
-    row_mats, col_mats = refs[:count], refs[count : count + 2]
-    own, halo, o_own, o_halo, kept, seed, psi, layers, goal, wave = refs[count + 2 :]
+    row_mats, col_mat = refs[:count], refs[count]
+    own, halo, o_own, o_halo, kept, seed, layers, goal, wave = refs[count + 1 :]
     sources = (own, halo, o_own, o_halo)
     core = lax.axis_index("core")
     total = phase_rows[0]
@@ -355,34 +363,26 @@
                 )
                 at = index * band + pair * TAIL
                 goal[at : at + TAIL] = both + swap_halves(both)
-    psi[...] = wave[pl.ds(pl.multiple_of(core * reach, band), total)]
-
     fill_layers(layers, sources, 0, band, core)
+    psi = two_tiles(parts_of(wave[pl.ds(pl.multiple_of(core * reach, band), total)]))
+    done = 0
     for phase, y_first, each, skip, rows, wide in phases((phase_rows, y_count)):
-        lanes = (3 if wide else 2) * LANES
-        here = slice(skip, skip + rows)
         mine_rows = slice(head - skip, head - skip + own_rows)
+        psi = tuple(part[skip - done : skip - done + rows] for part in psi)
+        done = skip
         if phase == count // 2:
-            narrow_state(psi, skip, rows)
-
-        def two_slices(step, _):
-            y = y_first + step
-            fill_layers(layers, sources, jnp.minimum(y + 1, y_count - 1), band, core)
+            psi = one_tile(psi)
+        for y in range(y_first, y_first + each):
+            if y + 1 < y_count:
+                fill_layers(layers, sources, y + 1, band, core)
             for parity in range(CORES):
                 t = layer_parts(layers, CORES * y + parity, core, reach, skip, rows, wide)
-                product = times(t, parts_of(psi[here, :lanes]), False)
+                product = times(t, psi, False)
                 inner = [part[mine_rows] for part in product]
                 kept[CORES * y + parity] = own_columns(inner, own_rows).astype(BF16)
-                field = with_quarter_turn(product)
-                spread = jnp.dot(row_mats[phase][...], field, preferred_element_type=F32)
-                col_mat = col_mats[0 if wide else 1][...]
-                psi[here, :lanes] = jnp.dot(
-                    spread.astype(BF16), col_mat, preferred_element_type=F32
-                )
-            return 0
-
-        lax.fori_loop(0, each, two_slices, 0)
-    wave_out = own_columns(parts_of(psi[head : head + own_rows, : 2 * LANES]), own_rows)
+                spread = along_rows(row_mats[phase][...], product)
+                psi = along_cols(col_mat[...], spread)
+    wave_out = own_columns([part[head - done : head - done + own_rows] for part in psi], own_rows)
     square = wave_out * wave_out
     residual = square + swap_halves(square) - goal[...]
     seed[...] = (2.0 * residual * wave_out).astype(BF16)
@@ -391,9 +391,9 @@
 def backward_body(dims, *refs):
     band, phase_rows = dims
     count = len(phase_rows)
-    row_mats, col_mats = refs[:count], refs[count : count + 2]
-    own, halo, o_own, o_halo, kept, seeds, beside, beyond = refs[count + 2 : count + 10]
-    terms, field, layers = refs[count + 10 :]
+    row_mats, col_mat = refs[:count], refs[count]
+    own, halo, o_own, o_halo, kept, seeds, beside, beyond = refs[count + 1 : count + 9]
+    terms, field, layers = refs[count + 9 :]
     sources = (own, halo, o_own, o_halo)
     core = lax.axis_index("core")
     own_rows = own.shape[0] * band // CORES
@@ -411,26 +411,22 @@
         field[rows, 2 * LANES :] = jnp.where(low_own, swap_halves(left), middle).astype(BF16)
 
     fill_layers(layers, sources, y_count - 1, band, core)
+    state = two_tiles(parts_of(field[...].astype(F32)))
+    done = 0
     for phase, y_first, each, skip, rows, wide in phases((phase_rows, y_count)):
-        lanes = (3 if wide else 2) * LANES
-        here = slice(skip, skip + rows)
         mine_rows = slice(head - skip, head - skip + own_rows)
+        state = tuple(part[skip - done : skip - done + rows] for part in state)
+        done = skip
         if phase == count // 2:
-            narrow_state(field, skip, rows)
-
-        def two_slices(step, _):
-            y = y_count - 1 - y_first - step
-            fill_layers(layers, sources, jnp.maximum(y - 1, 0), band, core)
+            state = one_tile(state)
+        for y in reversed(range(y_count - y_first - each, y_count - y_first)):
+            if y > 0:
+                fill_layers(layers, sources, y - 1, band, core)
             for parity in reversed(range(CORES)):
-                col_mat = col_mats[0 if wide else 1][...]
-                spread = jnp.dot(field[here, :lanes], col_mat, preferred_element_type=F32)
-                both = with_quarter_turn(parts_of(spread))
-                back = parts_of(
-                    jnp.dot(row_mats[phase][...], both, preferred_element_type=F32)
-                )
+                spread = along_cols(col_mat[...], state)
+                back = along_rows(row_mats[phase][...], spread)
                 t = layer_parts(layers, CORES * y + parity, core, reach, skip, rows, wide)
-                earlier = times(t, back, True)
-                field[here, :lanes] = jnp.concatenate(earlier, axis=1).astype(BF16)
+                state = times(t, back, True)
                 u = kept[CORES * y + parity].astype(F32)
                 v = own_columns([part[mine_rows] for part in back], own_rows)
                 u_turn, v_turn = swap_halves(u), swap_halves(v)
@@ -439,9 +435,6 @@
                 owner = lax.rem(core + parity, CORES)
                 for index in range(terms.shape[1]):
                     terms[owner, index, y] = term[index * band : (index + 1) * band]
-            return 0
-
-        lax.fori_loop(0, each, two_slices, 0)
 
 
 def collect_body(dims, offsets, terms, gradient):
@@ -511,7 +504,7 @@
         grant=WIDE_BYTES,
     )
     mat_shapes = tuple(shape(rows, 2 * rows) for rows in phase_rows)
-    mat_shapes += (shape(lanes, lanes), shape(2 * LANES, 2 * LANES))
+    mat_shapes += (shape(2 * LANES, 2 * LANES),)
     mat_dims = (band, half_width, y_count, probes, lat_count, reach, phase_rows)
 
     def matrices(conj, taps):
@@ -549,10 +542,9 @@
     own = exchange(sent).reshape(GROUP, y_count, 3 * band + TAIL, LANES)
     edge = lax.ppermute(own[GROUP - reach :], ("core", "z"), same)
     o_edge = lax.ppermute(own[:reach], ("core", "z"), cross)
-    swapped, *forward_mats = lax.optimization_barrier((own, *matrices(False, taps)))
-    o_own = other_core(swapped)
-    edge, o_edge, o_own, *forward_mats = lax.optimization_barrier(
-        (edge, o_edge, o_own, *forward_mats)
+    o_own, tied_taps = lax.optimization_barrier((other_core(own), taps))
+    edge, o_edge, *forward_mats = lax.optimization_barrier(
+        (edge, o_edge, *matrices(False, tied_taps))
     )
     layers = (own, edge, o_own, o_edge)
 
@@ -564,7 +556,6 @@
         [*forward_mats, *layers],
         (flops, 6_000_000),
         [
-            pltpu.VMEM((phase_rows[0], lanes), F32),
             pltpu.VMEM((slices, (GROUP + 2 * reach) * band, lanes), BF16),
             pltpu.VMEM((own_rows, LANES), F32),
             pltpu.VMEM(((GROUP + 2 * reach) * band, lanes), F32),

time: 115 us -> 111 us (0.965)
  blocking collectives: 18.1 us -> 50.4 us
  waiting for transfers between devices: 27.6 us -> 8.2 us
  starting transfers between devices: 42.9 us -> 31.7 us
  Pallas kernels: 25.3 us -> 20 us
    all_to_all x1 -> x2, blocking collectives: 18.1 us -> 50.4 us  [exchange(): lax.all_to_all(blocks, axes, 0, 0, axis_index_groups=groups, tiled=False)]
    all_to_all x1 -> x0, waiting for transfers between devices: 18 us -> none  [exchange(): lax.all_to_all(blocks, axes, 0, 0, axis_index_groups=groups, tiled=False)]
    all_to_all x1 -> x0, starting transfers between devices: 11.2 us -> none  [exchange(): lax.all_to_all(blocks, axes, 0, 0, axis_index_groups=groups, tiled=False)]
    pallas_call x6, Pallas kernels: 25.3 us -> 20 us  [call(): pl.pallas_call(body, out_shape=outs, in_specs=in_specs, out_specs=jax.tre...]
    ppermute x1, waiting for transfers between devices: 4.86 us -> 3.36 us  [local(): edge = lax.ppermute(own[GROUP - reach:], ('core', 'z'), same)]
  transfers between devices with their start and end apart: 9 -> 8, of which waited for: 5 -> 4; matrix products, arithmetic and copies ran while one was open for 0% -> 0% of each run, Pallas kernels for 3% -> 2%
where the time goes in v6:
time: 111 us
  blocking collectives  50.4 us (45%)
  starting transfers between devices  31.7 us (29%)
  Pallas kernels  20 us (18%)
  waiting for transfers between devices  8.2 us (7%)
    all_to_all x2, blocking collectives, exchange(): lax.all_to_all(blocks, axes, 0, 0, axis_index_groups=groups, tiled=False)  50.4 us
    pallas_call x6, Pallas kernels, call(): pl.pallas_call(body, out_shape=outs, in_specs=in_specs, out_specs=jax.tre...  20 us
    ppermute x3, starting transfers between devices, other_core(): lax.ppermute(cells, 'core', [(i, CORES - 1 - i) for i in range(CORES)])  11.6 us
    ppermute x1, starting transfers between devices, local(): edge = lax.ppermute(own[GROUP - reach:], ('core', 'z'), same)  10.7 us
    ppermute x1, starting transfers between devices, local(): from_left = lax.ppermute(seed, ('y', 'x'), right)  3.99 us
    ppermute x1, waiting for transfers between devices, local(): edge = lax.ppermute(own[GROUP - reach:], ('core', 'z'), same)  3.36 us
    ppermute x1, waiting for transfers between devices, local(): o_edge = lax.ppermute(own[:reach], ('core', 'z'), cross)  3.01 us
    ppermute x1, starting transfers between devices, local(): beyond = lax.ppermute(seeds, ('core', 'z'), cross)  2.24 us
  transfers between devices with their start and end apart: 8, of which 4 were waited for; matrix products, arithmetic and copies ran while one was open for 0% of the time, Pallas kernels for 2%

profile of v6, /device:TPU:1, one launch (start us, length us, event | category | flops | bytes accessed | tf_op | source)
XLA Modules:
  0.0 110.7 jit_solution(5113947027706584820)
XLA Ops:
  0.0 3.8 %shard_map.55 = bf16[32,104,128]{2,1,0:T(8,128)(2,1)} custom-call(s32[2,2]{1,0:T(2,128)} %offsets.7, f32[2,2,32,2048]{3,2,1,0:T(8,128)} %bitcast.19, f32[2,2,32,1024]{3,2,1,0:T(8,128)} %incident.1, f32[2,32,1024]{2,1,0:T(8,128)} %measured.1), custom_call_target="tpu_custom_call" | custom-call | flops 20000000 | bytes 3000000 | tf_op jit(solution)/shard_map/pallas_call | solution.py:35
  3.8 31.8 %all_to_all.10 = bf16[32,104,128]{2,1,0:T(8,128)(2,1)S(1)} all-to-all(bf16[32,104,128]{2,1,0:T(8,128)(2,1)} %shard_map.55), channel_id=1, replica_groups={{0,64,128,192,256,320,384,448,1,65,129,193,257,321,385,449,2,66,130,194..., dimensions={0} | all-to-all | bytes 1703936 | tf_op jit(solution)/shard_map/all_to_all | solution.py:540
  35.6 4.4 %collective-permute-start.2 = (bf16[4,8,104,128]{3,2,1,0:T(8,128)(2,1)S(1)}, bf16[4,8,104,128]{3,2,1,0:T(8,128)(2,1)S(1)}, u32[]{:S(2)}, u32[]{:S(2)}) collective-permute-start(bf16[4,8,104,128]{3,2,1,0:T(8,128)(2,1)S(1)} %bitcast.15), channel_id=1, source_target_pairs={{0,32},{32,0},{1,33},{33,1},{2,34},{34,2},{3,35},{35,3},{4,36},{36... | collective-permute-start | bytes 2555912 | tf_op jit(solution)/shard_map/ppermute | solution.py:524
  40.1 0.1 fusion
  40.1 10.7 %collective-permute-start = (bf16[2,8,104,128]{3,2,1,0:T(8,128)(2,1)S(1)}, bf16[2,8,104,128]{3,2,1,0:T(8,128)(2,1)S(1)}, u32[]{:S(2)}, u32[]{:S(2)}) collective-permute-start(bf16[2,8,104,128]{3,2,1,0:T(8,128)(2,1)S(1)} %bitcast.22), channel_id=1, source_target_pairs={{0,4},{4,8},{8,12},{12,16},{16,20},{20,24},{24,28},{28,0},{36,32},... | collective-permute-start | bytes 1277960 | tf_op jit(solution)/shard_map/ppermute | solution.py:543
  50.8 0.0 copy-start.1
  50.8 0.0 copy-start
  50.8 1.9 %collective-permute-start.1 = (bf16[2,8,104,128]{3,2,1,0:T(8,128)(2,1)S(1)}, bf16[2,8,104,128]{3,2,1,0:T(8,128)(2,1)S(1)}, u32[]{:S(2)}, u32[]{:S(2)}) collective-permute-start(bf16[2,8,104,128]{3,2,1,0:T(8,128)(2,1)S(1)} %bitcast.21), channel_id=1, source_target_pairs={{32,4},{36,8},{40,12},{44,16},{48,20},{52,24},{56,28},{60,0},{4,32... | collective-permute-start | bytes 1277960 | tf_op jit(solution)/shard_map/ppermute | solution.py:544
  52.8 0.0 copy-done.1
  52.8 0.1 reshape.19.taps
  52.8 0.0 collective-permute-done.2.refs_7_
  52.9 0.0 copy-done
  52.9 1.3 %shard_map.56 = (bf16[192,384]{1,0:T(8,128)(2,1)S(1)}, bf16[160,320]{1,0:T(8,128)(2,1)S(1)}, bf16[128,256]{1,0:T(8,128)(2,1)S(1)}, bf16[96,192]{1,0:T(8,128)(2,1)S(1)}, bf16[256,256]{1,0:T(8,128)(2,1)S(1)}) custom-call(s32[2,2]{1,0:T(2,128)S(1)} %copy-done, f32[18]{0:T(128)S(1)} %reshape.19.taps), custom_call_target="tpu_custom_call" | custom-call | flops 20000000 | bytes 700000 | tf_op jit(solution)/shard_map/pallas_call | solution.py:35
  54.2 3.4 %collective-permute-done.refs_6_ = bf16[2,8,104,128]{3,2,1,0:T(8,128)(2,1)S(1)} collective-permute-done((bf16[2,8,104,128]{3,2,1,0:T(8,128)(2,1)S(1)}, bf16[2,8,104,128]{3,2,1,0:T(8,128)(2,1)S(1)}, u32[]{:S(2)}, u32[]{:S(2)}) %collective-permute-start) | collective-permute-done | bytes 426016 | tf_op jit(solution)/shard_map/ppermute | solution.py:543
  57.6 3.0 %collective-permute-done.1.refs_8_ = bf16[2,8,104,128]{3,2,1,0:T(8,128)(2,1)S(1)} collective-permute-done((bf16[2,8,104,128]{3,2,1,0:T(8,128)(2,1)S(1)}, bf16[2,8,104,128]{3,2,1,0:T(8,128)(2,1)S(1)}, u32[]{:S(2)}, u32[]{:S(2)}) %collective-permute-start.1) | collective-permute-done | bytes 426016 | tf_op jit(solution)/shard_map/ppermute | solution.py:544
  60.6 5.8 %shard_map.57 = (bf16[16,64,128]{2,1,0:T(8,128)(2,1)S(1)}, bf16[64,128]{1,0:T(8,128)(2,1)S(1)}) custom-call(bf16[192,384]{1,0:T(8,128)(2,1)S(1)} %get-tuple-element.41.refs_0_, bf16[160,320]{1,0:T(8,128)(2,1)S(1)} %get-tuple-element.42.refs_1_, bf16[128,256]{1,0:T(8,128)(2,1)S(1)} %get-tuple-element.43.refs_2_, ...), custom_call_target="tpu_custom_call" | custom-call | flops 1384120320 | bytes 6000000 | tf_op jit(solution)/shard_map/pallas_call | solution.py:35
  66.4 1.3 %collective-permute-start.4 = (bf16[64,128]{1,0:T(8,128)(2,1)S(1)}, bf16[64,128]{1,0:T(8,128)(2,1)S(1)}, u32[]{:S(2)}, u32[]{:S(2)}) collective-permute-start(bf16[64,128]{1,0:T(8,128)(2,1)S(1)} %get-tuple-element.50), channel_id=1, source_target_pairs={{1,0},{2,1},{3,2},{67,3},{66,67},{65,66},{64,65},{128,64},{129,128... | collective-permute-start | bytes 49160 | tf_op jit(solution)/shard_map/ppermute | solution.py:571
  67.7 4.0 %collective-permute-start.3 = (bf16[64,128]{1,0:T(8,128)(2,1)S(1)}, bf16[64,128]{1,0:T(8,128)(2,1)S(1)}, u32[]{:S(2)}, u32[]{:S(2)}) collective-permute-start(bf16[64,128]{1,0:T(8,128)(2,1)S(1)} %get-tuple-element.50), channel_id=1, source_target_pairs={{0,1},{1,2},{2,3},{3,67},{67,66},{66,65},{65,64},{64,128},{128,129... | collective-permute-start | bytes 49160 | tf_op jit(solution)/shard_map/ppermute | solution.py:570
  71.7 1.3 %shard_map.58 = (bf16[192,384]{1,0:T(8,128)(2,1)S(1)}, bf16[160,320]{1,0:T(8,128)(2,1)S(1)}, bf16[128,256]{1,0:T(8,128)(2,1)S(1)}, bf16[96,192]{1,0:T(8,128)(2,1)S(1)}, bf16[256,256]{1,0:T(8,128)(2,1)S(1)}) custom-call(s32[2,2]{1,0:T(2,128)S(1)} %copy-done, f32[18]{0:T(128)S(1)} %reshape.19.taps), custom_call_target="tpu_custom_call" | custom-call | flops 20000000 | bytes 700000 | tf_op jit(solution)/shard_map/pallas_call | solution.py:35
  73.0 0.0 collective-permute-done.4
  73.0 0.0 collective-permute-done.3
  73.1 2.2 %collective-permute-start.6 = (bf16[3,64,128]{2,1,0:T(8,128)(2,1)S(1)}, bf16[3,64,128]{2,1,0:T(8,128)(2,1)S(1)}, u32[]{:S(2)}, u32[]{:S(2)}) collective-permute-start(bf16[3,64,128]{2,1,0:T(8,128)(2,1)S(1)} %pad_maximum_fusion.1.refs_10_), channel_id=1, source_target_pairs={{32,4},{36,8},{40,12},{44,16},{48,20},{52,24},{56,28},{60,0},{4,32... | collective-permute-start | bytes 147464 | tf_op jit(solution)/shard_map/ppermute | solution.py:576
  75.3 4.9 %collective-permute-start.5 = (bf16[3,64,128]{2,1,0:T(8,128)(2,1)S(1)}, bf16[3,64,128]{2,1,0:T(8,128)(2,1)S(1)}, u32[]{:S(2)}, u32[]{:S(2)}) collective-permute-start(bf16[3,64,128]{2,1,0:T(8,128)(2,1)S(1)} %pad_maximum_fusion.1.refs_10_), channel_id=1, source_target_pairs={{0,32},{32,0},{1,33},{33,1},{2,34},{34,2},{3,35},{35,3},{4,36},{36... | collective-permute-start | bytes 147464 | tf_op jit(solution)/shard_map/ppermute | solution.py:524
  80.2 0.0 collective-permute-done.6.refs_12_
  80.3 0.8 collective-permute-done.5.refs_11_
  81.1 5.7 %shard_map.59 = bf16[2,2,8,32,128]{4,3,2,1,0:T(8,128)(2,1)S(1)} custom-call(bf16[192,384]{1,0:T(8,128)(2,1)S(1)} %get-tuple-element.57.refs_0_, bf16[160,320]{1,0:T(8,128)(2,1)S(1)} %get-tuple-element.58.refs_1_, bf16[128,256]{1,0:T(8,128)(2,1)S(1)} %get-tuple-element.59.refs_2_, bf16[96,192]{1,0:T(8,128)(2,1)S(1)} %get-tuple-element.60.refs_3_, ...), custom_call_target="tpu_custom_call" | custom-call | flops 1384120320 | bytes 6000000 | tf_op jit(solution)/shard_map/pallas_call | solution.py:35
  86.8 2.3 %collective-permute-start.7 = (bf16[2,8,32,128]{3,2,1,0:T(8,128)(2,1)S(1)}, bf16[2,8,32,128]{3,2,1,0:T(8,128)(2,1)S(1)}, u32[]{:S(2)}, u32[]{:S(2)}) collective-permute-start(bf16[2,8,32,128]{3,2,1,0:T(8,128)(2,1)S(1)} %get-tuple-element.68), channel_id=1, source_target_pairs={{0,32},{32,0},{1,33},{33,1},{2,34},{34,2},{3,35},{35,3},{4,36},{36... | collective-permute-start | bytes 393224 | tf_op jit(solution)/shard_map/ppermute | solution.py:524
  89.1 1.0 collective-permute-done.7
  90.1 18.6 %all_to_all.11.terms = bf16[32,32,128]{2,1,0:T(8,128)(2,1)S(1)} all-to-all(bf16[32,32,128]{2,1,0:T(8,128)(2,1)S(1)} %bitcast.20), channel_id=1, replica_groups={{0,64,128,192,256,320,384,448,1,65,129,193,257,321,385,449,2,66,130,194..., dimensions={0} | all-to-all | bytes 524288 | tf_op jit(solution)/shard_map/all_to_all | solution.py:540
  108.7 2.0 %shard_map.60 = f32[2,2,32,2048]{3,2,1,0:T(8,128)} custom-call(s32[2,2]{1,0:T(2,128)S(1)} %copy-done, bf16[32,32,128]{2,1,0:T(8,128)(2,1)S(1)} %all_to_all.11.terms), custom_call_target="tpu_custom_call" | custom-call | flops 1000000 | bytes 2000000 | tf_op jit(solution)/shard_map/pallas_call | solution.py:35
  (3 shorter events, 0.1 us)
Async XLA Ops:
  35.6 17.2 %collective-permute-start.2 = (bf16[4,8,104,128]{3,2,1,0:T(8,128)(2,1)S(1)}, bf16[4,8,104,128]{3,2,1,0:T(8,128)(2,1)S(1)}, u32[]{:S(2)}, u32[]{:S(2)}) collective-permute-start(bf16[4,8,104,128]{3,2,1,0:T(8,128)(2,1)S(1)} %bitcast.15), channel_id=1, source_target_pairs={{0,32},{32,0},{1,33},{33,1},{2,34},{34,2},{3,35},{35,3},{4,36},{36... | collective-permute-start | bytes 2555912 | tf_op jit(solution)/shard_map/ppermute | solution.py:524
  40.1 17.4 %collective-permute-start = (bf16[2,8,104,128]{3,2,1,0:T(8,128)(2,1)S(1)}, bf16[2,8,104,128]{3,2,1,0:T(8,128)(2,1)S(1)}, u32[]{:S(2)}, u32[]{:S(2)}) collective-permute-start(bf16[2,8,104,128]{3,2,1,0:T(8,128)(2,1)S(1)} %bitcast.22), channel_id=1, source_target_pairs={{0,4},{4,8},{8,12},{12,16},{16,20},{20,24},{24,28},{28,0},{36,32},... | collective-permute-start | bytes 1277960 | tf_op jit(solution)/shard_map/ppermute | solution.py:543
  50.8 2.0 %copy-start.1 = (bf16[2,9]{1,0:T(2,128)(2,1)S(1)}, bf16[2,9]{1,0:T(2,128)(2,1)}, u32[]{:S(2)}) copy-start(bf16[2,9]{1,0:T(2,128)(2,1)} %param.9) | copy-start | bytes 112
  50.8 2.0 %copy-start = (s32[2,2]{1,0:T(2,128)S(1)}, s32[2,2]{1,0:T(2,128)}, u32[]{:S(2)}) copy-start(s32[2,2]{1,0:T(2,128)} %offsets.7) | copy-start | bytes 52
  50.8 9.7 %collective-permute-start.1 = (bf16[2,8,104,128]{3,2,1,0:T(8,128)(2,1)S(1)}, bf16[2,8,104,128]{3,2,1,0:T(8,128)(2,1)S(1)}, u32[]{:S(2)}, u32[]{:S(2)}) collective-permute-start(bf16[2,8,104,128]{3,2,1,0:T(8,128)(2,1)S(1)} %bitcast.21), channel_id=1, source_target_pairs={{32,4},{36,8},{40,12},{44,16},{48,20},{52,24},{56,28},{60,0},{4,32... | collective-permute-start | bytes 1277960 | tf_op jit(solution)/shard_map/ppermute | solution.py:544
  66.4 6.6 %collective-permute-start.4 = (bf16[64,128]{1,0:T(8,128)(2,1)S(1)}, bf16[64,128]{1,0:T(8,128)(2,1)S(1)}, u32[]{:S(2)}, u32[]{:S(2)}) collective-permute-start(bf16[64,128]{1,0:T(8,128)(2,1)S(1)} %get-tuple-element.50), channel_id=1, source_target_pairs={{1,0},{2,1},{3,2},{67,3},{66,67},{65,66},{64,65},{128,64},{129,128... | collective-permute-start | bytes 49160 | tf_op jit(solution)/shard_map/ppermute | solution.py:571
  67.7 5.3 %collective-permute-start.3 = (bf16[64,128]{1,0:T(8,128)(2,1)S(1)}, bf16[64,128]{1,0:T(8,128)(2,1)S(1)}, u32[]{:S(2)}, u32[]{:S(2)}) collective-permute-start(bf16[64,128]{1,0:T(8,128)(2,1)S(1)} %get-tuple-element.50), channel_id=1, source_target_pairs={{0,1},{1,2},{2,3},{3,67},{67,66},{66,65},{65,64},{64,128},{128,129... | collective-permute-start | bytes 49160 | tf_op jit(solution)/shard_map/ppermute | solution.py:570
  73.1 7.2 %collective-permute-start.6 = (bf16[3,64,128]{2,1,0:T(8,128)(2,1)S(1)}, bf16[3,64,128]{2,1,0:T(8,128)(2,1)S(1)}, u32[]{:S(2)}, u32[]{:S(2)}) collective-permute-start(bf16[3,64,128]{2,1,0:T(8,128)(2,1)S(1)} %pad_maximum_fusion.1.refs_10_), channel_id=1, source_target_pairs={{32,4},{36,8},{40,12},{44,16},{48,20},{52,24},{56,28},{60,0},{4,32... | collective-permute-start | bytes 147464 | tf_op jit(solution)/shard_map/ppermute | solution.py:576
  75.3 5.8 %collective-permute-start.5 = (bf16[3,64,128]{2,1,0:T(8,128)(2,1)S(1)}, bf16[3,64,128]{2,1,0:T(8,128)(2,1)S(1)}, u32[]{:S(2)}, u32[]{:S(2)}) collective-permute-start(bf16[3,64,128]{2,1,0:T(8,128)(2,1)S(1)} %pad_maximum_fusion.1.refs_10_), channel_id=1, source_target_pairs={{0,32},{32,0},{1,33},{33,1},{2,34},{34,2},{3,35},{35,3},{4,36},{36... | collective-permute-start | bytes 147464 | tf_op jit(solution)/shard_map/ppermute | solution.py:524
  86.8 3.2 %collective-permute-start.7 = (bf16[2,8,32,128]{3,2,1,0:T(8,128)(2,1)S(1)}, bf16[2,8,32,128]{3,2,1,0:T(8,128)(2,1)S(1)}, u32[]{:S(2)}, u32[]{:S(2)}) collective-permute-start(bf16[2,8,32,128]{3,2,1,0:T(8,128)(2,1)S(1)} %get-tuple-element.68), channel_id=1, source_target_pairs={{0,32},{32,0},{1,33},{33,1},{2,34},{34,2},{3,35},{35,3},{4,36},{36... | collective-permute-start | bytes 393224 | tf_op jit(solution)/shard_map/ppermute | solution.py:524

commit v7 on v6

--- a/solution.py
+++ b/solution.py
@@ -105,19 +105,22 @@
     dims, offsets, potential, incident, measured, sent, pot_buf, inc_buf, mea_buf, sems
 ):
     probes, tiles, halo, y_count, lat_count = dims
-    band, columns = pot_buf.shape[2], pot_buf.shape[3]
+    band, columns = pot_buf.shape[2], potential.shape[3]
     window = inc_buf.shape[3]
     span = window + 2 * halo
     y, core = lax.axis_index("y"), lax.axis_index("core")
     lat = lax.axis_index("z") * GROUP + lax.axis_index("x")
     row = (y * CORES + core) * STRIP
     first = pl.multiple_of(row // TAIL * TAIL, TAIL)
+    def first_column(probe):
+        at = jnp.minimum(offsets[probe, 1] // LANES * LANES, columns - span)
+        return pl.multiple_of(at, LANES)
+
     copies = []
     for probe in range(probes):
         half = half_of(offsets, probe, band, lat, lat_count)
-        copies.append(
-            pltpu.make_async_copy(potential.at[:, half], pot_buf.at[probe], sems.at[probe])
-        )
+        cut = potential.at[:, half, :, pl.ds(first_column(probe), span)]
+        copies.append(pltpu.make_async_copy(cut, pot_buf.at[probe], sems.at[probe]))
     copies.append(
         pltpu.make_async_copy(incident.at[:, :, pl.ds(first, TAIL)], inc_buf, sems.at[probes])
     )
@@ -131,9 +134,9 @@
     inside = (lane >= halo) & (lane < window + halo)
     for probe in range(probes):
         copies[probe].wait()
-        turn = lax.rem(columns + halo - offsets[probe, 1], columns)
-        phase = pltpu.roll(pot_buf[probe, 0], turn, 1)[:, :span]
-        absorb = pltpu.roll(pot_buf[probe, 1], turn, 1)[:, :span]
+        turn = lax.rem(span + halo - (offsets[probe, 1] - first_column(probe)), span)
+        phase = pltpu.roll(pot_buf[probe, 0], turn, 1)
+        absorb = pltpu.roll(pot_buf[probe, 1], turn, 1)
         damping = jnp.where(inside, jnp.exp(-absorb), 0.0)
         cos, sin = cos_sin(phase)
         for tile, parts in enumerate(packed(damping * cos, damping * sin, tiles)):
@@ -187,10 +190,8 @@
     start = lax.axis_index("z") * GROUP + lax.axis_index("core") * (GROUP // CORES) - reach
     base = lax.rem(start - offsets[own, 0] // band + 2 * lat_count, lat_count)
 
-    def window_row(rows, axis):
-        skip = (phase_rows[0] - rows) // 2
-        index = lax.broadcasted_iota(jnp.int32, (rows, rows), axis) + skip
-        at = index + base * band
+    def window_row(shape, start, axis):
+        at = lax.broadcasted_iota(jnp.int32, shape, axis) + start + base * band
         return jnp.where(at >= lat_count * band, at - lat_count * band, at)
 
     def column(lanes, axis):
@@ -199,9 +200,12 @@
 
     count = len(phase_rows)
     for out, rows in zip(outs[:count], phase_rows):
-        diff = window_row(rows, 1) - window_row(rows, 0)
-        real, imag = banded(taps, diff, half_width, conj)
-        out[...] = jnp.concatenate([real, imag], axis=1).astype(BF16)
+        skip = (phase_rows[0] - rows) // 2
+        for block, (start, end, first, last) in enumerate(row_blocks(rows)):
+            size = (end - start, last - first)
+            diff = window_row(size, first + skip, 1) - window_row(size, start + skip, 0)
+            real, imag = banded(taps, diff, half_width, conj)
+            out[block] = jnp.concatenate([real, imag], axis=1).astype(BF16)
     for out in outs[count:]:
         in_col, in_imag = column(out.shape[0], 0)
         out_col, out_imag = column(out.shape[0], 1)
@@ -282,13 +286,24 @@
     return tuple(out)
 
 
-def along_rows(matrix, parts):
+def row_blocks(rows):
+    if rows <= LANES:
+        return [(0, rows, 0, rows)]
+    half, edge = rows // 2, 16
+    return [(0, half, 0, half + edge), (half, rows, half - edge, rows)]
+
+
+def along_rows(matrices, parts):
     crossed = []
     for at in range(0, len(parts), 2):
         crossed += [-parts[at + 1], parts[at]]
     both = [jnp.concatenate(rows, axis=1) for rows in (parts, crossed)]
-    field = jnp.concatenate(both, axis=0).astype(BF16)
-    return parts_of(jnp.dot(matrix, field, preferred_element_type=F32))
+    both = [cells.astype(BF16) for cells in both]
+    out = []
+    for block, (_, _, first, last) in enumerate(row_blocks(both[0].shape[0])):
+        field = jnp.concatenate([cells[first:last] for cells in both], axis=0)
+        out.append(jnp.dot(matrices[block], field, preferred_element_type=F32))
+    return parts_of(jnp.concatenate(out, axis=0))
 
 
 def along_cols(matrix, parts):
@@ -380,7 +395,7 @@
                 product = times(t, psi, False)
                 inner = [part[mine_rows] for part in product]
                 kept[CORES * y + parity] = own_columns(inner, own_rows).astype(BF16)
-                spread = along_rows(row_mats[phase][...], product)
+                spread = along_rows(row_mats[phase], product)
                 psi = along_cols(col_mat[...], spread)
     wave_out = own_columns([part[head - done : head - done + own_rows] for part in psi], own_rows)
     square = wave_out * wave_out
@@ -424,7 +439,7 @@
                 fill_layers(layers, sources, y - 1, band, core)
             for parity in reversed(range(CORES)):
                 spread = along_cols(col_mat[...], state)
-                back = along_rows(row_mats[phase][...], spread)
+                back = along_rows(row_mats[phase], spread)
                 t = layer_parts(layers, CORES * y + parity, core, reach, skip, rows, wide)
                 state = times(t, back, True)
                 u = kept[CORES * y + parity].astype(F32)
@@ -495,7 +510,7 @@
         [potential[:, 0], incident, measured],
         (20_000_000, 3_000_000),
         [
-            pltpu.VMEM((probes, 2, band, columns), F32),
+            pltpu.VMEM((probes, 2, band, window + 2 * halo), F32),
             pltpu.VMEM((2, probes, TAIL, window), F32),
             pltpu.VMEM((probes, TAIL, window), F32),
             pltpu.SemaphoreType.DMA((probes + 2,)),
@@ -503,7 +518,10 @@
         outside=3,
         grant=WIDE_BYTES,
     )
-    mat_shapes = tuple(shape(rows, 2 * rows) for rows in phase_rows)
+    mat_shapes = ()
+    for blocks in map(row_blocks, phase_rows):
+        start, end, first, last = blocks[0]
+        mat_shapes += (shape(len(blocks), end - start, 2 * (last - first)),)
     mat_shapes += (shape(2 * LANES, 2 * LANES),)
     mat_dims = (band, half_width, y_count, probes, lat_count, reach, phase_rows)
 

time: 111 us -> 111 us (level)
  no operation moved by 1% of the time
where the time goes in v7:
time: 111 us; the launch traced here: 110 us
  blocking collectives  50.4 us (45%)
  starting transfers between devices  31.9 us (29%)
  Pallas kernels  19.1 us (17%)
  waiting for transfers between devices  8.4 us (8%)
    all_to_all x2, blocking collectives, exchange(): lax.all_to_all(blocks, axes, 0, 0, axis_index_groups=groups, tiled=False)  50.4 us
    pallas_call x6, Pallas kernels, call(): pl.pallas_call(body, out_shape=outs, in_specs=in_specs, out_specs=jax.tre...  19.1 us
    ppermute x3, starting transfers between devices, other_core(): lax.ppermute(cells, 'core', [(i, CORES - 1 - i) for i in range(CORES)])  11.6 us
    ppermute x1, starting transfers between devices, local(): edge = lax.ppermute(own[GROUP - reach:], ('core', 'z'), same)  10.7 us
    ppermute x1, starting transfers between devices, local(): from_left = lax.ppermute(seed, ('y', 'x'), right)  3.99 us
    ppermute x1, waiting for transfers between devices, local(): edge = lax.ppermute(own[GROUP - reach:], ('core', 'z'), same)  3.57 us
    ppermute x1, waiting for transfers between devices, local(): o_edge = lax.ppermute(own[:reach], ('core', 'z'), cross)  3.01 us
    ppermute x1, starting transfers between devices, local(): beyond = lax.ppermute(seeds, ('core', 'z'), cross)  2.44 us
  transfers between devices with their start and end apart: 8, of which 4 were waited for; matrix products, arithmetic and copies ran while one was open for 0% of the time, Pallas kernels for 2%

profile of v7, /device:TPU:1, one launch (start us, length us, event | category | flops | bytes accessed | tf_op | source)
XLA Modules:
  0.0 110.2 jit_solution(5349009794572616443)
XLA Ops:
  0.0 3.7 %shard_map.55 = bf16[32,104,128]{2,1,0:T(8,128)(2,1)} custom-call(s32[2,2]{1,0:T(2,128)} %offsets.7, f32[2,2,32,2048]{3,2,1,0:T(8,128)} %bitcast.19, f32[2,2,32,1024]{3,2,1,0:T(8,128)} %incident.1, f32[2,32,1024]{2,1,0:T(8,128)} %measured.1), custom_call_target="tpu_custom_call" | custom-call | flops 20000000 | bytes 3000000 | tf_op jit(solution)/shard_map/pallas_call | solution.py:35
  3.7 31.8 %all_to_all.10 = bf16[32,104,128]{2,1,0:T(8,128)(2,1)S(1)} all-to-all(bf16[32,104,128]{2,1,0:T(8,128)(2,1)} %shard_map.55), channel_id=1, replica_groups={{0,64,128,192,256,320,384,448,1,65,129,193,257,321,385,449,2,66,130,194..., dimensions={0} | all-to-all | bytes 1703936 | tf_op jit(solution)/shard_map/all_to_all | solution.py:558
  35.5 4.4 %collective-permute-start.2 = (bf16[4,8,104,128]{3,2,1,0:T(8,128)(2,1)S(1)}, bf16[4,8,104,128]{3,2,1,0:T(8,128)(2,1)S(1)}, u32[]{:S(2)}, u32[]{:S(2)}) collective-permute-start(bf16[4,8,104,128]{3,2,1,0:T(8,128)(2,1)S(1)} %bitcast.15), channel_id=1, source_target_pairs={{0,32},{32,0},{1,33},{33,1},{2,34},{34,2},{3,35},{35,3},{4,36},{36... | collective-permute-start | bytes 2555912 | tf_op jit(solution)/shard_map/ppermute | solution.py:542
  39.9 0.1 fusion
  40.0 10.7 %collective-permute-start = (bf16[2,8,104,128]{3,2,1,0:T(8,128)(2,1)S(1)}, bf16[2,8,104,128]{3,2,1,0:T(8,128)(2,1)S(1)}, u32[]{:S(2)}, u32[]{:S(2)}) collective-permute-start(bf16[2,8,104,128]{3,2,1,0:T(8,128)(2,1)S(1)} %bitcast.22), channel_id=1, source_target_pairs={{0,4},{4,8},{8,12},{12,16},{16,20},{20,24},{24,28},{28,0},{36,32},... | collective-permute-start | bytes 1277960 | tf_op jit(solution)/shard_map/ppermute | solution.py:561
  50.7 0.0 copy-start.1
  50.7 0.0 copy-start
  50.7 1.9 %collective-permute-start.1 = (bf16[2,8,104,128]{3,2,1,0:T(8,128)(2,1)S(1)}, bf16[2,8,104,128]{3,2,1,0:T(8,128)(2,1)S(1)}, u32[]{:S(2)}, u32[]{:S(2)}) collective-permute-start(bf16[2,8,104,128]{3,2,1,0:T(8,128)(2,1)S(1)} %bitcast.21), channel_id=1, source_target_pairs={{32,4},{36,8},{40,12},{44,16},{48,20},{52,24},{56,28},{60,0},{4,32... | collective-permute-start | bytes 1277960 | tf_op jit(solution)/shard_map/ppermute | solution.py:562
  52.6 0.0 copy-done.1
  52.6 0.1 reshape.19.taps
  52.7 0.0 collective-permute-done.2.refs_7_
  52.7 0.0 copy-done
  52.7 1.1 %shard_map.56 = (bf16[2,96,224]{2,1,0:T(8,128)(2,1)S(1)}, bf16[2,80,192]{2,1,0:T(8,128)(2,1)S(1)}, bf16[1,128,256]{2,1,0:T(8,128)(2,1)S(1)}, bf16[1,96,192]{2,1,0:T(8,128)(2,1)S(1)}, bf16[256,256]{1,0:T(8,128)(2,1)S(1)}) custom-call(s32[2,2]{1,0:T(2,128)S(1)} %copy-done, f32[18]{0:T(128)S(1)} %reshape.19.taps), custom_call_target="tpu_custom_call" | custom-call | flops 20000000 | bytes 700000 | tf_op jit(solution)/shard_map/pallas_call | solution.py:35
  53.8 3.6 %collective-permute-done.refs_6_ = bf16[2,8,104,128]{3,2,1,0:T(8,128)(2,1)S(1)} collective-permute-done((bf16[2,8,104,128]{3,2,1,0:T(8,128)(2,1)S(1)}, bf16[2,8,104,128]{3,2,1,0:T(8,128)(2,1)S(1)}, u32[]{:S(2)}, u32[]{:S(2)}) %collective-permute-start) | collective-permute-done | bytes 426016 | tf_op jit(solution)/shard_map/ppermute | solution.py:561
  57.4 3.0 %collective-permute-done.1.refs_8_ = bf16[2,8,104,128]{3,2,1,0:T(8,128)(2,1)S(1)} collective-permute-done((bf16[2,8,104,128]{3,2,1,0:T(8,128)(2,1)S(1)}, bf16[2,8,104,128]{3,2,1,0:T(8,128)(2,1)S(1)}, u32[]{:S(2)}, u32[]{:S(2)}) %collective-permute-start.1) | collective-permute-done | bytes 426016 | tf_op jit(solution)/shard_map/ppermute | solution.py:562
  60.4 5.6 %shard_map.57 = (bf16[16,64,128]{2,1,0:T(8,128)(2,1)S(1)}, bf16[64,128]{1,0:T(8,128)(2,1)S(1)}) custom-call(bf16[2,96,224]{2,1,0:T(8,128)(2,1)S(1)} %get-tuple-element.41.refs_0_, bf16[2,80,192]{2,1,0:T(8,128)(2,1)S(1)} %get-tuple-element.42.refs_1_, bf16[1,128,256]{2,1,0:T(8,128)(2,1)S(1)} %get-tuple-element.43.refs_2_, ...), custom_call_target="tpu_custom_call" | custom-call | flops 1384120320 | bytes 6000000 | tf_op jit(solution)/shard_map/pallas_call | solution.py:35
  66.0 1.3 %collective-permute-start.4 = (bf16[64,128]{1,0:T(8,128)(2,1)S(1)}, bf16[64,128]{1,0:T(8,128)(2,1)S(1)}, u32[]{:S(2)}, u32[]{:S(2)}) collective-permute-start(bf16[64,128]{1,0:T(8,128)(2,1)S(1)} %get-tuple-element.50), channel_id=1, source_target_pairs={{1,0},{2,1},{3,2},{67,3},{66,67},{65,66},{64,65},{128,64},{129,128... | collective-permute-start | bytes 49160 | tf_op jit(solution)/shard_map/ppermute | solution.py:589
  67.3 4.0 %collective-permute-start.3 = (bf16[64,128]{1,0:T(8,128)(2,1)S(1)}, bf16[64,128]{1,0:T(8,128)(2,1)S(1)}, u32[]{:S(2)}, u32[]{:S(2)}) collective-permute-start(bf16[64,128]{1,0:T(8,128)(2,1)S(1)} %get-tuple-element.50), channel_id=1, source_target_pairs={{0,1},{1,2},{2,3},{3,67},{67,66},{66,65},{65,64},{64,128},{128,129... | collective-permute-start | bytes 49160 | tf_op jit(solution)/shard_map/ppermute | solution.py:588
  71.3 1.1 %shard_map.58 = (bf16[2,96,224]{2,1,0:T(8,128)(2,1)S(1)}, bf16[2,80,192]{2,1,0:T(8,128)(2,1)S(1)}, bf16[1,128,256]{2,1,0:T(8,128)(2,1)S(1)}, bf16[1,96,192]{2,1,0:T(8,128)(2,1)S(1)}, bf16[256,256]{1,0:T(8,128)(2,1)S(1)}) custom-call(s32[2,2]{1,0:T(2,128)S(1)} %copy-done, f32[18]{0:T(128)S(1)} %reshape.19.taps), custom_call_target="tpu_custom_call" | custom-call | flops 20000000 | bytes 700000 | tf_op jit(solution)/shard_map/pallas_call | solution.py:35
  72.4 0.0 collective-permute-done.4
  72.4 0.0 collective-permute-done.3
  72.5 2.4 %collective-permute-start.6 = (bf16[3,64,128]{2,1,0:T(8,128)(2,1)S(1)}, bf16[3,64,128]{2,1,0:T(8,128)(2,1)S(1)}, u32[]{:S(2)}, u32[]{:S(2)}) collective-permute-start(bf16[3,64,128]{2,1,0:T(8,128)(2,1)S(1)} %pad_maximum_fusion.1.refs_10_), channel_id=1, source_target_pairs={{32,4},{36,8},{40,12},{44,16},{48,20},{52,24},{56,28},{60,0},{4,32... | collective-permute-start | bytes 147464 | tf_op jit(solution)/shard_map/ppermute | solution.py:594
  74.9 4.7 %collective-permute-start.5 = (bf16[3,64,128]{2,1,0:T(8,128)(2,1)S(1)}, bf16[3,64,128]{2,1,0:T(8,128)(2,1)S(1)}, u32[]{:S(2)}, u32[]{:S(2)}) collective-permute-start(bf16[3,64,128]{2,1,0:T(8,128)(2,1)S(1)} %pad_maximum_fusion.1.refs_10_), channel_id=1, source_target_pairs={{0,32},{32,0},{1,33},{33,1},{2,34},{34,2},{3,35},{35,3},{4,36},{36... | collective-permute-start | bytes 147464 | tf_op jit(solution)/shard_map/ppermute | solution.py:542
  79.7 0.0 collective-permute-done.6.refs_12_
  79.7 0.8 collective-permute-done.5.refs_11_
  80.5 5.5 %shard_map.59 = bf16[2,2,8,32,128]{4,3,2,1,0:T(8,128)(2,1)S(1)} custom-call(bf16[2,96,224]{2,1,0:T(8,128)(2,1)S(1)} %get-tuple-element.57.refs_0_, bf16[2,80,192]{2,1,0:T(8,128)(2,1)S(1)} %get-tuple-element.58.refs_1_, bf16[1,128,256]{2,1,0:T(8,128)(2,1)S(1)} %get-tuple-element.59.refs_2_, bf16[1,96,192]{2,1,0:T(8,128)(2,1)S(1)} %get-tuple-element.60.refs_3_, ...), custom_call_target="tpu_custom_call" | custom-call | flops 1384120320 | bytes 6000000 | tf_op jit(solution)/shard_map/pallas_call | solution.py:35
  86.1 2.5 %collective-permute-start.7 = (bf16[2,8,32,128]{3,2,1,0:T(8,128)(2,1)S(1)}, bf16[2,8,32,128]{3,2,1,0:T(8,128)(2,1)S(1)}, u32[]{:S(2)}, u32[]{:S(2)}) collective-permute-start(bf16[2,8,32,128]{3,2,1,0:T(8,128)(2,1)S(1)} %get-tuple-element.68), channel_id=1, source_target_pairs={{0,32},{32,0},{1,33},{33,1},{2,34},{34,2},{3,35},{35,3},{4,36},{36... | collective-permute-start | bytes 393224 | tf_op jit(solution)/shard_map/ppermute | solution.py:542
  88.6 1.0 collective-permute-done.7
  89.6 18.6 %all_to_all.11.terms = bf16[32,32,128]{2,1,0:T(8,128)(2,1)S(1)} all-to-all(bf16[32,32,128]{2,1,0:T(8,128)(2,1)S(1)} %bitcast.20), channel_id=1, replica_groups={{0,64,128,192,256,320,384,448,1,65,129,193,257,321,385,449,2,66,130,194..., dimensions={0} | all-to-all | bytes 524288 | tf_op jit(solution)/shard_map/all_to_all | solution.py:558
  108.2 2.0 %shard_map.60 = f32[2,2,32,2048]{3,2,1,0:T(8,128)} custom-call(s32[2,2]{1,0:T(2,128)S(1)} %copy-done, bf16[32,32,128]{2,1,0:T(8,128)(2,1)S(1)} %all_to_all.11.terms), custom_call_target="tpu_custom_call" | custom-call | flops 1000000 | bytes 2000000 | tf_op jit(solution)/shard_map/pallas_call | solution.py:35
  (3 shorter events, 0.1 us)
Async XLA Ops:
  35.5 17.2 %collective-permute-start.2 = (bf16[4,8,104,128]{3,2,1,0:T(8,128)(2,1)S(1)}, bf16[4,8,104,128]{3,2,1,0:T(8,128)(2,1)S(1)}, u32[]{:S(2)}, u32[]{:S(2)}) collective-permute-start(bf16[4,8,104,128]{3,2,1,0:T(8,128)(2,1)S(1)} %bitcast.15), channel_id=1, source_target_pairs={{0,32},{32,0},{1,33},{33,1},{2,34},{34,2},{3,35},{35,3},{4,36},{36... | collective-permute-start | bytes 2555912 | tf_op jit(solution)/shard_map/ppermute | solution.py:542
  40.0 17.4 %collective-permute-start = (bf16[2,8,104,128]{3,2,1,0:T(8,128)(2,1)S(1)}, bf16[2,8,104,128]{3,2,1,0:T(8,128)(2,1)S(1)}, u32[]{:S(2)}, u32[]{:S(2)}) collective-permute-start(bf16[2,8,104,128]{3,2,1,0:T(8,128)(2,1)S(1)} %bitcast.22), channel_id=1, source_target_pairs={{0,4},{4,8},{8,12},{12,16},{16,20},{20,24},{24,28},{28,0},{36,32},... | collective-permute-start | bytes 1277960 | tf_op jit(solution)/shard_map/ppermute | solution.py:561
  50.7 2.0 %copy-start.1 = (bf16[2,9]{1,0:T(2,128)(2,1)S(1)}, bf16[2,9]{1,0:T(2,128)(2,1)}, u32[]{:S(2)}) copy-start(bf16[2,9]{1,0:T(2,128)(2,1)} %param.9) | copy-start | bytes 112
  50.7 2.0 %copy-start = (s32[2,2]{1,0:T(2,128)S(1)}, s32[2,2]{1,0:T(2,128)}, u32[]{:S(2)}) copy-start(s32[2,2]{1,0:T(2,128)} %offsets.7) | copy-start | bytes 52
  50.7 9.7 %collective-permute-start.1 = (bf16[2,8,104,128]{3,2,1,0:T(8,128)(2,1)S(1)}, bf16[2,8,104,128]{3,2,1,0:T(8,128)(2,1)S(1)}, u32[]{:S(2)}, u32[]{:S(2)}) collective-permute-start(bf16[2,8,104,128]{3,2,1,0:T(8,128)(2,1)S(1)} %bitcast.21), channel_id=1, source_target_pairs={{32,4},{36,8},{40,12},{44,16},{48,20},{52,24},{56,28},{60,0},{4,32... | collective-permute-start | bytes 1277960 | tf_op jit(solution)/shard_map/ppermute | solution.py:562
  66.0 6.4 %collective-permute-start.4 = (bf16[64,128]{1,0:T(8,128)(2,1)S(1)}, bf16[64,128]{1,0:T(8,128)(2,1)S(1)}, u32[]{:S(2)}, u32[]{:S(2)}) collective-permute-start(bf16[64,128]{1,0:T(8,128)(2,1)S(1)} %get-tuple-element.50), channel_id=1, source_target_pairs={{1,0},{2,1},{3,2},{67,3},{66,67},{65,66},{64,65},{128,64},{129,128... | collective-permute-start | bytes 49160 | tf_op jit(solution)/shard_map/ppermute | solution.py:589
  67.3 5.1 %collective-permute-start.3 = (bf16[64,128]{1,0:T(8,128)(2,1)S(1)}, bf16[64,128]{1,0:T(8,128)(2,1)S(1)}, u32[]{:S(2)}, u32[]{:S(2)}) collective-permute-start(bf16[64,128]{1,0:T(8,128)(2,1)S(1)} %get-tuple-element.50), channel_id=1, source_target_pairs={{0,1},{1,2},{2,3},{3,67},{67,66},{66,65},{65,64},{64,128},{128,129... | collective-permute-start | bytes 49160 | tf_op jit(solution)/shard_map/ppermute | solution.py:588
  72.5 7.2 %collective-permute-start.6 = (bf16[3,64,128]{2,1,0:T(8,128)(2,1)S(1)}, bf16[3,64,128]{2,1,0:T(8,128)(2,1)S(1)}, u32[]{:S(2)}, u32[]{:S(2)}) collective-permute-start(bf16[3,64,128]{2,1,0:T(8,128)(2,1)S(1)} %pad_maximum_fusion.1.refs_10_), channel_id=1, source_target_pairs={{32,4},{36,8},{40,12},{44,16},{48,20},{52,24},{56,28},{60,0},{4,32... | collective-permute-start | bytes 147464 | tf_op jit(solution)/shard_map/ppermute | solution.py:594
  74.9 5.6 %collective-permute-start.5 = (bf16[3,64,128]{2,1,0:T(8,128)(2,1)S(1)}, bf16[3,64,128]{2,1,0:T(8,128)(2,1)S(1)}, u32[]{:S(2)}, u32[]{:S(2)}) collective-permute-start(bf16[3,64,128]{2,1,0:T(8,128)(2,1)S(1)} %pad_maximum_fusion.1.refs_10_), channel_id=1, source_target_pairs={{0,32},{32,0},{1,33},{33,1},{2,34},{34,2},{3,35},{35,3},{4,36},{36... | collective-permute-start | bytes 147464 | tf_op jit(solution)/shard_map/ppermute | solution.py:542
  86.1 3.4 %collective-permute-start.7 = (bf16[2,8,32,128]{3,2,1,0:T(8,128)(2,1)S(1)}, bf16[2,8,32,128]{3,2,1,0:T(8,128)(2,1)S(1)}, u32[]{:S(2)}, u32[]{:S(2)}) collective-permute-start(bf16[2,8,32,128]{3,2,1,0:T(8,128)(2,1)S(1)} %get-tuple-element.68), channel_id=1, source_target_pairs={{0,32},{32,0},{1,33},{33,1},{2,34},{34,2},{3,35},{35,3},{4,36},{36... | collective-permute-start | bytes 393224 | tf_op jit(solution)/shard_map/ppermute | solution.py:542
